TPU v7x, 32 devices: a whole 2x2x4 slice. The times are simulated.
32 devices in a mesh: ctx: 8 (over z, y), shard: 4 (over x, core).
Axes of the slice: x: 2, y: 2, z: 4, core: 2. Of those that a mesh axis runs over, the one named last changes fastest.
Arguments:
- block_in: bfloat16 [1024, 1024], P('ctx'), may hold values from -6 to 6
- attn_gain: float32 [1024], replicated, may hold values from 0.5 to 1.5
- q_weight: bfloat16 [1024, 1024], P(None, 'shard'), may hold values from -0.1875 to 0.1875
- k_weight: bfloat16 [1024, 512], P(None, 'shard'), may hold values from -0.1875 to 0.1875
- v_weight: bfloat16 [1024, 512], P(None, 'shard'), may hold values from -0.1875 to 0.1875
- o_weight: bfloat16 [1024, 1024], P('shard'), may hold values from -1.5 to 1.5
- moe_gain: float32 [1024], replicated, may hold values from 0.5 to 1.5
- router_weight: bfloat16 [1024, 16], replicated, may hold values from -0.1875 to 0.1875
- expert_gate: bfloat16 [16, 1024, 512], P('shard'), may hold values from -0.1875 to 0.1875
- expert_up: bfloat16 [16, 1024, 512], P('shard'), may hold values from -0.1875 to 0.1875
- expert_down: bfloat16 [16, 512, 1024], P('shard'), may hold values from -0.5 to 0.5
- routes: int32 [1024, 8], P('ctx'), may hold values from 0 to 15, all different within a row; in each aligned block of 128 rows (0 to 127, 128 to 255, ...) at most 112 rows name the same one
- out_grad: float32 [1024, 1024], P('ctx'), may hold values from -6 to 6
Outputs:
- block_out: float32 [1024, 1024], P('ctx')
- in_grad: float32 [1024, 1024], P('ctx')
- attn_gain_grad: float32 [1024], P('ctx')
- q_weight_grad: float32 [1024, 1024], P('ctx', 'shard')
- k_weight_grad: float32 [1024, 512], P('ctx', 'shard')
- v_weight_grad: float32 [1024, 512], P('ctx', 'shard')
- o_weight_grad: float32 [1024, 1024], P('shard', 'ctx')
- moe_gain_grad: float32 [1024], P('ctx')
- router_grad: float32 [1024, 16], P('ctx')
- gate_grad: float32 [16, 1024, 512], P('shard', 'ctx')
- up_grad: float32 [16, 1024, 512], P('shard', 'ctx')
- down_grad: float32 [16, 512, 1024], P('shard', None, 'ctx')
Inputs may be any that keep to these rules, and one draw needn't show every extreme that they name: `routes`: each row names 8 different experts; in each aligned block of 128 rows (128; a device may hold several) no expert is named by more than 112 rows.
All inputs are finite; a program needn't handle non-finite values.
Results may differ from a plain program's by a relative error of at most 0.015.
Values may be sent and summed in bfloat16 or wider, within the bound.
No kernel may reach another device: no remote copies, remote signals or barrier semaphores. Data moves between devices by JAX's collectives and lax.ppermute only.
A program may use at most 128 MiB of HBM per device.

v0:
```python
import math

import jax
import jax.numpy as jnp
from jax import lax
from jax.sharding import PartitionSpec as P

HD = 64
CAP = 112


NORM_EPS = 1e-06
ROPE_BASE = 10000.0


def rope_tables(positions, head_width):
    half_width = head_width // 2
    freq_steps = jnp.arange(half_width, dtype=jnp.float32) * (2.0 / head_width)
    inv_freq = jnp.exp(-math.log(ROPE_BASE) * freq_steps)
    angles = positions.astype(jnp.float32)[:, None] * inv_freq[None, :]
    cos_tab = jnp.concatenate([jnp.cos(angles), jnp.cos(angles)], axis=1)
    sin_tab = jnp.concatenate([jnp.sin(angles), jnp.sin(angles)], axis=1)
    return (cos_tab, sin_tab)


def rotate_heads(head_vals, cos_tab, sin_tab):
    half_width = head_vals.shape[-1] // 2
    turned = jnp.concatenate([-head_vals[..., half_width:], head_vals[..., :half_width]], axis=-1)
    return head_vals * cos_tab[:, None, :] + turned * sin_tab[:, None, :]


def unrotate_heads(head_grads, cos_tab, sin_tab):
    half_width = head_grads.shape[-1] // 2
    scaled = head_grads * sin_tab[:, None, :]
    back = jnp.concatenate([scaled[..., half_width:], -scaled[..., :half_width]], axis=-1)
    return head_grads * cos_tab[:, None, :] + back


def rms_forward(inputs, gain):
    inverse = lax.rsqrt(jnp.mean(inputs * inputs, axis=-1, keepdims=True) + NORM_EPS)
    return (inputs * inverse * gain, inverse)


def rms_backward(inputs, inverse, gain, grads):
    scaled = grads * gain
    inner = jnp.mean(scaled * inputs, axis=-1, keepdims=True)
    d_inputs = inverse * scaled - inputs * inverse * inverse * inverse * inner
    d_gain = jnp.sum(grads * inputs * inverse, axis=0)
    return (d_inputs, d_gain)


def slot_tables(routes, n_experts):
    expert_ids = jnp.arange(n_experts, dtype=jnp.int32)
    expert_hits = jnp.sum(
        (routes[:, :, None] == expert_ids[None, None, :]).astype(jnp.int32), axis=1
    )
    earlier_hits = jnp.cumsum(expert_hits, axis=0) - expert_hits
    slot_ids = jnp.take_along_axis(earlier_hits, routes, axis=1)
    return (expert_hits, earlier_hits, slot_ids)


def spread_to_experts(values_tk, routes, n_experts):
    expert_ids = jnp.arange(n_experts, dtype=jnp.int32)
    return jnp.sum(
        jnp.where(routes[:, :, None] == expert_ids[None, None, :], values_tk[:, :, None], 0.0),
        axis=1,
    )


def slot_rows(expert_hits, earlier_hits, weight_table, first_expert, expert_count, capacity):
    local_hits = lax.dynamic_slice_in_dim(expert_hits, first_expert, expert_count, 1).T
    local_earlier = lax.dynamic_slice_in_dim(earlier_hits, first_expert, expert_count, 1).T
    local_weight = lax.dynamic_slice_in_dim(weight_table, first_expert, expert_count, 1).T
    slot_range = jnp.arange(capacity, dtype=jnp.int32)
    matched = (local_hits[:, None, :] > 0) & (
        local_earlier[:, None, :] == slot_range[None, :, None]
    )
    row_range = jnp.arange(expert_hits.shape[0], dtype=jnp.int32)
    row_ids = jnp.sum(jnp.where(matched, row_range[None, None, :], 0), axis=2)
    row_valid = jnp.any(matched, axis=2)
    slot_weight = jnp.sum(jnp.where(matched, local_weight[:, None, :], 0.0), axis=2)
    return (row_ids, row_valid, slot_weight)


def body(
    block_in,
    attn_gain,
    q_weight,
    k_weight,
    v_weight,
    o_weight,
    moe_gain,
    router_weight,
    expert_gate,
    expert_up,
    expert_down,
    routes,
    out_grad,
):
    row_count = block_in.shape[0]
    model_width = block_in.shape[1]
    seq_len = row_count * lax.axis_size("ctx")
    q_local = q_weight.shape[1] // HD
    kv_local = k_weight.shape[1] // HD
    group = q_local // kv_local
    scale = HD ** (-0.5)
    key_block = math.gcd(512, seq_len)
    first_row = lax.axis_index("ctx") * row_count
    blocks_needed = (first_row + row_count + key_block - 1) // key_block
    positions = first_row + jnp.arange(row_count, dtype=jnp.int32)
    cos_tab, sin_tab = rope_tables(positions, HD)
    resid_in = block_in.astype(jnp.float32)
    normed_one, inverse_one = rms_forward(resid_in, attn_gain)
    normed_one = normed_one.astype(jnp.bfloat16)
    query_rot = rotate_heads(
        jnp.dot(normed_one, q_weight, preferred_element_type=jnp.float32).reshape(
            row_count, q_local, HD
        ),
        cos_tab,
        sin_tab,
    ).astype(jnp.bfloat16)
    query_groups = query_rot.reshape(row_count, kv_local, group, HD)
    key_rot = (
        rotate_heads(
            jnp.dot(normed_one, k_weight, preferred_element_type=jnp.float32).reshape(
                row_count, kv_local, HD
            ),
            cos_tab,
            sin_tab,
        )
        .astype(jnp.bfloat16)
        .reshape(row_count, kv_local * HD)
    )
    value_proj = jnp.dot(normed_one, v_weight, preferred_element_type=jnp.float32).astype(
        jnp.bfloat16
    )

    def masked_scores(key_piece, key_start):
        piece_len = key_piece.shape[0]
        raw = (
            jnp.einsum(
                "tngd,jnd->ngtj",
                query_groups,
                key_piece.reshape(piece_len, kv_local, HD),
                preferred_element_type=jnp.float32,
            )
            * scale
        )
        key_pos = key_start + jnp.arange(piece_len, dtype=jnp.int32)
        allowed = key_pos[None, :] <= positions[:, None]
        return jnp.where(allowed[None, None], raw, -jnp.inf)

    running_top = jnp.full((kv_local, group, row_count), -1e30, jnp.float32)
    scores = masked_scores(lax.all_gather(key_rot, "ctx", axis=0, tiled=True), jnp.int32(0))
    new_top = jnp.maximum(running_top, jnp.max(scores, axis=-1))
    new_total = jnp.sum(jnp.exp(scores - new_top[..., None]), axis=-1)
    log_total = new_top + jnp.log(new_total)
    key_piece = lax.all_gather(key_rot, "ctx", axis=0, tiled=True)
    value_piece = lax.all_gather(value_proj, "ctx", axis=0, tiled=True)
    scores = masked_scores(key_piece, jnp.int32(0))
    probs = jnp.exp(scores - log_total[..., None]).astype(jnp.bfloat16)
    piece_len = value_piece.shape[0]
    running_acc = jnp.einsum(
        "ngtj,jnd->ngtd",
        probs,
        value_piece.reshape(piece_len, kv_local, HD),
        preferred_element_type=jnp.float32,
    )
    heads_out = (
        running_acc.transpose(2, 0, 1, 3).reshape(row_count, q_local * HD).astype(jnp.bfloat16)
    )
    resid_mid = resid_in + lax.psum(
        jnp.dot(heads_out, o_weight, preferred_element_type=jnp.float32), "shard"
    )
    normed_two, inverse_two = rms_forward(resid_mid, moe_gain)
    normed_two = normed_two.astype(jnp.bfloat16)
    logits = jnp.dot(normed_two, router_weight, preferred_element_type=jnp.float32)
    gate = jax.nn.softmax(jnp.take_along_axis(logits, routes, axis=1), axis=-1)
    local_count = expert_gate.shape[0]
    n_experts = local_count * lax.axis_size("shard")
    first_expert = lax.axis_index("shard") * local_count
    expert_hits, earlier_hits, slot_ids = slot_tables(routes, n_experts)
    gate_table = spread_to_experts(gate, routes, n_experts)
    row_ids, row_valid, slot_weight = slot_rows(
        expert_hits, earlier_hits, gate_table, first_expert, local_count, CAP
    )
    buffer = jnp.where(row_valid[..., None], normed_two[row_ids], jnp.zeros((), jnp.bfloat16))
    pre_gate = jnp.einsum("ecd,edf->ecf", buffer, expert_gate, preferred_element_type=jnp.float32)
    pre_up = jnp.einsum("ecd,edf->ecf", buffer, expert_up, preferred_element_type=jnp.float32)
    sig_gate = jax.nn.sigmoid(pre_gate)
    hidden = (pre_gate * sig_gate * pre_up).astype(jnp.bfloat16)
    expert_out = jnp.einsum("ecf,efd->ecd", hidden, expert_down, preferred_element_type=jnp.float32)
    is_local = (routes >= first_expert) & (routes < first_expert + local_count)
    flat_ids = jnp.where(is_local, (routes - first_expert) * CAP + slot_ids, 0)
    picked = expert_out.reshape(local_count * CAP, model_width)[flat_ids]
    moe_part = jnp.sum(jnp.where(is_local, gate, 0.0)[..., None] * picked, axis=1)
    d_gate_part = jnp.where(is_local, jnp.sum(picked * out_grad[:, None, :], axis=-1), 0.0)
    block_out = resid_mid + lax.psum(moe_part.astype(jnp.bfloat16), "shard").astype(jnp.float32)
    d_expert_out = (jnp.where(row_valid, slot_weight, 0.0)[..., None] * out_grad[row_ids]).astype(
        jnp.bfloat16
    )
    d_hidden = jnp.einsum(
        "ecd,efd->ecf", d_expert_out, expert_down, preferred_element_type=jnp.float32
    )
    down_part = jnp.einsum("ecf,ecd->efd", hidden, d_expert_out, preferred_element_type=jnp.float32)
    d_silu = sig_gate * (1.0 + pre_gate * (1.0 - sig_gate))
    d_pre_gate = (d_hidden * pre_up * d_silu).astype(jnp.bfloat16)
    d_pre_up = (d_hidden * pre_gate * sig_gate).astype(jnp.bfloat16)
    gate_part = jnp.einsum("ecd,ecf->edf", buffer, d_pre_gate, preferred_element_type=jnp.float32)
    up_part = jnp.einsum("ecd,ecf->edf", buffer, d_pre_up, preferred_element_type=jnp.float32)
    d_buffer = jnp.einsum(
        "ecf,edf->ecd", d_pre_gate, expert_gate, preferred_element_type=jnp.float32
    ) + jnp.einsum("ecf,edf->ecd", d_pre_up, expert_up, preferred_element_type=jnp.float32)
    d_normed_part = jnp.sum(
        jnp.where(
            is_local[..., None], d_buffer.reshape(local_count * CAP, model_width)[flat_ids], 0.0
        ),
        axis=1,
    )
    d_normed_exp, d_gate = lax.psum((d_normed_part, d_gate_part), "shard")
    d_chosen = gate * (d_gate - jnp.sum(gate * d_gate, axis=-1, keepdims=True))
    d_logits = spread_to_experts(d_chosen, routes, n_experts)
    router_f = router_weight.astype(jnp.float32)
    d_normed_two = d_normed_exp + jnp.dot(d_logits, router_f.T, precision=lax.Precision.HIGHEST)
    router_part = jnp.dot(
        normed_two.astype(jnp.float32).T, d_logits, precision=lax.Precision.HIGHEST
    )
    d_resid_norm, moe_gain_part = rms_backward(resid_mid, inverse_two, moe_gain, d_normed_two)
    d_resid_mid = out_grad + d_resid_norm
    d_mid_b = d_resid_mid.astype(jnp.bfloat16)
    o_part = jnp.dot(heads_out.T, d_mid_b, preferred_element_type=jnp.float32)
    d_heads = jnp.dot(d_mid_b, o_weight.T, preferred_element_type=jnp.float32).astype(jnp.bfloat16)
    d_head_groups = d_heads.reshape(row_count, kv_local, group, HD)
    delta = jnp.sum(
        d_heads.astype(jnp.float32).reshape(row_count, kv_local, group, HD)
        * heads_out.astype(jnp.float32).reshape(row_count, kv_local, group, HD),
        axis=-1,
    ).transpose(1, 2, 0)
    keys_back, values_back = (
        lax.all_gather(key_rot, "ctx", axis=0, tiled=True),
        lax.all_gather(value_proj, "ctx", axis=0, tiled=True),
    )

    def key_step(block_idx, carry):
        d_query_acc, d_key_term, d_value_term = carry
        key_start = block_idx * key_block
        key_piece = lax.dynamic_slice_in_dim(keys_back, key_start, key_block, 0)
        value_piece = lax.dynamic_slice_in_dim(values_back, key_start, key_block, 0)
        scores = masked_scores(key_piece, key_start)
        probs = jnp.exp(scores - log_total[..., None])
        key_heads = key_piece.reshape(key_block, kv_local, HD)
        value_heads = value_piece.reshape(key_block, kv_local, HD)
        d_probs = jnp.einsum(
            "tngd,jnd->ngtj", d_head_groups, value_heads, preferred_element_type=jnp.float32
        )
        d_scores = (probs * (d_probs - delta[..., None])).astype(jnp.bfloat16)
        d_query_acc = d_query_acc + scale * jnp.einsum(
            "ngtj,jnd->tngd", d_scores, key_heads, preferred_element_type=jnp.float32
        )
        d_key_blk = scale * jnp.einsum(
            "ngtj,tngd->jnd", d_scores, query_groups, preferred_element_type=jnp.float32
        )
        d_value_blk = jnp.einsum(
            "ngtj,tngd->jnd",
            probs.astype(jnp.bfloat16),
            d_head_groups,
            preferred_element_type=jnp.float32,
        )
        d_key_term = lax.dynamic_update_slice_in_dim(
            d_key_term, d_key_blk.reshape(key_block, kv_local * HD), key_start, 0
        )
        d_value_term = lax.dynamic_update_slice_in_dim(
            d_value_term, d_value_blk.reshape(key_block, kv_local * HD), key_start, 0
        )
        return (d_query_acc, d_key_term, d_value_term)

    zero_terms = jnp.zeros((seq_len, kv_local * HD), jnp.float32)
    d_query_acc, d_key_term, d_value_term = lax.fori_loop(
        0,
        blocks_needed,
        key_step,
        (jnp.zeros((row_count, kv_local, group, HD), jnp.float32), zero_terms, zero_terms),
    )
    d_key_own, d_value_own = (
        lax.psum_scatter(d_key_term, "ctx", scatter_dimension=0, tiled=True),
        lax.psum_scatter(d_value_term, "ctx", scatter_dimension=0, tiled=True),
    )
    d_query = (
        unrotate_heads(d_query_acc.reshape(row_count, q_local, HD), cos_tab, sin_tab)
        .astype(jnp.bfloat16)
        .reshape(row_count, q_local * HD)
    )
    d_key = (
        unrotate_heads(d_key_own.reshape(row_count, kv_local, HD), cos_tab, sin_tab)
        .astype(jnp.bfloat16)
        .reshape(row_count, kv_local * HD)
    )
    d_value = d_value_own.astype(jnp.bfloat16)
    q_part = jnp.dot(normed_one.T, d_query, preferred_element_type=jnp.float32)
    k_part = jnp.dot(normed_one.T, d_key, preferred_element_type=jnp.float32)
    v_part = jnp.dot(normed_one.T, d_value, preferred_element_type=jnp.float32)
    d_normed_part_one = (
        jnp.dot(d_query, q_weight.T, preferred_element_type=jnp.float32)
        + jnp.dot(d_key, k_weight.T, preferred_element_type=jnp.float32)
        + jnp.dot(d_value, v_weight.T, preferred_element_type=jnp.float32)
    )
    d_normed_one = lax.psum(d_normed_part_one, "shard")
    d_resid_first, attn_gain_part = rms_backward(resid_in, inverse_one, attn_gain, d_normed_one)
    in_grad = d_resid_mid + d_resid_first
    (
        attn_gain_grad,
        q_weight_grad,
        k_weight_grad,
        v_weight_grad,
        o_weight_grad,
        moe_gain_grad,
        router_grad,
        gate_grad,
        up_grad,
        down_grad,
    ) = (
        lax.psum_scatter(attn_gain_part, "ctx", scatter_dimension=0, tiled=True),
        lax.psum_scatter(q_part, "ctx", scatter_dimension=0, tiled=True),
        lax.psum_scatter(k_part, "ctx", scatter_dimension=0, tiled=True),
        lax.psum_scatter(v_part, "ctx", scatter_dimension=0, tiled=True),
        lax.psum_scatter(o_part, "ctx", scatter_dimension=1, tiled=True),
        lax.psum_scatter(moe_gain_part, "ctx", scatter_dimension=0, tiled=True),
        lax.psum_scatter(router_part, "ctx", scatter_dimension=0, tiled=True),
        lax.psum_scatter(gate_part, "ctx", scatter_dimension=1, tiled=True),
        lax.psum_scatter(up_part, "ctx", scatter_dimension=1, tiled=True),
        lax.psum_scatter(down_part, "ctx", scatter_dimension=2, tiled=True),
    )
    return (
        block_out,
        in_grad,
        attn_gain_grad,
        q_weight_grad,
        k_weight_grad,
        v_weight_grad,
        o_weight_grad,
        moe_gain_grad,
        router_grad,
        gate_grad,
        up_grad,
        down_grad,
    )


def solution(mesh):
    in_specs = (
        P("ctx", None),
        P(),
        P(None, "shard"),
        P(None, "shard"),
        P(None, "shard"),
        P("shard", None),
        P(),
        P(),
        P("shard", None, None),
        P("shard", None, None),
        P("shard", None, None),
        P("ctx", None),
        P("ctx", None),
    )
    out_specs = (
        P("ctx", None),
        P("ctx", None),
        P("ctx"),
        P("ctx", "shard"),
        P("ctx", "shard"),
        P("ctx", "shard"),
        P("shard", "ctx"),
        P("ctx"),
        P("ctx", None),
        P("shard", "ctx", None),
        P("shard", "ctx", None),
        P("shard", None, "ctx"),
    )
    return jax.shard_map(body, mesh=mesh, in_specs=in_specs, out_specs=out_specs, check_vma=False)
```

profile of v0, /device:TPU:0, one launch (start us, length us, event | category | flops | bytes accessed | tf_op | source)
XLA Modules:
  0.0 1194.1 jit_solution(7015718147966698272)
XLA Ops:
  7.3 1.1 fusion.29
  8.4 1.3 convolution_convert_fusion.2
  9.8 1.4 fusion.71
  11.3 1.5 fusion.69
  13.0 28.3 %all_gather.4 = bf16[1024,128]{0,1:T(8,128)(2,1)S(1)} all-gather(bf16[128,128]{0,1:T(8,128)(2,1)S(1)} %fusion.48), channel_id=1, replica_groups=mesh['ctx'=8,'shard'=4] {'ctx'}, dimensions={0}, use_global_device_ids=true | all-gather | bytes 294912 | tf_op jit(solution)/shard_map/all_gather | solution.py:158
  41.3 30.8 %all_gather.10 = bf16[1024,128]{1,0:T(8,128)(2,1)S(1)} all-gather(bf16[128,128]{1,0:T(8,128)(2,1)S(1)} %convolution_convert_fusion.2), channel_id=1, replica_groups=mesh['ctx'=8,'shard'=4] {'ctx'}, dimensions={0}, use_global_device_ids=true | all-gather | bytes 294912 | tf_op jit(solution)/shard_map/all_gather | solution.py:159
  73.7 1.1 fusion.77
  75.7 7.1 gather_fusion.5
  83.1 2.6 gather_fusion.2
  85.8 21.8 %all-reduce.8.cloned.1.call-done = f32[128,1024]{1,0:T(8,128)} async-done(((f32[128,1024]{1,0:T(8,128)}), f32[128,1024]{1,0:T(8,128)}) %all-reduce.8.cloned.1.call-update) | async-done | bytes 524304 | tf_op jit(solution)/shard_map/psum | solution.py:172
  107.6 1.2 multiply_reduce_fusion.2
  109.7 2.1 gather_fusion
  112.0 7.0 gather_fusion.4
  121.0 3.1 fusion.23
  124.4 1.8 multiply_convert_fusion.3
  126.2 1.2 copy-done.6
  128.1 5.4 gather_fusion.1
  133.6 4.6 fusion.15
  138.2 0.9 copy.150
  139.1 1.3 broadcast_select_fusion.5
  140.4 5.9 psum.38
  147.0 0.8 select_reduce_fusion
  148.4 4.5 multiply_convert_fusion.1
  153.0 1.4 fusion.80
  154.4 1.1 copy-done.15
  155.5 1.5 convolution_add_fusion
  157.0 5.4 gather_fusion.3
  162.4 4.4 fusion.14
  167.6 32.7 %all-reduce.12.cloned.1.call-done = f32[128,1024]{1,0:T(8,128)} async-done(((f32[128,1024]{1,0:T(8,128)}), f32[128,1024]{1,0:T(8,128)}) %all-reduce.12.cloned.1.call-update) | async-done | bytes 524304 | tf_op jit(solution)/shard_map/psum | solution.py:220
  200.3 2.9 multiply_reduce_fusion
  203.2 31.4 %all-reduce.10.cloned.1.call-done = bf16[128,1024]{1,0:T(8,128)(2,1)} async-done(((bf16[128,1024]{1,0:T(8,128)(2,1)}), bf16[128,1024]{1,0:T(8,128)(2,1)}) %all-reduce.10.cloned.1.call-update) | async-done | bytes 262160 | tf_op jit(solution)/shard_map/psum | solution.py:198
  234.6 2.1 subtract_add_fusion
  237.2 0.8 broadcast_in_dim.200.clone
  238.1 0.8 broadcast_in_dim.200
  239.0 2.9 while.15
  240.9 0.8 copy-done.20
  242.8 64.4 %reduce-scatter.11.cloned.1.call-done = f32[128,128]{0,1:T(8,128)} async-done(((f32[1024,128]{0,1:T(8,128)}), f32[128,128]{0,1:T(8,128)}) %reduce-scatter.11.cloned.1.call-update) | async-done | bytes 65552 | tf_op jit(solution)/shard_map/reduce_scatter | solution.py:285
  307.3 0.8 broadcast_multiply_fusion
  308.1 0.9 fusion.50
  309.0 1.2 convolution_add_fusion.2
  310.2 62.2 %reduce-scatter.13.cloned.1.call-done = f32[128,128]{0,1:T(8,128)} async-done(((f32[1024,128]{0,1:T(8,128)}), f32[128,128]{0,1:T(8,128)}) %reduce-scatter.13.cloned.1.call-update) | async-done | bytes 65552 | tf_op jit(solution)/shard_map/reduce_scatter | solution.py:286
  372.5 2.0 convolution_add_fusion.1
  374.5 0.8 fusion.82
  375.4 1.3 fusion.44
  376.9 1.1 fusion.51
  378.0 1.1 fusion.64
  379.3 1.3 fusion.66
  380.7 6.0 fusion.37
  386.8 1.1 copy-done.4
  388.0 4.6 fusion.20
  392.7 0.9 copy-done.25
  393.7 4.6 fusion.21
  400.1 7.4 all-reduce.14.cloned.1.call-done
  407.5 1.2 fusion.32
  408.7 21.6 %all-reduce.2 = (f32[1024]{0:T(1024)S(1)}, f32[1024]{0:T(1024)S(1)}) all-reduce(f32[1024]{0:T(1024)S(1)} %get-tuple-element.184, f32[1024]{0:T(1024)S(1)} %copy-done.46), channel_id=4, replica_groups=mesh['ctx'=8,'shard'=4] {'ctx'}, use_global_device_ids=true, to_apply=%region_30.31.clone | all-reduce | flops 2048 | bytes 16384
  431.6 2.0 fusion.28
  433.6 31.6 %reduce-scatter.23.cloned.1.call-done = f32[128,16]{0,1:T(8,128)} async-done(((f32[1024,16]{0,1:T(8,128)}), f32[128,16]{0,1:T(8,128)}) %reduce-scatter.23.cloned.1.call-update) | async-done | bytes 8208 | tf_op jit(solution)/shard_map/reduce_scatter | solution.py:328
  465.3 67.3 %reduce-scatter.21.cloned.1.call-done = f32[256,128]{1,0:T(8,128)} async-done(((f32[256,1024]{1,0:T(8,128)}), f32[256,128]{1,0:T(8,128)}) %reduce-scatter.21.cloned.1.call-update) | async-done | bytes 131088 | tf_op jit(solution)/shard_map/reduce_scatter | solution.py:326
  532.6 64.9 %reduce-scatter.19.cloned.1.call-done = f32[128,128]{1,0:T(8,128)} async-done(((f32[1024,128]{1,0:T(8,128)}), f32[128,128]{1,0:T(8,128)}) %reduce-scatter.19.cloned.1.call-update) | async-done | bytes 65552 | tf_op jit(solution)/shard_map/reduce_scatter | solution.py:325
  597.4 65.0 %reduce-scatter.17.cloned.1.call-done = f32[128,128]{1,0:T(8,128)} async-done(((f32[1024,128]{1,0:T(8,128)}), f32[128,128]{1,0:T(8,128)}) %reduce-scatter.17.cloned.1.call-update) | async-done | bytes 65552 | tf_op jit(solution)/shard_map/reduce_scatter | solution.py:324
  662.5 66.5 %reduce-scatter.15.cloned.1.call-done = f32[128,256]{1,0:T(8,128)} async-done(((f32[1024,256]{1,0:T(8,128)}), f32[128,256]{1,0:T(8,128)}) %reduce-scatter.15.cloned.1.call-update) | async-done | bytes 131088 | tf_op jit(solution)/shard_map/reduce_scatter | solution.py:323
  728.9 153.0 %reduce-scatter.29.cloned.1.call-done = f32[4,512,128]{2,1,0:T(8,128)} async-done(((f32[4,512,1024]{2,1,0:T(8,128)}), f32[4,512,128]{2,1,0:T(8,128)}) %reduce-scatter.29.cloned.1.call-update) | async-done | bytes 1048592 | tf_op jit(solution)/shard_map/reduce_scatter | solution.py:331
  881.9 152.7 %reduce-scatter.27.cloned.1.call-done = f32[4,128,512]{2,1,0:T(8,128)} async-done(((f32[4,1024,512]{2,1,0:T(8,128)}), f32[4,128,512]{2,1,0:T(8,128)}) %reduce-scatter.27.cloned.1.call-update) | async-done | bytes 1048592 | tf_op jit(solution)/shard_map/reduce_scatter | solution.py:330
  1034.6 153.0 %reduce-scatter.25.cloned.1.call-done = f32[4,128,512]{2,1,0:T(8,128)} async-done(((f32[4,1024,512]{2,1,0:T(8,128)}), f32[4,128,512]{2,1,0:T(8,128)}) %reduce-scatter.25.cloned.1.call-update) | async-done | bytes 1048592 | tf_op jit(solution)/shard_map/reduce_scatter | solution.py:329
  (217 shorter events, 15.6 us)
Async XLA Ops:
  7.2 66.5 %copy-start = (bf16[256,1024]{1,0:T(8,128)(2,1)S(1)}, bf16[256,1024]{1,0:T(8,128)(2,1)}, u32[]{:S(2)}) copy-start(bf16[256,1024]{1,0:T(8,128)(2,1)} %param.20) | copy-start | bytes 1572868
  7.2 100.4 %all-reduce.8.cloned.1.call-start = ((), (), s32[]{:S(2)}) async-start(), calls=%async_computation.10 | async-start | bytes 1048576 | tf_op jit(solution)/shard_map/psum | solution.py:172
  8.4 4.4 copy-start.44
  13.0 60.7 %copy-start.28 = (f32[128,64]{0,1:T(8,128)}, f32[128,64]{0,1:T(8,128)S(1)}, u32[]{:S(2)}) copy-start(f32[128,64]{0,1:T(8,128)S(1)} %get-tuple-element.243) | copy-start | bytes 98308
  13.0 60.7 %copy-start.30 = (f32[128,64]{0,1:T(8,128)}, f32[128,64]{0,1:T(8,128)S(1)}, u32[]{:S(2)}) copy-start(f32[128,64]{0,1:T(8,128)S(1)} %get-tuple-element.242) | copy-start | bytes 98308
  41.3 33.4 %copy-start.10 = (bf16[1024,128]{0,1:T(8,128)(2,1)}, bf16[1024,128]{0,1:T(8,128)(2,1)S(1)}, u32[]{:S(2)}) copy-start(bf16[1024,128]{0,1:T(8,128)(2,1)S(1)} %all_gather.4) | copy-start | bytes 786436
  72.3 2.4 copy-start.12
  72.3 2.5 copy-start.35
  73.2 2.4 copy-start.51
  74.8 125.5 %all-reduce.12.cloned.1.call-start = ((), (), s32[]{:S(2)}) async-start(), calls=%async_computation.12 | async-start | bytes 1048576 | tf_op jit(solution)/shard_map/psum | solution.py:220
  75.0 10.7 copy-start.50
  75.3 10.3 copy-start.43
  75.7 7.3 copy-start.1
  83.0 24.5 %copy-start.5 = (bf16[128,1024]{1,0:T(8,128)(2,1)S(1)}, bf16[128,1024]{1,0:T(8,128)(2,1)}, u32[]{:S(2)}) copy-start(bf16[128,1024]{1,0:T(8,128)(2,1)} %param.15) | copy-start | bytes 786436
  83.1 26.5 %copy-start.39 = (f32[1024]{0:T(1024)S(1)}, f32[1024]{0:T(1024)}, u32[]{:S(2)}) copy-start(f32[1024]{0:T(1024)} %param.21) | copy-start | bytes 12292
  85.8 38.3 %copy-start.41 = (pred[4,112]{1,0:T(4,128)(4,1)}, pred[4,112]{1,0:T(4,128)(4,1)S(1)}, u32[]{:S(2)}) copy-start(pred[4,112]{1,0:T(4,128)(4,1)S(1)} %fusion.40) | copy-start | bytes 1348
  108.8 3.0 copy-start.53
  109.7 2.1 copy-start.36
  111.8 12.3 %copy-start.3 = (bf16[448,1024]{1,0:T(8,128)(2,1)}, bf16[448,1024]{1,0:T(8,128)(2,1)S(1)}, u32[]{:S(2)}) copy-start(bf16[448,1024]{1,0:T(8,128)(2,1)S(1)} %gather_fusion) | copy-start | bytes 2752516
  119.3 1.7 copy-start.47
  119.3 27.0 %copy-start.38 = (f32[128,8]{0,1:T(8,128)}, f32[128,8]{0,1:T(8,128)S(1)}, u32[]{:S(2)}) copy-start(f32[128,8]{0,1:T(8,128)S(1)} %get-tuple-element.215) | copy-start | bytes 12292
  120.9 3.5 copy-start.14
  124.4 1.8 copy-start.23
  124.4 3.0 copy-start.6
  126.2 1.9 copy-start.16
  133.6 14.9 %copy-start.9 = (f32[448,1024]{1,0:T(8,128)S(1)}, f32[448,1024]{1,0:T(8,128)}, u32[]{:S(2)}) copy-start(f32[448,1024]{1,0:T(8,128)} %gather_fusion.2) | copy-start | bytes 5505028
  148.4 4.5 copy-start.48
  148.4 4.5 copy-start.2
  152.9 4.0 copy-start.24
  152.9 4.0 copy-start.26
  153.0 2.5 copy-start.15
  162.4 37.9 %copy-start.8 = (f32[128,1024]{1,0:T(8,128)S(1)}, f32[128,1024]{1,0:T(8,128)}, u32[]{:S(2)}) copy-start(f32[128,1024]{1,0:T(8,128)} %copy-done.7) | copy-start | bytes 1572868
  162.4 37.9 %copy-start.37 = (bf16[1024,16]{0,1:T(8,128)(2,1)S(1)}, bf16[1024,16]{0,1:T(8,128)(2,1)}, u32[]{:S(2)}) copy-start(bf16[1024,16]{0,1:T(8,128)(2,1)} %param.22) | copy-start | bytes 98308
  162.4 37.9 %copy-start.40 = (f32[1024]{0:T(1024)S(1)}, f32[1024]{0:T(1024)}, u32[]{:S(2)}) copy-start(f32[1024]{0:T(1024)} %param.21) | copy-start | bytes 12292
  162.4 37.9 %copy-start.54 = (f32[128]{0:T(128)S(1)}, f32[128]{0:T(128)}, u32[]{:S(2)}) copy-start(f32[128]{0:T(128)} %copy-done.53) | copy-start | bytes 1540
  166.7 72.2 %copy-start.11 = (bf16[1024,128]{0,1:T(8,128)(2,1)S(1)}, bf16[1024,128]{0,1:T(8,128)(2,1)}, u32[]{:S(2)}) copy-start(bf16[1024,128]{0,1:T(8,128)(2,1)} %copy-done.10) | copy-start | bytes 786436
  166.7 72.2 %copy-start.13 = (bf16[1024,128]{0,1:T(8,128)(2,1)S(1)}, bf16[1024,128]{0,1:T(8,128)(2,1)}, u32[]{:S(2)}) copy-start(bf16[1024,128]{0,1:T(8,128)(2,1)} %copy-done.12) | copy-start | bytes 786436
  166.7 72.2 %copy-start.52 = (f32[2,2,128]{2,1,0:T(2,128)S(1)}, f32[2,2,128]{2,1,0:T(2,128)}, u32[]{:S(2)}) copy-start(f32[2,2,128]{2,1,0:T(2,128)} %copy-done.51) | copy-start | bytes 6148
  166.8 67.9 %all-reduce.10.cloned.1.call-start = ((), (), s32[]{:S(2)}) async-start(), calls=%async_computation.11 | async-start | bytes 524288 | tf_op jit(solution)/shard_map/psum | solution.py:198
  167.5 139.8 %reduce-scatter.11.cloned.1.call-start = ((), (), s32[]{:S(2)}) async-start(), calls=%async_computation.13 | async-start | bytes 589824 | tf_op jit(solution)/shard_map/reduce_scatter | solution.py:285
  238.9 3.0 copy-start.29
  238.9 3.0 copy-start.31
  239.0 3.5 copy-start.18
  239.0 1.8 copy-start.19
  239.0 1.8 copy-start.21
  241.8 130.6 %copy-start.32 = (bf16[1024,128]{1,0:T(8,128)(2,1)S(1)}, bf16[1024,128]{1,0:T(8,128)(2,1)}, u32[]{:S(2)}) copy-start(bf16[1024,128]{1,0:T(8,128)(2,1)} %param.19) | copy-start | bytes 786436
  241.9 130.6 %reduce-scatter.13.cloned.1.call-start = ((), (), s32[]{:S(2)}) async-start(), calls=%async_computation.14 | async-start | bytes 589824 | tf_op jit(solution)/shard_map/reduce_scatter | solution.py:286
  242.0 134.8 %copy-start.34 = (f32[1024]{0:T(1024)S(1)}, f32[1024]{0:T(1024)}, u32[]{:S(2)}) copy-start(f32[1024]{0:T(1024)} %param.16) | copy-start | bytes 12292
  242.0 134.8 %copy-start.45 = (f32[128]{0:T(128)S(1)}, f32[128]{0:T(128)}, u32[]{:S(2)}) copy-start(f32[128]{0:T(128)} %copy-done.44) | copy-start | bytes 1540
  242.5 165.1 %all-reduce.14.cloned.1.call-start = ((), (), s32[]{:S(2)}) async-start(), calls=%async_computation.15 | async-start | bytes 1048576 | tf_op jit(solution)/shard_map/psum | solution.py:307
  372.5 4.4 copy-start.33
  374.4 6.2 copy-start.17
  374.4 6.2 copy-start.49
  374.5 90.8 %reduce-scatter.23.cloned.1.call-start = ((), (), s32[]{:S(2)}) async-start(), calls=%async_computation.20 | async-start | bytes 73728 | tf_op jit(solution)/shard_map/reduce_scatter | solution.py:328
  375.4 157.2 %reduce-scatter.21.cloned.1.call-start = ((), (), s32[]{:S(2)}) async-start(), calls=%async_computation.19 | async-start | bytes 1179648 | tf_op jit(solution)/shard_map/reduce_scatter | solution.py:326
  376.8 220.7 %reduce-scatter.19.cloned.1.call-start = ((), (), s32[]{:S(2)}) async-start(), calls=%async_computation.18 | async-start | bytes 589824 | tf_op jit(solution)/shard_map/reduce_scatter | solution.py:325
  378.0 284.5 %reduce-scatter.17.cloned.1.call-start = ((), (), s32[]{:S(2)}) async-start(), calls=%async_computation.17 | async-start | bytes 589824 | tf_op jit(solution)/shard_map/reduce_scatter | solution.py:324
  379.2 349.7 %reduce-scatter.15.cloned.1.call-start = ((), (), s32[]{:S(2)}) async-start(), calls=%async_computation.16 | async-start | bytes 1179648 | tf_op jit(solution)/shard_map/reduce_scatter | solution.py:323
  380.6 501.3 %reduce-scatter.29.cloned.1.call-start = ((), (), s32[]{:S(2)}) async-start(), calls=%async_computation.23 | async-start | bytes 9437184 | tf_op jit(solution)/shard_map/reduce_scatter | solution.py:331
  386.7 1.3 copy-start.27
  386.7 1.3 copy-start.42
  386.8 647.8 %reduce-scatter.27.cloned.1.call-start = ((), (), s32[]{:S(2)}) async-start(), calls=%async_computation.22 | async-start | bytes 9437184 | tf_op jit(solution)/shard_map/reduce_scatter | solution.py:330
  392.7 794.9 %reduce-scatter.25.cloned.1.call-start = ((), (), s32[]{:S(2)}) async-start(), calls=%async_computation.21 | async-start | bytes 9437184 | tf_op jit(solution)/shard_map/reduce_scatter | solution.py:329
  398.2 10.5 copy-start.46
  (6 other events, 5.4 us)
Sparse Core Ops, SparseCore 0:
  74.9 32.6 all-reduce.7
  166.9 33.3 all-reduce.11
  202.6 31.9 all-reduce.9
  242.0 65.2 reduce-scatter.10
  311.0 61.3 reduce-scatter.12
  375.3 32.1 all-reduce.13
  411.5 53.6 reduce-scatter.22
  469.6 62.9 reduce-scatter.20
  536.5 60.8 reduce-scatter.18
  601.6 60.8 reduce-scatter.16
  666.4 62.4 reduce-scatter.14
  733.4 148.4 reduce-scatter.28
  886.1 148.4 reduce-scatter.26
  1039.1 148.4 reduce-scatter.24
where the time goes:
time: 1200 us; the launch traced here: 1190 us
  waiting for transfers between devices  975 us (81%)
  blocking collectives  86.6 us (7%)
  matrix products  48.7 us (4%)
  local copies, waits for them, and re-layouts  44 us (4%)
  other arithmetic  23.5 us (2%)
  between operations  15.5 us (1%)
    reduce_scatter x1, waiting for transfers between devices, body(): lax.psum_scatter(down_part, 'ctx', scatter_dimension=2, tiled=True)  153 us
    reduce_scatter x1, waiting for transfers between devices, body(): lax.psum_scatter(gate_part, 'ctx', scatter_dimension=1, tiled=True)  153 us
    reduce_scatter x1, waiting for transfers between devices, body(): lax.psum_scatter(up_part, 'ctx', scatter_dimension=1, tiled=True)  153 us
    reduce_scatter x1, waiting for transfers between devices, body(): lax.psum_scatter(o_part, 'ctx', scatter_dimension=1, tiled=True)  67.3 us
    reduce_scatter x1, waiting for transfers between devices, body(): lax.psum_scatter(q_part, 'ctx', scatter_dimension=0, tiled=True)  66.5 us
    reduce_scatter x1, waiting for transfers between devices, body(): lax.psum_scatter(k_part, 'ctx', scatter_dimension=0, tiled=True)  65 us
    reduce_scatter x1, waiting for transfers between devices, body(): lax.psum_scatter(v_part, 'ctx', scatter_dimension=0, tiled=True)  64.9 us
    reduce_scatter x1, waiting for transfers between devices, body(): lax.psum_scatter(d_key_term, 'ctx', scatter_dimension=0, tiled=True)  64.4 us
  transfers between devices with their start and end apart: 14, of which 14 were waited for; matrix products, arithmetic and copies ran while one was open for 4% of the time, Pallas kernels for 0%

commit v1 on v0

v1 whole, which is shorter than its diff:
```python
import functools
import math

import jax
import jax.numpy as jnp
import numpy as np
from jax import lax
from jax.experimental import pallas as pl
from jax.experimental.pallas import tpu as pltpu
from jax.sharding import PartitionSpec as P

HD = 64
NORM_EPS = 1e-06
ROPE_BASE = 10000.0
BF = jnp.bfloat16
F32 = jnp.float32
LANES = 128
COST = 0.05
VMEM_LIMIT = 56 * 1024 * 1024


def nn(a, b):
    return lax.dot_general(a, b, (((1,), (0,)), ((), ())), preferred_element_type=F32)


def nt(a, b):
    return lax.dot_general(a, b, (((1,), (1,)), ((), ())), preferred_element_type=F32)


def tn(a, b):
    return lax.dot_general(a, b, (((0,), (0,)), ((), ())), preferred_element_type=F32)


def rope_constants(seq_len):
    half = HD // 2
    steps = np.arange(half, dtype=np.float32) * np.float32(2.0 / HD)
    inv_freq = np.exp(np.float32(-math.log(ROPE_BASE)) * steps).astype(np.float32)
    angles = np.arange(seq_len, dtype=np.float32)[:, None] * inv_freq[None, :]
    cos, sin = np.cos(angles), np.sin(angles)
    cos_tab = np.concatenate([cos, cos, cos, cos], axis=1)
    sin_tab = np.concatenate([-sin, sin, -sin, sin], axis=1)
    return jnp.asarray(cos_tab, F32), jnp.asarray(sin_tab, F32)


def swap_halves(vals):
    width = vals.shape[-1]
    lane = lax.broadcasted_iota(jnp.int32, vals.shape, 1)
    up = pltpu.roll(vals, width - HD // 2, 1)
    down = pltpu.roll(vals, HD // 2, 1)
    return jnp.where(lane % HD < HD // 2, up, down)


def widen(tab, width):
    reps = width // tab.shape[1]
    return tab if reps == 1 else jnp.concatenate([tab] * reps, axis=1)


def rope(vals, cos, sin):
    width = vals.shape[-1]
    return vals * widen(cos, width) + swap_halves(vals) * widen(sin, width)


def unrope(vals, cos, sin):
    width = vals.shape[-1]
    return vals * widen(cos, width) - swap_halves(vals) * widen(sin, width)


def params(semantics=None):
    return pltpu.CompilerParams(dimension_semantics=semantics, vmem_limit_bytes=VMEM_LIMIT)


def cost(micros):
    return pl.CostEstimate(flops=0, transcendentals=0, bytes_accessed=int(micros * COST * 3.69e6))


def project_kernel(pos_ref, x_ref, gain_ref, wq_ref, wk_ref, wv_ref, cos_ref, sin_ref, og_ref, kv_ref, aux_ref):
    x = x_ref[...].astype(F32)
    inv = lax.rsqrt(jnp.mean(x * x, axis=-1, keepdims=True) + NORM_EPS)
    x1 = (x * inv * gain_ref[...]).astype(BF)
    cos, sin = cos_ref[...], sin_ref[...]
    q = rope(nn(x1, wq_ref[...]), cos, sin).astype(BF)
    q = (q.astype(F32) * (HD**-0.5)).astype(BF)
    k = rope(nn(x1, wk_ref[...]), cos, sin).astype(BF)
    v = nn(x1, wv_ref[...]).astype(BF)
    peers, _, rows, _ = aux_ref.shape
    og = og_ref[...].astype(BF)
    aux = [t[:, m * LANES : (m + 1) * LANES] for t in (q, og) for m in range(t.shape[1] // LANES)]
    db = x.shape[1] // peers
    for p in range(peers):
        kv_ref[p, 0] = k
        kv_ref[p, 1] = v
        for m in range(len(aux)):
            aux_ref[p, m] = aux[m]
        cols = x1[:, p * db : (p + 1) * db]
        if db < LANES:
            cols = jnp.concatenate([cols, jnp.zeros((rows, LANES - db), BF)], axis=1)
        aux_ref[p, len(aux)] = cols


def project(pos, peers, block_in, gain, wq, wk, wv, cos, sin, out_grad, piece):
    rows, width = block_in.shape
    planes = (wq.shape[1] + piece) // LANES + 1
    full = lambda shape: pl.BlockSpec(shape, lambda g, p: (0,) * len(shape))
    tab = pl.BlockSpec((rows, LANES), lambda g, p: (p[0], 0))
    return pl.pallas_call(
        project_kernel,
        grid_spec=pltpu.PrefetchScalarGridSpec(
            num_scalar_prefetch=1,
            grid=(1,),
            in_specs=[
                full((rows, width)),
                full((1, width)),
                full(wq.shape),
                full(wk.shape),
                full(wv.shape),
                tab,
                tab,
                pl.BlockSpec((rows, piece), lambda g, p: (0, p[1])),
            ],
            out_specs=[full((peers, 2, rows, LANES)), full((peers, planes, rows, LANES))],
        ),
        out_shape=[
            jax.ShapeDtypeStruct((peers, 2, rows, LANES), BF),
            jax.ShapeDtypeStruct((peers, planes, rows, LANES), BF),
        ],
        compiler_params=params(),
        cost_estimate=cost(3),
        name="project",
    )(pos, block_in, gain, wq, wk, wv, cos, sin, out_grad)


def attend_kernel(pos_ref, q_ref, kv_ref, out_ref):
    i = pos_ref[0]
    blocks, _, rows, kw = kv_ref.shape
    heads = kw // HD
    group = q_ref.shape[2] // HD
    n = blocks * rows
    k_all = kv_ref[:, 0].reshape(n, kw)
    v_all = kv_ref[:, 1].reshape(n, kw)
    col = lax.broadcasted_iota(jnp.int32, (group * rows, n), 1)
    row = lax.broadcasted_iota(jnp.int32, (group * rows, n), 0) % rows + i * rows
    allowed = col <= row
    for h in range(heads):
        k = k_all[:, h * HD : (h + 1) * HD]
        v = v_all[:, h * HD : (h + 1) * HD]
        q = jnp.concatenate([q_ref[h, :, g * HD : (g + 1) * HD] for g in range(group)], axis=0)
        s = jnp.where(allowed, nt(q, k), -1e30)
        top = jnp.max(s, axis=-1, keepdims=True)
        e = jnp.exp(s - top)
        total = jnp.sum(e, axis=-1, keepdims=True)
        o = (nn(e.astype(BF), v) / total).astype(BF)
        for g in range(group):
            c = (h * group + g) * HD
            out_ref[:, c : c + HD] = o[g * rows : (g + 1) * rows]


def attend(pos, aux, kv_all):
    _, _, rows, _ = aux.shape
    q_planes = kv_all.shape[3] // HD
    return pl.pallas_call(
        attend_kernel,
        grid_spec=pltpu.PrefetchScalarGridSpec(
            num_scalar_prefetch=1,
            grid=(1,),
            in_specs=[
                pl.BlockSpec((None, q_planes, rows, LANES), lambda g, p: (0, 0, 0, 0)),
                pl.BlockSpec(kv_all.shape, lambda g, p: (0, 0, 0, 0)),
            ],
            out_specs=pl.BlockSpec((rows, q_planes * LANES), lambda g, p: (0, 0)),
        ),
        out_shape=jax.ShapeDtypeStruct((rows, q_planes * LANES), BF),
        compiler_params=params(),
        cost_estimate=cost(3),
        name="attend",
    )(pos, aux, kv_all)


def mid_kernel(n_sh, *refs):
    pos_ref = refs[0]
    heads = refs[1 : n_sh + 1]
    ow = refs[n_sh + 1 : 2 * n_sh + 1]
    x_ref, gain_ref, router_ref, routes_ref, resid_ref, x2_ref, gates_ref, send_ref = refs[2 * n_sh + 1 :]
    acc = x_ref[...].astype(F32)
    for h, w in zip(heads, ow):
        acc = acc + nn(h[...], w[...])
    resid_ref[...] = acc
    inv = lax.rsqrt(jnp.mean(acc * acc, axis=-1, keepdims=True) + NORM_EPS)
    x2 = (acc * inv * gain_ref[...]).astype(BF)
    x2_ref[...] = x2
    logits = nn(x2, router_ref[...])
    lane = lax.broadcasted_iota(jnp.int32, logits.shape, 1)
    chosen = lane < 0
    for k in range(routes_ref.shape[1]):
        chosen = chosen | (routes_ref[:, k : k + 1] == lane)
    masked = jnp.where(chosen, logits, -1e30)
    e = jnp.where(chosen, jnp.exp(masked - jnp.max(masked, axis=-1, keepdims=True)), 0.0)
    gates = e / jnp.sum(e, axis=-1, keepdims=True)
    gates_ref[...] = gates
    rows, width = acc.shape
    planes = width // n_sh // LANES
    n_gate = send_ref.shape[1] - planes * rows
    g_rows = jnp.transpose(gates)[:n_gate].astype(BF)
    s = pos_ref[1]
    mine = []
    for m in range(planes):
        plane = x2[:, m * LANES : (m + 1) * LANES]
        for k in range(1, n_sh):
            at = (k * planes + m) * LANES
            plane = jnp.where(s == k, x2[:, at : at + LANES], plane)
        mine.append(plane)
    for m in range(planes):
        send_ref[0, m * rows : (m + 1) * rows] = mine[m]
    send_ref[0, planes * rows :] = g_rows


def mid(pos, n_gate, heads, ow, block_in, gain, router_pad, routes):
    rows, width = block_in.shape
    n_sh = len(heads)
    total = width // n_sh // LANES * rows + n_gate
    return pl.pallas_call(
        functools.partial(mid_kernel, n_sh),
        in_specs=[pl.BlockSpec(memory_space=pltpu.SMEM)] + [pl.BlockSpec()] * (2 * n_sh + 4),
        out_shape=[
            jax.ShapeDtypeStruct((rows, width), F32),
            jax.ShapeDtypeStruct((rows, width), BF),
            jax.ShapeDtypeStruct((rows, LANES), F32),
            jax.ShapeDtypeStruct((1, total, LANES), BF),
        ],
        compiler_params=params(),
        cost_estimate=cost(4),
        name="mid",
    )(pos, *heads, *ow, block_in, gain, router_pad, routes)


def expert_terms(pg, pu, g_out, gate):
    sig = jax.nn.sigmoid(pg)
    silu = pg * sig
    hid = silu * pu
    dh = gate * g_out
    dpg = (dh * pu * (sig * (1.0 + pg * (1.0 - sig)))).astype(BF)
    dpu = (dh * silu).astype(BF)
    return hid, dpg, dpu


def experts_own_kernel(pos_ref, x_ref, og_ref, gates_ref, wg_ref, wu_ref, wd_ref, moe_ref, ex_ref, acc_m, acc_d, acc_g):
    e = pl.program_id(0)
    n_e = pl.num_programs(0)
    width = x_ref.shape[1]

    @pl.when(e == 0)
    def _():
        acc_m[...] = jnp.zeros_like(acc_m)
        acc_d[...] = jnp.zeros_like(acc_d)
        acc_g[...] = jnp.zeros_like(acc_g)

    lane = lax.broadcasted_iota(jnp.int32, gates_ref.shape, 1)
    mine = lane == pos_ref[1] * n_e + e
    gate = jnp.sum(jnp.where(mine, gates_ref[...], 0.0), axis=-1, keepdims=True)
    x = x_ref[...]
    wg, wu, wd = wg_ref[0], wu_ref[0], wd_ref[0]
    pg, pu, g_out = nn(x, wg), nn(x, wu), nt(og_ref[...].astype(BF), wd)
    hid, dpg, dpu = expert_terms(pg, pu, g_out, gate)
    d_gate = jnp.sum(hid.astype(BF).astype(F32) * g_out, axis=-1, keepdims=True)
    acc_m[...] += nn((gate * hid).astype(BF), wd)
    acc_d[...] += nt(dpg, wg) + nt(dpu, wu)
    acc_g[...] += jnp.where(mine, d_gate, 0.0)

    @pl.when(e == n_e - 1)
    def _():
        moe_ref[...] = acc_m[...].astype(BF)
        ex_ref[:, :width] = acc_d[...].astype(BF)
        ex_ref[:, width:] = acc_g[...].astype(BF)


def experts_own(pos, x2, og, gates, wg, wu, wd):
    rows, width = x2.shape
    n_e, _, ff = wg.shape
    full = lambda shape: pl.BlockSpec(shape, lambda e, p: (0,) * len(shape))
    return pl.pallas_call(
        experts_own_kernel,
        grid_spec=pltpu.PrefetchScalarGridSpec(
            num_scalar_prefetch=1,
            grid=(n_e,),
            in_specs=[
                full((rows, width)),
                full((rows, width)),
                full((rows, LANES)),
                pl.BlockSpec((1, width, ff), lambda e, p: (e, 0, 0)),
                pl.BlockSpec((1, width, ff), lambda e, p: (e, 0, 0)),
                pl.BlockSpec((1, ff, width), lambda e, p: (e, 0, 0)),
            ],
            out_specs=[full((rows, width)), full((rows, width + LANES))],
            scratch_shapes=[
                pltpu.VMEM((rows, width), F32),
                pltpu.VMEM((rows, width), F32),
                pltpu.VMEM((rows, LANES), F32),
            ],
        ),
        out_shape=[
            jax.ShapeDtypeStruct((rows, width), BF),
            jax.ShapeDtypeStruct((rows, width + LANES), BF),
        ],
        compiler_params=params(("arbitrary",)),
        cost_estimate=cost(11),
        name="experts_own",
    )(pos, x2, og, gates, wg, wu, wd)


def back_mid_kernel(
    n_exp, ex_ref, far_ref, resid_ref, gain_ref, gates_ref, router_ref, og_ref, ow_ref, dmid_ref, send_ref, cols_ref
):
    rows, width = resid_ref.shape
    ex = ex_ref[...].astype(F32) + far_ref[...].astype(F32)
    gates = gates_ref[...]
    d_gate = ex[:, width:]
    d_logits = gates * (d_gate - jnp.sum(gates * d_gate, axis=-1, keepdims=True))
    d_norm = ex[:, :width] + nt(d_logits.astype(BF), router_ref[...])
    resid = resid_ref[...]
    inv = lax.rsqrt(jnp.mean(resid * resid, axis=-1, keepdims=True) + NORM_EPS)
    hat = resid * inv
    d_gain = jnp.sum(d_norm * hat, axis=0, keepdims=True)
    u = gain_ref[...] * d_norm
    inner = jnp.mean(u * hat, axis=-1, keepdims=True)
    d_mid = og_ref[...] + inv * (u - hat * inner)
    dmid_ref[...] = d_mid
    dmb = d_mid.astype(BF)
    d_heads = nt(dmb, ow_ref[...]).astype(BF)
    planes = d_heads.shape[1] // LANES
    gain_rows = [d_gain[:, k * LANES : (k + 1) * LANES] for k in range(width // LANES)]
    small = jnp.concatenate([jnp.transpose(d_logits)[:n_exp]] + gain_rows, axis=0).astype(BF)
    peers = send_ref.shape[0]
    db = width // peers
    for p in range(peers):
        for m in range(planes):
            send_ref[p, m * rows : (m + 1) * rows] = d_heads[:, m * LANES : (m + 1) * LANES]
        send_ref[p, planes * rows :] = small
        cols_ref[p] = dmb[:, p * db : (p + 1) * db]


def back_mid(peers, n_exp, ex, far, resid, gain, gates, router_pad, og, ow):
    rows, width = resid.shape
    total = ow.shape[0] // LANES * rows + n_exp + width // LANES
    return pl.pallas_call(
        functools.partial(back_mid_kernel, n_exp),
        out_shape=[
            jax.ShapeDtypeStruct((rows, width), F32),
            jax.ShapeDtypeStruct((peers, total, LANES), BF),
            jax.ShapeDtypeStruct((peers, rows, width // peers), BF),
        ],
        compiler_params=params(),
        cost_estimate=cost(3),
        name="back_mid",
    )(ex, far, resid, gain, gates, router_pad, og, ow)


def attend_back_kernel(
    pos_ref, q_ref, kv_ref, do_ref, cos_ref, sin_ref, wq_ref, wk_ref, wv_ref,
    dn_ref, qkvg_ref, ho_ref, qs, ks, vs, dos, dqs, hos, dkt, dvt, dqkv,
):
    i = pos_ref[0]
    blocks, _, rows, kw = kv_ref.shape
    heads = kw // HD
    group = LANES // HD
    q_planes = heads
    qw = q_planes * LANES
    n = blocks * rows
    bq = 2 * rows if n <= 1024 else rows // 2
    for j in range(blocks):
        at = slice(j * rows, (j + 1) * rows)
        kb, vb = kv_ref[j, 0], kv_ref[j, 1]
        for h in range(heads):
            ks[h, at] = kb[:, h * HD : (h + 1) * HD]
            vs[h, at] = vb[:, h * HD : (h + 1) * HD]
            for g in range(group):
                qs[h, g, at] = q_ref[j, h, :, g * HD : (g + 1) * HD]
                dos[h, g, at] = do_ref[j, h * rows : (h + 1) * rows, g * HD : (g + 1) * HD]
    dkt[...] = jnp.zeros_like(dkt)
    dvt[...] = jnp.zeros_like(dvt)

    def step(h, start, ext, full):
        k, v = ks[h, :ext], vs[h, :ext]
        q = jnp.concatenate([qs[h, g, pl.ds(start, bq)] for g in range(group)], axis=0)
        do = jnp.concatenate([dos[h, g, pl.ds(start, bq)] for g in range(group)], axis=0)
        s = nt(q, k)
        edge = s if full else s[:, ext - bq :]
        first = 0 if full else ext - bq
        col = lax.broadcasted_iota(jnp.int32, edge.shape, 1) + first
        row = lax.broadcasted_iota(jnp.int32, edge.shape, 0) % bq + start
        edge = jnp.where(col <= row, edge, -1e30)
        s = edge if first == 0 else jnp.concatenate([s[:, :first], edge], axis=1)
        top = jnp.max(s, axis=-1, keepdims=True)
        e = jnp.exp(s - top)
        p = e * (1.0 / jnp.sum(e, axis=-1, keepdims=True))
        dp = nt(do, v)
        delta = jnp.sum(p * dp, axis=-1, keepdims=True)
        ds = (p * (dp - delta)).astype(BF)
        pb = p.astype(BF)
        o = nn(pb, v)
        dq = nn(ds, k) * (HD**-0.5)
        dkt[h, :, :ext] += tn(q, ds)
        dvt[h, :, :ext] += tn(do, pb)
        for g in range(group):
            dqs[h, g, pl.ds(start, bq)] = dq[g * bq : (g + 1) * bq]
            hos[h, g, pl.ds(start, bq)] = o[g * bq : (g + 1) * bq].astype(BF)

    def per_head(h, carry):
        if n <= 1024:
            for r in range(n // bq):
                step(h, r * bq, (r + 1) * bq, False)
        else:

            def loop(r, c):
                step(h, pl.multiple_of(r * bq, bq), n, True)
                return c

            lax.fori_loop(0, n // bq, loop, 0)
        return carry

    lax.fori_loop(0, heads, per_head, 0)
    pieces = [(h, g) for h in range(heads) for g in range(group)]
    qkvg_ref[...] = jnp.zeros_like(qkvg_ref)

    def per_block(j, carry):
        at = pl.ds(pl.multiple_of(j * rows, rows), rows)
        cos, sin = cos_ref[at], sin_ref[at]
        ho_ref[j] = jnp.concatenate([hos[h, g, at] for h, g in pieces], axis=1)
        dq = jnp.concatenate([dqs[h, g, at] for h, g in pieces], axis=1)
        dk = jnp.transpose(jnp.concatenate([dkt[h, :, at] for h in range(heads)], axis=0))
        dv = jnp.transpose(jnp.concatenate([dvt[h, :, at] for h in range(heads)], axis=0))
        out = jnp.concatenate([unrope(dq, cos, sin), unrope(dk, cos, sin), dv], axis=1).astype(BF)
        dqkv[j] = out
        qkvg_ref[...] += tn(q_ref[j, q_ref.shape[1] - 1], out)
        return carry

    lax.fori_loop(0, blocks, per_block, 0)
    own = dqkv[i]
    width = wq_ref.shape[0]
    db = width // blocks
    dn_ref[:, :width] = (
        nt(own[:, :qw], wq_ref[...]) + nt(own[:, qw : qw + kw], wk_ref[...]) + nt(own[:, qw + kw :], wv_ref[...])
    ).astype(BF)
    mine = pl.ds(pl.multiple_of(i * db, db), db)
    w_rows = jnp.concatenate([wq_ref[mine], wk_ref[mine], wv_ref[mine]], axis=1).astype(F32)
    gain = jnp.sum(qkvg_ref[:db] * w_rows, axis=1, keepdims=True)
    if db < rows:
        gain = jnp.concatenate([gain, jnp.zeros((rows - db, 1), F32)], axis=0)
    dn_ref[:, width:] = jnp.broadcast_to(gain, (rows, LANES)).astype(BF)


def attend_back(pos, q_all, kv_all, do_all, cos, sin, wq, wk, wv):
    blocks, _, rows, kw = kv_all.shape
    width, qw = wq.shape
    heads, group = kw // HD, LANES // HD
    n = blocks * rows
    return pl.pallas_call(
        attend_back_kernel,
        in_specs=[pl.BlockSpec(memory_space=pltpu.SMEM)] + [pl.BlockSpec()] * 8,
        out_shape=[
            jax.ShapeDtypeStruct((rows, width + LANES), BF),
            jax.ShapeDtypeStruct((LANES, qw + 2 * kw), F32),
            jax.ShapeDtypeStruct((blocks, rows, qw), BF),
        ],
        scratch_shapes=[
            pltpu.VMEM((heads, group, n, HD), BF),
            pltpu.VMEM((heads, n, HD), BF),
            pltpu.VMEM((heads, n, HD), BF),
            pltpu.VMEM((heads, group, n, HD), BF),
            pltpu.VMEM((heads, group, n, HD), F32),
            pltpu.VMEM((heads, group, n, HD), BF),
            pltpu.VMEM((heads, HD, n), F32),
            pltpu.VMEM((heads, HD, n), F32),
            pltpu.VMEM((blocks, rows, qw + 2 * kw), BF),
        ],
        compiler_params=params(),
        cost_estimate=cost(18),
        name="attend_back",
    )(pos, q_all, kv_all, do_all, cos, sin, wq, wk, wv)


def experts_all_kernel(n_sh, rows, *refs):
    pos_ref, refs = refs[0], refs[1:]
    xs, ogs = refs[:n_sh], refs[n_sh : 2 * n_sh]
    gates_ref = refs[2 * n_sh]
    base = 2 * n_sh + 1
    wgs, wus, wds = (refs[base + k * n_sh : base + (k + 1) * n_sh] for k in range(3))
    gg_ref, ug_ref, dg_ref, xc_ref, acc = refs[base + 3 * n_sh :]
    e, c = pl.program_id(0), pl.program_id(1)
    nb = xs[0].shape[0]
    tb = nb * rows
    planes = wgs[0].shape[1] // LANES
    lane = lax.broadcasted_iota(jnp.int32, (tb, LANES), 1)
    mine = lane == pos_ref[1] * pl.num_programs(0) + e
    gate = jnp.sum(jnp.where(mine, gates_ref[...], 0.0), axis=-1, keepdims=True)
    x_planes = [[x[:, m * rows : (m + 1) * rows].reshape(tb, LANES) for m in range(planes)] for x in xs]
    block = [pos_ref[3 + c * nb + t] for t in range(nb)]
    o_planes = [[jnp.concatenate([o[j, m] for j in block], axis=0) for m in range(planes)] for o in ogs]
    xv = [jnp.concatenate(p, axis=1) for p in x_planes]
    ov = [jnp.concatenate(p, axis=1) for p in o_planes]
    pg = sum(nn(x, w[0]) for x, w in zip(xv, wgs))
    pu = sum(nn(x, w[0]) for x, w in zip(xv, wus))
    g_out = sum(nt(o, w[0]) for o, w in zip(ov, wds))
    hid, dpg, dpu = expert_terms(pg, pu, g_out, gate)
    hg = (gate * hid).astype(BF)
    plane = pos_ref[2]
    xc, oc = x_planes[0][0], o_planes[0][0]
    for b in range(n_sh):
        for m in range(planes):
            hit = plane == (pos_ref[1] ^ b) * planes + m
            xc = jnp.where(hit, x_planes[b][m], xc)
            oc = jnp.where(hit, o_planes[b][m], oc)
    for t, j in enumerate(block):
        xc_ref[j] = xc[t * rows : (t + 1) * rows]
    gg, ug, dg = tn(xc, dpg), tn(xc, dpu), tn(oc, hg)

    @pl.when(c == 0)
    def _():
        gg_ref[0] = gg
        ug_ref[0] = ug
        acc[...] = dg

    @pl.when(c > 0)
    def _():
        gg_ref[0] += gg
        ug_ref[0] += ug
        acc[...] += dg

    @pl.when(c == pl.num_programs(1) - 1)
    def _():
        dg_ref[0] = jnp.transpose(acc[...])


def experts_all(pos, xs, ogs, gates, wg, wu, wd):
    n_sh = len(xs)
    blocks, total, _ = xs[0].shape
    _, planes, rows, _ = ogs[0].shape
    piece = planes * LANES
    n = blocks * rows
    n_e, width, ff = wg.shape
    nb = math.gcd(blocks, 4)
    x_tok = pl.BlockSpec((nb, total, LANES), lambda e, c, p: (c, 0, 0))
    o_tok = pl.BlockSpec(ogs[0].shape, lambda e, c, p: (0, 0, 0, 0))
    row_w = lambda b: pl.BlockSpec((1, piece, ff), lambda e, c, p, b=b: (e, p[1] ^ b, 0))
    col_w = lambda b: pl.BlockSpec((1, ff, piece), lambda e, c, p, b=b: (e, 0, p[1] ^ b))
    out = pl.BlockSpec((1, LANES, ff), lambda e, c, p: (e, 0, 0))
    out_t = pl.BlockSpec((1, ff, LANES), lambda e, c, p: (e, 0, 0))
    sh = range(n_sh)
    return pl.pallas_call(
        functools.partial(experts_all_kernel, n_sh, rows),
        grid_spec=pltpu.PrefetchScalarGridSpec(
            num_scalar_prefetch=1,
            grid=(n_e, blocks // nb),
            in_specs=[x_tok for _ in sh]
            + [o_tok for _ in sh]
            + [pl.BlockSpec((nb * rows, LANES), lambda e, c, p: (c, 0))]
            + [row_w(b) for b in sh]
            + [row_w(b) for b in sh]
            + [col_w(b) for b in sh],
            out_specs=[out, out, out_t, pl.BlockSpec((blocks, rows, LANES), lambda e, c, p: (0, 0, 0))],
            scratch_shapes=[pltpu.VMEM((LANES, ff), F32)],
        ),
        out_shape=[jax.ShapeDtypeStruct((n_e, LANES, ff), F32)] * 2
        + [jax.ShapeDtypeStruct((n_e, ff, LANES), F32), jax.ShapeDtypeStruct((blocks, rows, LANES), BF)],
        compiler_params=params(("arbitrary", "arbitrary")),
        cost_estimate=cost(25),
        name="experts_all",
    )(pos, *xs, *ogs, gates, *[wg] * n_sh, *[wu] * n_sh, *[wd] * n_sh)


def finish_kernel(dn_ref, far_ref, x_ref, gain_ref, dmid_ref, out_ref, dgain_ref):
    width = x_ref.shape[1]
    dn = dn_ref[...].astype(F32) + far_ref[...].astype(F32)
    dgain_ref[...] = dn[:, width:]
    x = x_ref[...].astype(F32)
    inv = lax.rsqrt(jnp.mean(x * x, axis=-1, keepdims=True) + NORM_EPS)
    hat = x * inv
    u = gain_ref[...] * dn[:, :width]
    out_ref[...] = dmid_ref[...] + inv * (u - hat * jnp.mean(u * hat, axis=-1, keepdims=True))


def finish(dn, far, block_in, gain, d_mid):
    rows, width = block_in.shape
    return pl.pallas_call(
        finish_kernel,
        out_shape=[jax.ShapeDtypeStruct((rows, width), F32), jax.ShapeDtypeStruct((rows, LANES), F32)],
        compiler_params=params(),
        cost_estimate=cost(2),
        name="finish",
    )(dn, far, block_in, gain, d_mid)


def exchange(x, bit):
    size = lax.axis_size("shard")
    return lax.ppermute(x, "shard", [(j, j ^ bit) for j in range(size)])


def gather_ctx(x):
    size = lax.axis_size("ctx")
    bit = size // 2
    while bit:
        far = lax.ppermute(x, "ctx", [(j, j ^ bit) for j in range(size)])
        x = jnp.concatenate([x, far], axis=0)
        bit //= 2
    return x


def ctx_order(size):
    order = [0]
    bit = size // 2
    while bit:
        order = order + [o ^ bit for o in order]
        bit //= 2
    return jnp.array(order, jnp.int32) ^ lax.axis_index("ctx")


def swap_ctx(x):
    return lax.all_to_all(x, "ctx", 0, 0, tiled=True)


def gather_shard(x):
    found = {0: x}
    bit = lax.axis_size("shard") // 2
    while bit:
        for off in list(found):
            found[off ^ bit] = exchange(found[off], bit)
        bit //= 2
    return [found[b] for b in range(len(found))]


def halves_shard(x):
    last = lax.axis_size("shard") // 2
    bit = 1
    while bit < last:
        x = (x.astype(F32) + exchange(x, bit).astype(F32)).astype(x.dtype)
        bit *= 2
    return x, exchange(x, last)


def after(x, token):
    return lax.optimization_barrier((x, token))[0]


def body(
    block_in,
    attn_gain,
    q_weight,
    k_weight,
    v_weight,
    o_weight,
    moe_gain,
    router_weight,
    expert_gate,
    expert_up,
    expert_down,
    routes,
    out_grad,
):
    rows, width = block_in.shape
    n_ctx, n_sh = lax.axis_size("ctx"), lax.axis_size("shard")
    seq_len = rows * n_ctx
    n_exp = router_weight.shape[1]
    db = width // n_ctx
    qw, kw = q_weight.shape[1], k_weight.shape[1]
    q_planes = qw // LANES
    i, s = lax.axis_index("ctx"), lax.axis_index("shard")
    lane_at = (i * db) % LANES
    pos = jnp.concatenate([jnp.stack([i, s, (i * db) // LANES]).astype(jnp.int32), ctx_order(n_ctx)])
    cos, sin = rope_constants(seq_len)
    gain_one = attn_gain.reshape(1, width)
    gain_two = moe_gain.reshape(1, width)
    router_pad = jnp.pad(router_weight, ((0, 0), (0, LANES - n_exp)))

    piece = width // n_sh
    kv_send, aux_send = project(
        pos, n_ctx, block_in, gain_one, q_weight, k_weight, v_weight, cos, sin, out_grad, piece
    )
    kv_all = swap_ctx(kv_send)
    ow = gather_shard(o_weight)
    aux_all = swap_ctx(after(aux_send, kv_all))
    heads = attend(pos, aux_send, kv_all)
    resid_mid, x2, gates, x2_send = mid(
        pos, n_exp, gather_shard(heads), ow, block_in, gain_two, router_pad, routes
    )
    x2_all = gather_ctx(x2_send)
    moe_part, ex_part = experts_own(pos, x2, out_grad, gates, expert_gate, expert_up, expert_down)
    d_mid, back_send, dmid_send = back_mid(
        n_ctx, n_exp, *halves_shard(ex_part), resid_mid, gain_two, gates, router_pad, out_grad, o_weight
    )
    back_all = swap_ctx(after(back_send, aux_all))
    moe_near, moe_far = halves_shard(moe_part)
    block_out = resid_mid + moe_near.astype(F32) + moe_far.astype(F32)
    dn_part, qkv_grad, heads_all = attend_back(
        pos, aux_all, kv_all, back_all, cos, sin, q_weight, k_weight, v_weight
    )
    in_grad, gain_sum = finish(*halves_shard(dn_part), block_in, gain_one, d_mid)
    attn_gain_grad = gain_sum[:db, 0] / lax.dynamic_slice_in_dim(attn_gain, i * db, db, 0)
    q_grad, k_grad, v_grad = qkv_grad[:db, :qw], qkv_grad[:db, qw : qw + kw], qkv_grad[:db, qw + kw :]

    dmid_cols = swap_ctx(after(dmid_send, back_all))
    o_grad = tn(heads_all.reshape(seq_len, qw), dmid_cols.reshape(seq_len, db))

    gates_all = x2_all[:, piece // LANES * rows :].swapaxes(1, 2).reshape(seq_len, n_exp).astype(F32)
    gates_all = jnp.pad(gates_all, ((0, 0), (0, LANES - n_exp)))
    ogs = gather_shard(aux_all[:, qw // LANES : -1])
    xs = gather_shard(x2_all[:, : piece // LANES * rows])
    gate_grad, up_grad, down_grad, x_cols = experts_all(
        pos, xs, ogs, gates_all, expert_gate, expert_up, expert_down
    )
    small = back_all[:, q_planes * rows :]
    d_logits_all = small[:, :n_exp].swapaxes(1, 2).reshape(seq_len, n_exp)
    router_grad = tn(x_cols.reshape(seq_len, LANES), d_logits_all)
    if db < LANES:
        gate_grad = lax.dynamic_slice_in_dim(gate_grad, lane_at, db, 1)
        up_grad = lax.dynamic_slice_in_dim(up_grad, lane_at, db, 1)
        down_grad = lax.dynamic_slice_in_dim(down_grad, lane_at, db, 2)
        router_grad = lax.dynamic_slice_in_dim(router_grad, lane_at, db, 0)
    moe_gain_sum = jnp.sum(small[:, n_exp:].astype(F32), axis=0).reshape(width)
    moe_gain_grad = lax.dynamic_slice_in_dim(moe_gain_sum, i * db, db, 0)
    return (
        block_out,
        in_grad,
        attn_gain_grad,
        q_grad,
        k_grad,
        v_grad,
        o_grad,
        moe_gain_grad,
        router_grad,
        gate_grad,
        up_grad,
        down_grad,
    )


def solution(mesh):
    in_specs = (
        P("ctx", None),
        P(),
        P(None, "shard"),
        P(None, "shard"),
        P(None, "shard"),
        P("shard", None),
        P(),
        P(),
        P("shard", None, None),
        P("shard", None, None),
        P("shard", None, None),
        P("ctx", None),
        P("ctx", None),
    )
    out_specs = (
        P("ctx", None),
        P("ctx", None),
        P("ctx"),
        P("ctx", "shard"),
        P("ctx", "shard"),
        P("ctx", "shard"),
        P("shard", "ctx"),
        P("ctx"),
        P("ctx", None),
        P("shard", "ctx", None),
        P("shard", "ctx", None),
        P("shard", None, "ctx"),
    )
    return jax.shard_map(body, mesh=mesh, in_specs=in_specs, out_specs=out_specs, check_vma=False)
```

time: 1200 us -> 184 us (0.15)
  waiting for transfers between devices: 975 us -> 29 us
  Pallas kernels: 0 us -> 71.9 us
  blocking collectives: 86.6 us -> 21.9 us
  matrix products: 48.7 us -> 2.72 us
  starting transfers between devices: 0.58 us -> 30 us
  local copies, waits for them, and re-layouts: 44 us -> 16.4 us
  between operations: 15.5 us -> 0.9 us
  other arithmetic: 23.5 us -> 10.1 us
    reduce_scatter x10 -> x0, waiting for transfers between devices: 881 us -> none  [the longest x1 153 us: body(): lax.psum_scatter(down_part, 'ctx', scatter_dimension=2, tiled=True)]
    psum x4 -> x0, waiting for transfers between devices: 93.3 us -> none  [the longest x1 32.7 us: body(): d_normed_exp, d_gate = lax.psum((d_normed_part, d_gate_part), 'shard')]
    pallas_call x0 -> x8, Pallas kernels: none -> 71.9 us  [the longest x1 25.9 us: experts_all(): pl.pallas_call(functools.partial(experts_all_kernel, n_sh, rows), grid_sp...]
    all_gather x2 -> x0, blocking collectives: 59.1 us -> none  [the longest x1 30.8 us: body(): value_piece = lax.all_gather(value_proj, 'ctx', axis=0, tiled=True)]
    dot_general x31 -> x2, matrix products: 48.7 us -> 2.72 us  [tn(): lax.dot_general(a, b, (((0,), (0,)), ((), ())), preferred_element_type=F32)]
    gather x12 -> x0, local copies, waits for them, and re-layouts: 30 us -> none  [the longest x5 7.36 us: body(): gate = jax.nn.softmax(jnp.take_along_axis(logits, routes, axis=1), axis=-1)]
    ppermute x0 -> x21, waiting for transfers between devices: none -> 29 us  [the longest x18 19.1 us: exchange(): return lax.ppermute(x, 'shard', [(j, j ^ bit) for j in range(size)])]
    all_to_all x0 -> x1, blocking collectives: none -> 21.9 us  [swap_ctx(): return lax.all_to_all(x, 'ctx', 0, 0, tiled=True)]
  transfers between devices with their start and end apart: 14 -> 24, of which waited for: 14 -> 5; matrix products, arithmetic and copies ran while one was open for 4% -> 11% of each run, Pallas kernels for 0% -> 36%
where the time goes in v1:
time: 184 us; the launch traced here: 183 us
  Pallas kernels  71.9 us (39%)
  starting transfers between devices  30 us (16%)
  waiting for transfers between devices  29 us (16%)
  blocking collectives  21.9 us (12%)
  local copies, waits for them, and re-layouts  16.4 us (9%)
  other arithmetic  10.1 us (5%)
  matrix products  2.72 us (1%)
    pallas_call x1, Pallas kernels, experts_all(): pl.pallas_call(functools.partial(experts_all_kernel, n_sh, rows), grid_sp...  25.9 us
    all_to_all x1, blocking collectives, swap_ctx(): return lax.all_to_all(x, 'ctx', 0, 0, tiled=True)  21.9 us
    ppermute x18, waiting for transfers between devices, exchange(): return lax.ppermute(x, 'shard', [(j, j ^ bit) for j in range(size)])  19.1 us
    pallas_call x1, Pallas kernels, attend_back(): pl.pallas_call(attend_back_kernel, in_specs=[pl.BlockSpec(memory_space=pl...  18.2 us
    all_to_all x3, starting transfers between devices, swap_ctx(): return lax.all_to_all(x, 'ctx', 0, 0, tiled=True)  13.2 us
    ppermute x18, starting transfers between devices, exchange(): return lax.ppermute(x, 'shard', [(j, j ^ bit) for j in range(size)])  11.5 us
    pallas_call x1, Pallas kernels, experts_own(): pl.pallas_call(experts_own_kernel, grid_spec=pltpu.PrefetchScalarGridSpec...  11 us
    ppermute x3, waiting for transfers between devices, gather_ctx(): far = lax.ppermute(x, 'ctx', [(j, j ^ bit) for j in range(size)])  9.96 us
  transfers between devices with their start and end apart: 24, of which 5 were waited for; matrix products, arithmetic and copies ran while one was open for 11% of the time, Pallas kernels for 36%

profile of v1, /device:TPU:0, one launch (start us, length us, event | category | flops | bytes accessed | tf_op | source)
XLA Modules:
  0.0 183.1 jit_solution(1495683363637916063)
XLA Ops:
  0.7 0.7 broadcast_xor_fusion
  1.4 0.7 pad_add_fusion.pos_ref.refs_0_
  2.1 4.0 %project.1 = (bf16[8,2,128,128]{3,2,1,0:T(8,128)(2,1)}, bf16[8,5,128,128]{3,2,1,0:T(8,128)(2,1)}) custom-call(s32[11]{0:T(128)} %pad_add_fusion.pos_ref.refs_0_, bf16[128,1024]{1,0:T(8,128)(2,1)} %x_ref.3, f32[1,1024]{1,0:T(1,128)} %bitcast.20, bf16[1024,256]{1,0:T(8,128)(2,1)} %wq_ref.3, bf16[1024,128]{1,0:T(8,128)(2,1)} %wk_ref.3, ...), custom_call_target="tpu_custom_call" | custom-call | bytes 553500 | tf_op jit(solution)/shard_map/project/pallas_call | solution.py:105
  6.1 21.9 %all_to_all.20.kv_ref = bf16[8,2,128,128]{3,2,1,0:T(8,128)(2,1)} all-to-all(bf16[8,2,128,128]{3,2,1,0:T(8,128)(2,1)} %get-tuple-element.36), channel_id=1, replica_groups=mesh['ctx'=8,'shard'=4] {'ctx'}, dimensions={0} | all-to-all | bytes 1048576 | tf_op jit(solution)/shard_map/all_to_all | solution.py:616
  28.0 3.6 %all-to-all-start.1 = ((bf16[8,5,128,128]{3,2,1,0:T(8,128)(2,1)}), bf16[8,5,128,128]{3,2,1,0:T(8,128)(2,1)S(1)}, u32[]{:S(2)}, u32[]{:S(2)}) async-start(bf16[8,5,128,128]{3,2,1,0:T(8,128)(2,1)} %get-tuple-element.41.q_ref), calls=%async_computation.1 | async-start | bytes 2621440 | tf_op jit(solution)/shard_map/all_to_all | solution.py:616
  31.6 1.6 collective-permute-start.4
  33.1 11.5 %collective-permute-done.4.refs_7_ = bf16[256,1024]{1,0:T(8,128)(2,1)S(1)} collective-permute-done((bf16[256,1024]{1,0:T(8,128)(2,1)S(1)}, bf16[256,1024]{1,0:T(8,128)(2,1)S(1)}, u32[]{:S(2)}, u32[]{:S(2)}) %collective-permute-start.4) | collective-permute-done | bytes 524320 | tf_op jit(solution)/shard_map/ppermute | solution.py:593
  44.7 3.7 %attend.1.refs_1_ = bf16[128,256]{1,0:T(8,128)(2,1)} custom-call(s32[11]{0:T(128)} %pad_add_fusion.pos_ref.refs_0_, bf16[8,5,128,128]{3,2,1,0:T(8,128)(2,1)} %get-tuple-element.41.q_ref, bf16[8,2,128,128]{3,2,1,0:T(8,128)(2,1)} %all_to_all.20.kv_ref), custom_call_target="tpu_custom_call" | custom-call | bytes 553500 | tf_op jit(solution)/shard_map/attend/pallas_call | solution.py:160
  48.4 1.5 collective-permute-start.1
  49.9 0.2 collective-permute-start
  50.1 3.0 %collective-permute-done.1.refs_3_ = bf16[128,256]{1,0:T(8,128)(2,1)S(1)} collective-permute-done((bf16[128,256]{1,0:T(8,128)(2,1)}, bf16[128,256]{1,0:T(8,128)(2,1)S(1)}, u32[]{:S(2)}, u32[]{:S(2)}) %collective-permute-start.1) | collective-permute-done | bytes 65568 | tf_op jit(solution)/shard_map/ppermute | solution.py:593
  53.1 0.7 copy.33.refs_12_
  53.9 0.2 copy.32
  54.0 0.7 pad.10.refs_11_.router_ref
  54.9 0.7 copy-done.13
  55.6 3.4 %mid.1 = (f32[128,1024]{1,0:T(8,128)}, bf16[128,1024]{1,0:T(8,128)(2,1)}, f32[128,128]{1,0:T(8,128)}, bf16[1,272,128]{2,1,0:T(8,128)(2,1)}) custom-call(s32[11]{0:T(128)} %pad_add_fusion.pos_ref.refs_0_, bf16[128,256]{1,0:T(8,128)(2,1)} %attend.1.refs_1_, bf16[128,256]{1,0:T(8,128)(2,1)} %copy-done.19, bf16[128,256]{1,0:T(8,128)(2,1)} %copy-done.18, ...), custom_call_target="tpu_custom_call" | custom-call | bytes 738000 | tf_op jit(solution)/shard_map/mid/pallas_call | solution.py:220
  59.0 11.0 %experts_own.1 = (bf16[128,1024]{1,0:T(8,128)(2,1)}, bf16[128,1152]{1,0:T(8,128)(2,1)}) custom-call(s32[11]{0:T(128)} %pad_add_fusion.pos_ref.refs_0_, bf16[128,1024]{1,0:T(8,128)(2,1)} %get-tuple-element.38.x_ref, f32[128,1024]{1,0:T(8,128)} %og_ref.5, f32[128,128]{1,0:T(8,128)} %get-tuple-element.39.gates_ref, bf16[4,1024,512]{2,1,0:T(8,128)(2,1)} %refs_13_.1, ...), custom_call_target="tpu_custom_call" | custom-call | bytes 2029500 | tf_op jit(solution)/shard_map/experts_own/pallas_call | solution.py:279
  70.1 0.5 collective-permute-start.8
  70.6 2.6 %collective-permute-start.12 = (bf16[1,272,128]{2,1,0:T(8,128)(2,1)S(1)}, bf16[1,272,128]{2,1,0:T(8,128)(2,1)S(1)}, u32[]{:S(2)}, u32[]{:S(2)}) collective-permute-start(bf16[1,272,128]{2,1,0:T(8,128)(2,1)S(1)} %copy-done.8), channel_id=1, source_target_pairs={{0,16},{4,20},{8,24},{12,28},{16,0},{20,4},{24,8},{28,12},{1,17},{... | collective-permute-start | bytes 208904 | tf_op jit(solution)/shard_map/ppermute | solution.py:600
  73.1 1.1 add_convert_fusion.1.ex_ref
  74.2 1.6 collective-permute-start.9
  75.8 1.5 collective-permute-done.12
  77.3 0.6 collective-permute-start.13
  77.9 0.6 constant_dynamic-update-slice_fusion.3
  78.5 4.5 %collective-permute-done.9.far_ref = bf16[128,1152]{1,0:T(8,128)(2,1)S(1)} collective-permute-done((bf16[128,1152]{1,0:T(8,128)(2,1)S(1)}, bf16[128,1152]{1,0:T(8,128)(2,1)S(1)}, u32[]{:S(2)}, u32[]{:S(2)}) %collective-permute-start.9) | collective-permute-done | bytes 294944 | tf_op jit(solution)/shard_map/ppermute | solution.py:593
  83.0 0.7 copy-done.15
  83.7 3.2 %back_mid.1 = (f32[128,1024]{1,0:T(8,128)}, bf16[8,280,128]{2,1,0:T(8,128)(2,1)}, bf16[8,128,128]{2,1,0:T(8,128)(2,1)}) custom-call(bf16[128,1152]{1,0:T(8,128)(2,1)} %copy-done.6, bf16[128,1152]{1,0:T(8,128)(2,1)} %copy-done.15, f32[128,1024]{1,0:T(8,128)} %get-tuple-element.37.resid_ref, f32[1,1024]{1,0:T(1,128)} %bitcast.23, ...), custom_call_target="tpu_custom_call" | custom-call | bytes 553500 | tf_op jit(solution)/shard_map/back_mid/pallas_call | solution.py:343
  87.0 5.1 %all-to-all-start.2 = ((bf16[8,280,128]{2,1,0:T(8,128)(2,1)}), bf16[8,280,128]{2,1,0:T(8,128)(2,1)S(1)}, u32[]{:S(2)}, u32[]{:S(2)}) async-start(bf16[8,280,128]{2,1,0:T(8,128)(2,1)} %get-tuple-element.44), calls=%async_computation.2 | async-start | bytes 1146880 | tf_op jit(solution)/shard_map/all_to_all | solution.py:616
  92.0 0.6 constant_dynamic-update-slice_fusion.2
  92.7 2.1 %collective-permute-start.14 = (bf16[4,272,128]{2,1,0:T(8,128)(2,1)S(1)}, bf16[4,272,128]{2,1,0:T(8,128)(2,1)S(1)}, u32[]{:S(2)}, u32[]{:S(2)}) collective-permute-start(bf16[4,272,128]{2,1,0:T(8,128)(2,1)S(1)} %pad_maximum_fusion), channel_id=1, source_target_pairs={{0,4},{4,0},{8,12},{12,8},{16,20},{20,16},{24,28},{28,24},{1,5},{5... | collective-permute-start | bytes 835592 | tf_op jit(solution)/shard_map/ppermute | solution.py:600
  94.8 0.7 constant_dynamic-update-slice_fusion.1
  95.5 0.8 add_convert_fusion.2
  96.3 1.5 collective-permute-start.7
  97.8 8.5 %collective-permute-done.14 = bf16[4,272,128]{2,1,0:T(8,128)(2,1)S(1)} collective-permute-done((bf16[4,272,128]{2,1,0:T(8,128)(2,1)S(1)}, bf16[4,272,128]{2,1,0:T(8,128)(2,1)S(1)}, u32[]{:S(2)}, u32[]{:S(2)}) %collective-permute-start.14) | collective-permute-done | bytes 278560 | tf_op jit(solution)/shard_map/ppermute | solution.py:600
  106.2 0.7 constant_dynamic-update-slice_fusion
  106.9 1.1 slice.41.refs_1_
  108.0 1.6 collective-permute-start.16
  109.6 0.6 collective-permute-start.19
  110.3 0.8 slice_bitcast_fusion
  111.0 0.8 copy.35
  111.9 1.8 pad_convert_fusion.refs_9_
  113.7 0.8 copy-done.1
  114.5 18.2 %attend_back.1 = (bf16[128,1152]{1,0:T(8,128)(2,1)}, f32[128,512]{1,0:T(8,128)}, bf16[8,128,256]{2,1,0:T(8,128)(2,1)}) custom-call(s32[11]{0:T(128)} %pad_add_fusion.pos_ref.refs_0_, bf16[8,5,128,128]{3,2,1,0:T(8,128)(2,1)} %copy-done, bf16[8,2,128,128]{3,2,1,0:T(8,128)(2,1)} %all_to_all.20.kv_ref, bf16[8,280,128]{2,1,0:T(8,128)(2,1)} %copy-done.1, ...), custom_call_target="tpu_custom_call" | custom-call | bytes 3321000 | tf_op jit(solution)/shard_map/attend_back/pallas_call | solution.py:455
  132.7 0.2 collective-permute-start.10
  132.9 1.9 %convert_add_fusion = f32[128,1024]{1,0:T(8,128)} fusion(bf16[128,1024]{1,0:T(8,128)(2,1)} %collective-permute-done.7, f32[128,1024]{1,0:T(8,128)S(1)} %copy-done.5, bf16[128,1024]{1,0:T(8,128)(2,1)} %add_convert_fusion.2), kind=kLoop, calls=%fused_computation.4 | loop fusion | flops 524288 | bytes 1572864 | tf_op jit(solution)/shard_map/add | solution.py:690
  134.8 0.3 collective-permute-start.17
  135.1 0.2 collective-permute-start.18
  135.3 0.3 collective-permute-start.20
  135.6 4.5 %all-to-all-start.3 = ((bf16[8,128,128]{2,1,0:T(8,128)(2,1)}), bf16[8,128,128]{2,1,0:T(8,128)(2,1)S(1)}, u32[]{:S(2)}, u32[]{:S(2)}) async-start(bf16[8,128,128]{2,1,0:T(8,128)(2,1)} %get-tuple-element.52), calls=%async_computation.3 | async-start | bytes 524288 | tf_op jit(solution)/shard_map/all_to_all | solution.py:616
  140.2 1.5 fusion
  141.7 1.1 add_convert_fusion.dn_ref
  142.8 1.6 collective-permute-start.11
  144.4 0.7 convert_reduce_fusion
  145.1 1.6 slice.31
  146.7 0.6 dynamic_slice.7
  147.3 0.8 copy-done.9
  148.3 0.8 copy-done.11
  149.1 25.9 %experts_all.1 = (f32[4,128,512]{2,1,0:T(8,128)}, f32[4,128,512]{2,1,0:T(8,128)}, f32[4,512,128]{2,1,0:T(8,128)}, bf16[8,128,128]{2,1,0:T(8,128)(2,1)}) custom-call(s32[11]{0:T(128)} %pad_add_fusion.pos_ref.refs_0_, bf16[8,256,128]{2,1,0:T(8,128)(2,1)} %copy-done.2, bf16[8,256,128]{2,1,0:T(8,128)(2,1)} %collective-permute-done.15.refs_2_, ...), custom_call_target="tpu_custom_call" | custom-call | bytes 4612500 | tf_op jit(solution)/shard_map/experts_all/pallas_call | solution.py:547
  175.0 1.7 convolution_bitcast_fusion.1
  176.7 1.0 convolution_bitcast_fusion
  177.7 0.7 copy-done.16
  178.4 2.4 %finish.1 = (f32[128,1024]{1,0:T(8,128)}, f32[128,128]{1,0:T(8,128)}) custom-call(bf16[128,1152]{1,0:T(8,128)(2,1)} %copy-done.7, bf16[128,1152]{1,0:T(8,128)(2,1)} %copy-done.16, bf16[128,1024]{1,0:T(8,128)(2,1)} %x_ref.3, f32[1,1024]{1,0:T(1,128)} %bitcast.21, f32[128,1024]{1,0:T(8,128)} %get-tuple-element.46.dmid_ref), custom_call_target="tpu_custom_call" | custom-call | bytes 369000 | tf_op jit(solution)/shard_map/finish/pallas_call | solution.py:582
  180.8 0.9 slice_reduce_fusion
  181.8 1.3 dynamic-slice_divide_fusion
  (67 shorter events, 0.4 us)
Async XLA Ops:
  0.6 30.9 %copy-start.4 = (bf16[256,1024]{1,0:T(8,128)(2,1)S(1)}, bf16[256,1024]{1,0:T(8,128)(2,1)}, u32[]{:S(2)}) copy-start(bf16[256,1024]{1,0:T(8,128)(2,1)} %ow_ref.1) | copy-start | bytes 1572868
  2.1 51.1 %copy-start.22 = (s32[128,8]{0,1:T(8,128)S(1)}, s32[128,8]{0,1:T(8,128)}, u32[]{:S(2)}) copy-start(s32[128,8]{0,1:T(8,128)} %param.27) | copy-start | bytes 12292
  2.1 51.8 %copy-start.21 = (bf16[1024,16]{0,1:T(8,128)(2,1)S(1)}, bf16[1024,16]{0,1:T(8,128)(2,1)}, u32[]{:S(2)}) copy-start(bf16[1024,16]{0,1:T(8,128)(2,1)} %param.23) | copy-start | bytes 98308
  28.0 59.0 %all-to-all-start.1 = ((bf16[8,5,128,128]{3,2,1,0:T(8,128)(2,1)}), bf16[8,5,128,128]{3,2,1,0:T(8,128)(2,1)S(1)}, u32[]{:S(2)}, u32[]{:S(2)}) async-start(bf16[8,5,128,128]{3,2,1,0:T(8,128)(2,1)} %get-tuple-element.41.q_ref), calls=%async_computation.1 | async-start | bytes 2621440 | tf_op jit(solution)/shard_map/all_to_all | solution.py:616
  31.6 13.1 %collective-permute-start.4 = (bf16[256,1024]{1,0:T(8,128)(2,1)S(1)}, bf16[256,1024]{1,0:T(8,128)(2,1)S(1)}, u32[]{:S(2)}, u32[]{:S(2)}) collective-permute-start(bf16[256,1024]{1,0:T(8,128)(2,1)S(1)} %copy-done.4), channel_id=1, source_target_pairs={{0,2},{1,3},{2,0},{3,1},{4,6},{5,7},{6,4},{7,5},{8,10},{9,11},{10,... | collective-permute-start | bytes 1572872 | tf_op jit(solution)/shard_map/ppermute | solution.py:593
  33.1 21.7 %collective-permute-start.3 = (bf16[256,1024]{1,0:T(8,128)(2,1)S(1)}, bf16[256,1024]{1,0:T(8,128)(2,1)S(1)}, u32[]{:S(2)}, u32[]{:S(2)}) collective-permute-start(bf16[256,1024]{1,0:T(8,128)(2,1)S(1)} %copy-done.4), channel_id=1, source_target_pairs={{0,1},{1,0},{2,3},{3,2},{4,5},{5,4},{6,7},{7,6},{8,9},{9,8},{10,11... | collective-permute-start | bytes 1572872 | tf_op jit(solution)/shard_map/ppermute | solution.py:593
  44.7 10.2 %copy-start.12 = (bf16[256,1024]{1,0:T(8,128)(2,1)}, bf16[256,1024]{1,0:T(8,128)(2,1)S(1)}, u32[]{:S(2)}) copy-start(bf16[256,1024]{1,0:T(8,128)(2,1)S(1)} %collective-permute-done.4.refs_7_) | copy-start | bytes 1572868
  44.7 10.1 %collective-permute-start.5 = (bf16[256,1024]{1,0:T(8,128)(2,1)S(1)}, bf16[256,1024]{1,0:T(8,128)(2,1)}, u32[]{:S(2)}, u32[]{:S(2)}) collective-permute-start(bf16[256,1024]{1,0:T(8,128)(2,1)S(1)} %collective-permute-done.4.refs_7_), channel_id=1, source_target_pairs={{0,1},{1,0},{2,3},{3,2},{4,5},{5,4},{6,7},{7,6},{8,9},{9,8},{10,11... | collective-permute-start | bytes 1572872 | tf_op jit(solution)/shard_map/ppermute | solution.py:593
  48.4 4.7 %collective-permute-start.1 = (bf16[128,256]{1,0:T(8,128)(2,1)}, bf16[128,256]{1,0:T(8,128)(2,1)S(1)}, u32[]{:S(2)}, u32[]{:S(2)}) collective-permute-start(bf16[128,256]{1,0:T(8,128)(2,1)} %attend.1.refs_1_), channel_id=1, source_target_pairs={{0,2},{1,3},{2,0},{3,1},{4,6},{5,7},{6,4},{7,5},{8,10},{9,11},{10,... | collective-permute-start | bytes 196616 | tf_op jit(solution)/shard_map/ppermute | solution.py:593
  49.9 4.9 %collective-permute-start = (bf16[128,256]{1,0:T(8,128)(2,1)}, bf16[128,256]{1,0:T(8,128)(2,1)S(1)}, u32[]{:S(2)}, u32[]{:S(2)}) collective-permute-start(bf16[128,256]{1,0:T(8,128)(2,1)} %attend.1.refs_1_), channel_id=1, source_target_pairs={{0,1},{1,0},{2,3},{3,2},{4,5},{5,4},{6,7},{7,6},{8,9},{9,8},{10,11... | collective-permute-start | bytes 196616 | tf_op jit(solution)/shard_map/ppermute | solution.py:593
  53.1 1.7 copy-start.18
  53.1 1.7 collective-permute-start.2
  54.8 0.8 copy-start.13
  54.8 0.8 copy-start.19
  54.8 0.8 copy-start.20
  59.0 11.5 %copy-start.8 = (bf16[1,272,128]{2,1,0:T(8,128)(2,1)S(1)}, bf16[1,272,128]{2,1,0:T(8,128)(2,1)}, u32[]{:S(2)}) copy-start(bf16[1,272,128]{2,1,0:T(8,128)(2,1)} %get-tuple-element.53) | copy-start | bytes 208900
  70.1 25.4 %copy-start.17 = (bf16[128,1024]{1,0:T(8,128)(2,1)S(1)}, bf16[128,1024]{1,0:T(8,128)(2,1)}, u32[]{:S(2)}) copy-start(bf16[128,1024]{1,0:T(8,128)(2,1)} %get-tuple-element.40) | copy-start | bytes 786436
  70.1 3.1 %collective-permute-start.8 = (bf16[128,1152]{1,0:T(8,128)(2,1)}, bf16[128,1152]{1,0:T(8,128)(2,1)S(1)}, u32[]{:S(2)}, u32[]{:S(2)}) collective-permute-start(bf16[128,1152]{1,0:T(8,128)(2,1)} %get-tuple-element.42), channel_id=1, source_target_pairs={{0,1},{1,0},{2,3},{3,2},{4,5},{5,4},{6,7},{7,6},{8,9},{9,8},{10,11... | collective-permute-start | bytes 884744 | tf_op jit(solution)/shard_map/ppermute | solution.py:593
  70.6 6.7 %collective-permute-start.12 = (bf16[1,272,128]{2,1,0:T(8,128)(2,1)S(1)}, bf16[1,272,128]{2,1,0:T(8,128)(2,1)S(1)}, u32[]{:S(2)}, u32[]{:S(2)}) collective-permute-start(bf16[1,272,128]{2,1,0:T(8,128)(2,1)S(1)} %copy-done.8), channel_id=1, source_target_pairs={{0,16},{4,20},{8,24},{12,28},{16,0},{20,4},{24,8},{28,12},{1,17},{... | collective-permute-start | bytes 208904 | tf_op jit(solution)/shard_map/ppermute | solution.py:600
  74.2 8.8 %copy-start.6 = (bf16[128,1152]{1,0:T(8,128)(2,1)}, bf16[128,1152]{1,0:T(8,128)(2,1)S(1)}, u32[]{:S(2)}) copy-start(bf16[128,1152]{1,0:T(8,128)(2,1)S(1)} %add_convert_fusion.1.ex_ref) | copy-start | bytes 884740
  74.2 8.8 %collective-permute-start.9 = (bf16[128,1152]{1,0:T(8,128)(2,1)S(1)}, bf16[128,1152]{1,0:T(8,128)(2,1)S(1)}, u32[]{:S(2)}, u32[]{:S(2)}) collective-permute-start(bf16[128,1152]{1,0:T(8,128)(2,1)S(1)} %add_convert_fusion.1.ex_ref), channel_id=1, source_target_pairs={{0,2},{1,3},{2,0},{3,1},{4,6},{5,7},{6,4},{7,5},{8,10},{9,11},{10,... | collective-permute-start | bytes 884744 | tf_op jit(solution)/shard_map/ppermute | solution.py:593
  77.3 15.4 %collective-permute-start.13 = (bf16[2,272,128]{2,1,0:T(8,128)(2,1)S(1)}, bf16[2,272,128]{2,1,0:T(8,128)(2,1)S(1)}, u32[]{:S(2)}, u32[]{:S(2)}) collective-permute-start(bf16[2,272,128]{2,1,0:T(8,128)(2,1)S(1)} %pad_maximum_fusion.1), channel_id=1, source_target_pairs={{0,8},{4,12},{8,0},{12,4},{16,24},{20,28},{24,16},{28,20},{1,9},{5... | collective-permute-start | bytes 417800 | tf_op jit(solution)/shard_map/ppermute | solution.py:600
  78.5 17.0 %collective-permute-start.6 = (bf16[128,1024]{1,0:T(8,128)(2,1)}, bf16[128,1024]{1,0:T(8,128)(2,1)S(1)}, u32[]{:S(2)}, u32[]{:S(2)}) collective-permute-start(bf16[128,1024]{1,0:T(8,128)(2,1)} %get-tuple-element.40), channel_id=1, source_target_pairs={{0,1},{1,0},{2,3},{3,2},{4,5},{5,4},{6,7},{7,6},{8,9},{9,8},{10,11... | collective-permute-start | bytes 786440 | tf_op jit(solution)/shard_map/ppermute | solution.py:593
  83.0 0.7 copy-start.15
  86.9 26.7 %copy-start = (bf16[8,5,128,128]{3,2,1,0:T(8,128)(2,1)}, bf16[8,5,128,128]{3,2,1,0:T(8,128)(2,1)S(1)}, u32[]{:S(2)}) copy-start(bf16[8,5,128,128]{3,2,1,0:T(8,128)(2,1)S(1)} %all-to-all-done.1.q_ref) | copy-start | bytes 3932164
  87.0 26.7 %all-to-all-start.2 = ((bf16[8,280,128]{2,1,0:T(8,128)(2,1)}), bf16[8,280,128]{2,1,0:T(8,128)(2,1)S(1)}, u32[]{:S(2)}, u32[]{:S(2)}) async-start(bf16[8,280,128]{2,1,0:T(8,128)(2,1)} %get-tuple-element.44), calls=%async_computation.2 | async-start | bytes 1146880 | tf_op jit(solution)/shard_map/all_to_all | solution.py:616
  92.7 13.5 %collective-permute-start.14 = (bf16[4,272,128]{2,1,0:T(8,128)(2,1)S(1)}, bf16[4,272,128]{2,1,0:T(8,128)(2,1)S(1)}, u32[]{:S(2)}, u32[]{:S(2)}) collective-permute-start(bf16[4,272,128]{2,1,0:T(8,128)(2,1)S(1)} %pad_maximum_fusion), channel_id=1, source_target_pairs={{0,4},{4,0},{8,12},{12,8},{16,20},{20,16},{24,28},{28,24},{1,5},{5... | collective-permute-start | bytes 835592 | tf_op jit(solution)/shard_map/ppermute | solution.py:600
  96.3 36.6 %copy-start.5 = (f32[128,1024]{1,0:T(8,128)S(1)}, f32[128,1024]{1,0:T(8,128)}, u32[]{:S(2)}) copy-start(f32[128,1024]{1,0:T(8,128)} %get-tuple-element.37.resid_ref) | copy-start | bytes 1572868
  96.3 36.6 %collective-permute-start.7 = (bf16[128,1024]{1,0:T(8,128)(2,1)}, bf16[128,1024]{1,0:T(8,128)(2,1)}, u32[]{:S(2)}, u32[]{:S(2)}) collective-permute-start(bf16[128,1024]{1,0:T(8,128)(2,1)} %add_convert_fusion.2), channel_id=1, source_target_pairs={{0,2},{1,3},{2,0},{3,1},{4,6},{5,7},{6,4},{7,5},{8,10},{9,11},{10,... | collective-permute-start | bytes 786440 | tf_op jit(solution)/shard_map/ppermute | solution.py:593
  108.0 27.6 %copy-start.2 = (bf16[8,256,128]{2,1,0:T(8,128)(2,1)}, bf16[8,256,128]{2,1,0:T(8,128)(2,1)S(1)}, u32[]{:S(2)}) copy-start(bf16[8,256,128]{2,1,0:T(8,128)(2,1)S(1)} %slice.41.refs_1_) | copy-start | bytes 1572868
  108.0 26.8 %collective-permute-start.16 = (bf16[8,256,128]{2,1,0:T(8,128)(2,1)S(1)}, bf16[8,256,128]{2,1,0:T(8,128)(2,1)}, u32[]{:S(2)}, u32[]{:S(2)}) collective-permute-start(bf16[8,256,128]{2,1,0:T(8,128)(2,1)S(1)} %slice.41.refs_1_), channel_id=1, source_target_pairs={{0,2},{1,3},{2,0},{3,1},{4,6},{5,7},{6,4},{7,5},{8,10},{9,11},{10,... | collective-permute-start | bytes 1572872 | tf_op jit(solution)/shard_map/ppermute | solution.py:593
  109.6 37.7 %collective-permute-start.15 = (bf16[8,256,128]{2,1,0:T(8,128)(2,1)S(1)}, bf16[8,256,128]{2,1,0:T(8,128)(2,1)}, u32[]{:S(2)}, u32[]{:S(2)}) collective-permute-start(bf16[8,256,128]{2,1,0:T(8,128)(2,1)S(1)} %slice.41.refs_1_), channel_id=1, source_target_pairs={{0,1},{1,0},{2,3},{3,2},{4,5},{5,4},{6,7},{7,6},{8,9},{9,8},{10,11... | collective-permute-start | bytes 1572872 | tf_op jit(solution)/shard_map/ppermute | solution.py:593
  109.6 33.2 %copy-start.3 = (bf16[8,2,128,128]{3,2,1,0:T(8,128)(2,1)}, bf16[8,2,128,128]{3,2,1,0:T(8,128)(2,1)S(1)}, u32[]{:S(2)}) copy-start(bf16[8,2,128,128]{3,2,1,0:T(8,128)(2,1)S(1)} %slice.42.refs_5_) | copy-start | bytes 1572868
  109.6 25.7 %collective-permute-start.19 = (bf16[8,2,128,128]{3,2,1,0:T(8,128)(2,1)S(1)}, bf16[8,2,128,128]{3,2,1,0:T(8,128)(2,1)}, u32[]{:S(2)}, u32[]{:S(2)}) collective-permute-start(bf16[8,2,128,128]{3,2,1,0:T(8,128)(2,1)S(1)} %slice.42.refs_5_), channel_id=1, source_target_pairs={{0,2},{1,3},{2,0},{3,1},{4,6},{5,7},{6,4},{7,5},{8,10},{9,11},{10,... | collective-permute-start | bytes 1572872 | tf_op jit(solution)/shard_map/ppermute | solution.py:593
  113.7 0.8 copy-start.1
  132.7 9.0 %collective-permute-start.10 = (bf16[128,1152]{1,0:T(8,128)(2,1)}, bf16[128,1152]{1,0:T(8,128)(2,1)}, u32[]{:S(2)}, u32[]{:S(2)}) collective-permute-start(bf16[128,1152]{1,0:T(8,128)(2,1)} %get-tuple-element.45), channel_id=1, source_target_pairs={{0,1},{1,0},{2,3},{3,2},{4,5},{5,4},{6,7},{7,6},{8,9},{9,8},{10,11... | collective-permute-start | bytes 884744 | tf_op jit(solution)/shard_map/ppermute | solution.py:593
  134.8 12.5 %collective-permute-start.17 = (bf16[8,256,128]{2,1,0:T(8,128)(2,1)}, bf16[8,256,128]{2,1,0:T(8,128)(2,1)S(1)}, u32[]{:S(2)}, u32[]{:S(2)}) collective-permute-start(bf16[8,256,128]{2,1,0:T(8,128)(2,1)} %collective-permute-done.16.refs_3_), channel_id=1, source_target_pairs={{0,1},{1,0},{2,3},{3,2},{4,5},{5,4},{6,7},{7,6},{8,9},{9,8},{10,11... | collective-permute-start | bytes 1572872 | tf_op jit(solution)/shard_map/ppermute | solution.py:593
  135.1 12.2 %collective-permute-start.18 = (bf16[8,2,128,128]{3,2,1,0:T(8,128)(2,1)S(1)}, bf16[8,2,128,128]{3,2,1,0:T(8,128)(2,1)S(1)}, u32[]{:S(2)}, u32[]{:S(2)}) collective-permute-start(bf16[8,2,128,128]{3,2,1,0:T(8,128)(2,1)S(1)} %slice.42.refs_5_), channel_id=1, source_target_pairs={{0,1},{1,0},{2,3},{3,2},{4,5},{5,4},{6,7},{7,6},{8,9},{9,8},{10,11... | collective-permute-start | bytes 1572872 | tf_op jit(solution)/shard_map/ppermute | solution.py:593
  135.3 12.0 %collective-permute-start.20 = (bf16[8,2,128,128]{3,2,1,0:T(8,128)(2,1)}, bf16[8,2,128,128]{3,2,1,0:T(8,128)(2,1)S(1)}, u32[]{:S(2)}, u32[]{:S(2)}) collective-permute-start(bf16[8,2,128,128]{3,2,1,0:T(8,128)(2,1)} %collective-permute-done.19.refs_7_), channel_id=1, source_target_pairs={{0,1},{1,0},{2,3},{3,2},{4,5},{5,4},{6,7},{7,6},{8,9},{9,8},{10,11... | collective-permute-start | bytes 1572872 | tf_op jit(solution)/shard_map/ppermute | solution.py:593
  135.6 41.1 %all-to-all-start.3 = ((bf16[8,128,128]{2,1,0:T(8,128)(2,1)}), bf16[8,128,128]{2,1,0:T(8,128)(2,1)S(1)}, u32[]{:S(2)}, u32[]{:S(2)}) async-start(bf16[8,128,128]{2,1,0:T(8,128)(2,1)} %get-tuple-element.52), calls=%async_computation.3 | async-start | bytes 524288 | tf_op jit(solution)/shard_map/all_to_all | solution.py:616
  142.8 32.1 %copy-start.7 = (bf16[128,1152]{1,0:T(8,128)(2,1)}, bf16[128,1152]{1,0:T(8,128)(2,1)S(1)}, u32[]{:S(2)}) copy-start(bf16[128,1152]{1,0:T(8,128)(2,1)S(1)} %add_convert_fusion.dn_ref) | copy-start | bytes 884740
  142.8 34.9 %collective-permute-start.11 = (bf16[128,1152]{1,0:T(8,128)(2,1)S(1)}, bf16[128,1152]{1,0:T(8,128)(2,1)S(1)}, u32[]{:S(2)}, u32[]{:S(2)}) collective-permute-start(bf16[128,1152]{1,0:T(8,128)(2,1)S(1)} %add_convert_fusion.dn_ref), channel_id=1, source_target_pairs={{0,2},{1,3},{2,0},{3,1},{4,6},{5,7},{6,4},{7,5},{8,10},{9,11},{10,... | collective-permute-start | bytes 884744 | tf_op jit(solution)/shard_map/ppermute | solution.py:593
  147.3 29.4 %copy-start.14 = (bf16[8,128,256]{2,1,0:T(8,128)(2,1)S(1)}, bf16[8,128,256]{2,1,0:T(8,128)(2,1)}, u32[]{:S(2)}) copy-start(bf16[8,128,256]{2,1,0:T(8,128)(2,1)} %get-tuple-element.50) | copy-start | bytes 1572868
  147.3 0.8 copy-start.9
  147.3 1.0 copy-start.10
  148.3 0.8 copy-start.11
  177.7 0.7 copy-start.16

commit v2 on v1

--- a/solution.py
+++ b/solution.py
@@ -73,7 +73,7 @@
     return pl.CostEstimate(flops=0, transcendentals=0, bytes_accessed=int(micros * COST * 3.69e6))
 
 
-def project_kernel(pos_ref, x_ref, gain_ref, wq_ref, wk_ref, wv_ref, cos_ref, sin_ref, og_ref, kv_ref, aux_ref):
+def project_kernel(pos_ref, x_ref, gain_ref, wq_ref, wk_ref, wv_ref, cos_ref, sin_ref, kv_ref, aux_ref):
     x = x_ref[...].astype(F32)
     inv = lax.rsqrt(jnp.mean(x * x, axis=-1, keepdims=True) + NORM_EPS)
     x1 = (x * inv * gain_ref[...]).astype(BF)
@@ -83,8 +83,7 @@
     k = rope(nn(x1, wk_ref[...]), cos, sin).astype(BF)
     v = nn(x1, wv_ref[...]).astype(BF)
     peers, _, rows, _ = aux_ref.shape
-    og = og_ref[...].astype(BF)
-    aux = [t[:, m * LANES : (m + 1) * LANES] for t in (q, og) for m in range(t.shape[1] // LANES)]
+    aux = [q[:, m * LANES : (m + 1) * LANES] for m in range(q.shape[1] // LANES)]
     db = x.shape[1] // peers
     for p in range(peers):
         kv_ref[p, 0] = k
@@ -97,9 +96,9 @@
         aux_ref[p, len(aux)] = cols
 
 
-def project(pos, peers, block_in, gain, wq, wk, wv, cos, sin, out_grad, piece):
+def project(pos, peers, block_in, gain, wq, wk, wv, cos, sin):
     rows, width = block_in.shape
-    planes = (wq.shape[1] + piece) // LANES + 1
+    planes = wq.shape[1] // LANES + 1
     full = lambda shape: pl.BlockSpec(shape, lambda g, p: (0,) * len(shape))
     tab = pl.BlockSpec((rows, LANES), lambda g, p: (p[0], 0))
     return pl.pallas_call(
@@ -115,7 +114,6 @@
                 full(wv.shape),
                 tab,
                 tab,
-                pl.BlockSpec((rows, piece), lambda g, p: (0, p[1])),
             ],
             out_specs=[full((peers, 2, rows, LANES)), full((peers, planes, rows, LANES))],
         ),
@@ -126,7 +124,7 @@
         compiler_params=params(),
         cost_estimate=cost(3),
         name="project",
-    )(pos, block_in, gain, wq, wk, wv, cos, sin, out_grad)
+    )(pos, block_in, gain, wq, wk, wv, cos, sin)
 
 
 def attend_kernel(pos_ref, q_ref, kv_ref, out_ref):
@@ -233,7 +231,7 @@
 
 
 def expert_terms(pg, pu, g_out, gate):
-    sig = jax.nn.sigmoid(pg)
+    sig = 0.5 + 0.5 * jnp.tanh(0.5 * pg)
     silu = pg * sig
     hid = silu * pu
     dh = gate * g_out
@@ -307,7 +305,7 @@
 
 
 def back_mid_kernel(
-    n_exp, ex_ref, far_ref, resid_ref, gain_ref, gates_ref, router_ref, og_ref, ow_ref, dmid_ref, send_ref, cols_ref
+    n_exp, ex_ref, far_ref, resid_ref, gain_ref, gates_ref, router_ref, og_ref, ow_ref, dmid_ref, send_ref
 ):
     rows, width = resid_ref.shape
     ex = ex_ref[...].astype(F32) + far_ref[...].astype(F32)
@@ -333,19 +331,21 @@
     for p in range(peers):
         for m in range(planes):
             send_ref[p, m * rows : (m + 1) * rows] = d_heads[:, m * LANES : (m + 1) * LANES]
-        send_ref[p, planes * rows :] = small
-        cols_ref[p] = dmb[:, p * db : (p + 1) * db]
+        cols = dmb[:, p * db : (p + 1) * db]
+        if db < LANES:
+            cols = jnp.concatenate([cols, jnp.zeros((rows, LANES - db), BF)], axis=1)
+        send_ref[p, planes * rows : (planes + 1) * rows] = cols
+        send_ref[p, (planes + 1) * rows :] = small
 
 
 def back_mid(peers, n_exp, ex, far, resid, gain, gates, router_pad, og, ow):
     rows, width = resid.shape
-    total = ow.shape[0] // LANES * rows + n_exp + width // LANES
+    total = (ow.shape[0] // LANES + 1) * rows + n_exp + width // LANES
     return pl.pallas_call(
         functools.partial(back_mid_kernel, n_exp),
         out_shape=[
             jax.ShapeDtypeStruct((rows, width), F32),
             jax.ShapeDtypeStruct((peers, total, LANES), BF),
-            jax.ShapeDtypeStruct((peers, rows, width // peers), BF),
         ],
         compiler_params=params(),
         cost_estimate=cost(3),
@@ -353,64 +353,77 @@
     )(ex, far, resid, gain, gates, router_pad, og, ow)
 
 
-def attend_back_kernel(
-    pos_ref, q_ref, kv_ref, do_ref, cos_ref, sin_ref, wq_ref, wk_ref, wv_ref,
-    dn_ref, qkvg_ref, ho_ref, qs, ks, vs, dos, dqs, hos, dkt, dvt, dqkv,
-):
+def block_probs(q, k, start, first, bq):
+    s = nt(q, k)
+    edge = s[:, first:]
+    col = lax.broadcasted_iota(jnp.int32, edge.shape, 1) + first
+    row = lax.broadcasted_iota(jnp.int32, edge.shape, 0) % bq + start
+    edge = jnp.where(col <= row, edge, -1e30)
+    s = edge if first == 0 else jnp.concatenate([s[:, :first], edge], axis=1)
+    e = jnp.exp(s - jnp.max(s, axis=-1, keepdims=True))
+    return e, 1.0 / jnp.sum(e, axis=-1, keepdims=True)
+
+
+def load_heads(dst, block, j, h):
+    rows = block.shape[0]
+    for g in range(LANES // HD):
+        dst[h, g, j * rows : (j + 1) * rows] = block[:, g * HD : (g + 1) * HD]
+
+
+def load_keys(ks, vs, kv_ref):
+    blocks, _, rows, kw = kv_ref.shape
+    for j in range(blocks):
+        for h in range(kw // HD):
+            ks[h, j * rows : (j + 1) * rows] = kv_ref[j, 0, :, h * HD : (h + 1) * HD]
+            vs[h, j * rows : (j + 1) * rows] = kv_ref[j, 1, :, h * HD : (h + 1) * HD]
+
+
+def stacked(src, h, start, bq):
+    return jnp.concatenate([src[h, g, pl.ds(start, bq)] for g in range(LANES // HD)], axis=0)
+
+
+def attend_back_kernel(n_exp, *refs):
+    pos_ref, q_ref, kv_ref, do_ref, cos_ref, sin_ref, wq_ref, wk_ref, wv_ref, gcol_ref, moe_ref = refs[:11]
+    dn_ref, qkvg_ref, og_ref, mg_ref, qs, ks, vs, dos, dqs, dkt, dvt, dqkv, hos, hfull = refs[11:]
     i = pos_ref[0]
     blocks, _, rows, kw = kv_ref.shape
     heads = kw // HD
     group = LANES // HD
-    q_planes = heads
-    qw = q_planes * LANES
+    qw = heads * LANES
     n = blocks * rows
-    bq = 2 * rows if n <= 1024 else rows // 2
+    bq = 4 * rows if n <= 1024 else rows // 2
+    load_keys(ks, vs, kv_ref)
     for j in range(blocks):
-        at = slice(j * rows, (j + 1) * rows)
-        kb, vb = kv_ref[j, 0], kv_ref[j, 1]
         for h in range(heads):
-            ks[h, at] = kb[:, h * HD : (h + 1) * HD]
-            vs[h, at] = vb[:, h * HD : (h + 1) * HD]
-            for g in range(group):
-                qs[h, g, at] = q_ref[j, h, :, g * HD : (g + 1) * HD]
-                dos[h, g, at] = do_ref[j, h * rows : (h + 1) * rows, g * HD : (g + 1) * HD]
+            load_heads(qs, q_ref[j, h], j, h)
+            load_heads(dos, do_ref[j, h * rows : (h + 1) * rows], j, h)
     dkt[...] = jnp.zeros_like(dkt)
     dvt[...] = jnp.zeros_like(dvt)
 
-    def step(h, start, ext, full):
+    def step(h, start, ext, first):
         k, v = ks[h, :ext], vs[h, :ext]
-        q = jnp.concatenate([qs[h, g, pl.ds(start, bq)] for g in range(group)], axis=0)
-        do = jnp.concatenate([dos[h, g, pl.ds(start, bq)] for g in range(group)], axis=0)
-        s = nt(q, k)
-        edge = s if full else s[:, ext - bq :]
-        first = 0 if full else ext - bq
-        col = lax.broadcasted_iota(jnp.int32, edge.shape, 1) + first
-        row = lax.broadcasted_iota(jnp.int32, edge.shape, 0) % bq + start
-        edge = jnp.where(col <= row, edge, -1e30)
-        s = edge if first == 0 else jnp.concatenate([s[:, :first], edge], axis=1)
-        top = jnp.max(s, axis=-1, keepdims=True)
-        e = jnp.exp(s - top)
-        p = e * (1.0 / jnp.sum(e, axis=-1, keepdims=True))
-        dp = nt(do, v)
-        delta = jnp.sum(p * dp, axis=-1, keepdims=True)
-        ds = (p * (dp - delta)).astype(BF)
+        q, do = stacked(qs, h, start, bq), stacked(dos, h, start, bq)
+        e, inv = block_probs(q, k, start, first, bq)
+        p = e * inv
         pb = p.astype(BF)
-        o = nn(pb, v)
+        o = nn(pb, v).astype(BF)
+        delta = jnp.sum(do.astype(F32) * o.astype(F32), axis=-1, keepdims=True)
+        ds = (p * (nt(do, v) - delta)).astype(BF)
         dq = nn(ds, k) * (HD**-0.5)
         dkt[h, :, :ext] += tn(q, ds)
         dvt[h, :, :ext] += tn(do, pb)
         for g in range(group):
             dqs[h, g, pl.ds(start, bq)] = dq[g * bq : (g + 1) * bq]
-            hos[h, g, pl.ds(start, bq)] = o[g * bq : (g + 1) * bq].astype(BF)
+            hos[h, g, pl.ds(start, bq)] = o[g * bq : (g + 1) * bq]
 
     def per_head(h, carry):
         if n <= 1024:
             for r in range(n // bq):
-                step(h, r * bq, (r + 1) * bq, False)
+                step(h, r * bq, (r + 1) * bq, r * bq)
         else:
 
             def loop(r, c):
-                step(h, pl.multiple_of(r * bq, bq), n, True)
+                step(h, pl.multiple_of(r * bq, bq), n, 0)
                 return c
 
             lax.fori_loop(0, n // bq, loop, 0)
@@ -418,21 +431,23 @@
 
     lax.fori_loop(0, heads, per_head, 0)
     pieces = [(h, g) for h in range(heads) for g in range(group)]
-    qkvg_ref[...] = jnp.zeros_like(qkvg_ref)
+    small = (heads + 1) * rows
+    mg_ref[...] = jnp.sum(do_ref[:, small + n_exp :].astype(F32), axis=0)
 
     def per_block(j, carry):
         at = pl.ds(pl.multiple_of(j * rows, rows), rows)
         cos, sin = cos_ref[at], sin_ref[at]
-        ho_ref[j] = jnp.concatenate([hos[h, g, at] for h, g in pieces], axis=1)
+        hfull[at] = jnp.concatenate([hos[h, g, at] for h, g in pieces], axis=1)
         dq = jnp.concatenate([dqs[h, g, at] for h, g in pieces], axis=1)
         dk = jnp.transpose(jnp.concatenate([dkt[h, :, at] for h in range(heads)], axis=0))
         dv = jnp.transpose(jnp.concatenate([dvt[h, :, at] for h in range(heads)], axis=0))
         out = jnp.concatenate([unrope(dq, cos, sin), unrope(dk, cos, sin), dv], axis=1).astype(BF)
         dqkv[j] = out
-        qkvg_ref[...] += tn(q_ref[j, q_ref.shape[1] - 1], out)
         return carry
 
-    lax.fori_loop(0, blocks, per_block, 0)
+    lax.fori_loop(0, blocks, per_block, 0, unroll=2)
+    qkvg_ref[...] = tn(q_ref[:, q_ref.shape[1] - 1].reshape(n, LANES), dqkv[...].reshape(n, qw + 2 * kw))
+    og_ref[...] = tn(hfull[...], do_ref[:, heads * rows : (heads + 1) * rows].reshape(n, LANES))
     own = dqkv[i]
     width = wq_ref.shape[0]
     db = width // blocks
@@ -441,59 +456,65 @@
     ).astype(BF)
     mine = pl.ds(pl.multiple_of(i * db, db), db)
     w_rows = jnp.concatenate([wq_ref[mine], wk_ref[mine], wv_ref[mine]], axis=1).astype(F32)
-    gain = jnp.sum(qkvg_ref[:db] * w_rows, axis=1, keepdims=True)
+    gain = jnp.sum(qkvg_ref[:db] * w_rows, axis=1, keepdims=True) / gcol_ref[mine]
     if db < rows:
         gain = jnp.concatenate([gain, jnp.zeros((rows - db, 1), F32)], axis=0)
-    dn_ref[:, width:] = jnp.broadcast_to(gain, (rows, LANES)).astype(BF)
-
-
-def attend_back(pos, q_all, kv_all, do_all, cos, sin, wq, wk, wv):
+    dn_ref[:, width : width + LANES] = jnp.broadcast_to(gain, (rows, LANES)).astype(BF)
+    dn_ref[:, width + LANES :] = moe_ref[...]
+
+
+def attend_back(n_exp, pos, q_all, kv_all, do_all, cos, sin, wq, wk, wv, gain_col, moe):
     blocks, _, rows, kw = kv_all.shape
     width, qw = wq.shape
     heads, group = kw // HD, LANES // HD
     n = blocks * rows
+    per_head = pltpu.VMEM((heads, group, n, HD), BF)
     return pl.pallas_call(
-        attend_back_kernel,
-        in_specs=[pl.BlockSpec(memory_space=pltpu.SMEM)] + [pl.BlockSpec()] * 8,
+        functools.partial(attend_back_kernel, n_exp),
+        in_specs=[pl.BlockSpec(memory_space=pltpu.SMEM)] + [pl.BlockSpec()] * 10,
         out_shape=[
-            jax.ShapeDtypeStruct((rows, width + LANES), BF),
+            jax.ShapeDtypeStruct((rows, 2 * width + LANES), BF),
             jax.ShapeDtypeStruct((LANES, qw + 2 * kw), F32),
-            jax.ShapeDtypeStruct((blocks, rows, qw), BF),
+            jax.ShapeDtypeStruct((qw, LANES), F32),
+            jax.ShapeDtypeStruct((width // LANES, LANES), F32),
         ],
         scratch_shapes=[
-            pltpu.VMEM((heads, group, n, HD), BF),
+            per_head,
             pltpu.VMEM((heads, n, HD), BF),
             pltpu.VMEM((heads, n, HD), BF),
-            pltpu.VMEM((heads, group, n, HD), BF),
+            per_head,
             pltpu.VMEM((heads, group, n, HD), F32),
-            pltpu.VMEM((heads, group, n, HD), BF),
             pltpu.VMEM((heads, HD, n), F32),
             pltpu.VMEM((heads, HD, n), F32),
             pltpu.VMEM((blocks, rows, qw + 2 * kw), BF),
+            per_head,
+            pltpu.VMEM((n, qw), BF),
         ],
         compiler_params=params(),
         cost_estimate=cost(18),
         name="attend_back",
-    )(pos, q_all, kv_all, do_all, cos, sin, wq, wk, wv)
-
-
-def experts_all_kernel(n_sh, rows, *refs):
+    )(pos, q_all, kv_all, do_all, cos, sin, wq, wk, wv, gain_col, moe)
+
+
+def experts_all_kernel(n_sh, rows, n_exp, *refs):
     pos_ref, refs = refs[0], refs[1:]
     xs, ogs = refs[:n_sh], refs[n_sh : 2 * n_sh]
-    gates_ref = refs[2 * n_sh]
+    small_ref = refs[2 * n_sh]
     base = 2 * n_sh + 1
     wgs, wus, wds = (refs[base + k * n_sh : base + (k + 1) * n_sh] for k in range(3))
-    gg_ref, ug_ref, dg_ref, xc_ref, acc = refs[base + 3 * n_sh :]
+    gg_ref, ug_ref, dg_ref, rg_ref, acc = refs[base + 3 * n_sh :]
     e, c = pl.program_id(0), pl.program_id(1)
     nb = xs[0].shape[0]
     tb = nb * rows
     planes = wgs[0].shape[1] // LANES
     lane = lax.broadcasted_iota(jnp.int32, (tb, LANES), 1)
     mine = lane == pos_ref[1] * pl.num_programs(0) + e
-    gate = jnp.sum(jnp.where(mine, gates_ref[...], 0.0), axis=-1, keepdims=True)
+    pad = jnp.zeros((LANES - n_exp, rows), F32)
+    gates = [jnp.transpose(jnp.concatenate([xs[0][t, planes * rows :].astype(F32), pad], axis=0)) for t in range(nb)]
+    gate = jnp.sum(jnp.where(mine, jnp.concatenate(gates, axis=0), 0.0), axis=-1, keepdims=True)
     x_planes = [[x[:, m * rows : (m + 1) * rows].reshape(tb, LANES) for m in range(planes)] for x in xs]
     block = [pos_ref[3 + c * nb + t] for t in range(nb)]
-    o_planes = [[jnp.concatenate([o[j, m] for j in block], axis=0) for m in range(planes)] for o in ogs]
+    o_planes = [[o[:, m].reshape(tb, LANES) for m in range(planes)] for o in ogs]
     xv = [jnp.concatenate(p, axis=1) for p in x_planes]
     ov = [jnp.concatenate(p, axis=1) for p in o_planes]
     pg = sum(nn(x, w[0]) for x, w in zip(xv, wgs))
@@ -508,8 +529,21 @@
             hit = plane == (pos_ref[1] ^ b) * planes + m
             xc = jnp.where(hit, x_planes[b][m], xc)
             oc = jnp.where(hit, o_planes[b][m], oc)
-    for t, j in enumerate(block):
-        xc_ref[j] = xc[t * rows : (t + 1) * rows]
+
+    @pl.when(e == 0)
+    def _():
+        part = nn(jnp.concatenate([small_ref[j, :n_exp] for j in block], axis=1), xc)
+        part = jnp.concatenate([part, jnp.zeros((LANES - n_exp, LANES), F32)], axis=0)
+        part = jnp.transpose(part)[:, :n_exp]
+
+        @pl.when(c == 0)
+        def _():
+            rg_ref[...] = part
+
+        @pl.when(c > 0)
+        def _():
+            rg_ref[...] += part
+
     gg, ug, dg = tn(xc, dpg), tn(xc, dpu), tn(oc, hg)
 
     @pl.when(c == 0)
@@ -529,63 +563,68 @@
         dg_ref[0] = jnp.transpose(acc[...])
 
 
-def experts_all(pos, xs, ogs, gates, wg, wu, wd):
+def experts_all(n_exp, pos, xs, ogs, small, wg, wu, wd):
     n_sh = len(xs)
     blocks, total, _ = xs[0].shape
     _, planes, rows, _ = ogs[0].shape
     piece = planes * LANES
     n = blocks * rows
     n_e, width, ff = wg.shape
-    nb = math.gcd(blocks, 4)
+    nb = math.gcd(blocks, 8)
     x_tok = pl.BlockSpec((nb, total, LANES), lambda e, c, p: (c, 0, 0))
-    o_tok = pl.BlockSpec(ogs[0].shape, lambda e, c, p: (0, 0, 0, 0))
+    o_tok = pl.BlockSpec((nb, planes, rows, LANES), lambda e, c, p: (c, 0, 0, 0))
     row_w = lambda b: pl.BlockSpec((1, piece, ff), lambda e, c, p, b=b: (e, p[1] ^ b, 0))
     col_w = lambda b: pl.BlockSpec((1, ff, piece), lambda e, c, p, b=b: (e, 0, p[1] ^ b))
     out = pl.BlockSpec((1, LANES, ff), lambda e, c, p: (e, 0, 0))
     out_t = pl.BlockSpec((1, ff, LANES), lambda e, c, p: (e, 0, 0))
     sh = range(n_sh)
     return pl.pallas_call(
-        functools.partial(experts_all_kernel, n_sh, rows),
+        functools.partial(experts_all_kernel, n_sh, rows, n_exp),
         grid_spec=pltpu.PrefetchScalarGridSpec(
             num_scalar_prefetch=1,
             grid=(n_e, blocks // nb),
             in_specs=[x_tok for _ in sh]
             + [o_tok for _ in sh]
-            + [pl.BlockSpec((nb * rows, LANES), lambda e, c, p: (c, 0))]
+            + [pl.BlockSpec(small.shape, lambda e, c, p: (0, 0, 0))]
             + [row_w(b) for b in sh]
             + [row_w(b) for b in sh]
             + [col_w(b) for b in sh],
-            out_specs=[out, out, out_t, pl.BlockSpec((blocks, rows, LANES), lambda e, c, p: (0, 0, 0))],
+            out_specs=[out, out, out_t, pl.BlockSpec((LANES, n_exp), lambda e, c, p: (0, 0))],
             scratch_shapes=[pltpu.VMEM((LANES, ff), F32)],
         ),
         out_shape=[jax.ShapeDtypeStruct((n_e, LANES, ff), F32)] * 2
-        + [jax.ShapeDtypeStruct((n_e, ff, LANES), F32), jax.ShapeDtypeStruct((blocks, rows, LANES), BF)],
+        + [jax.ShapeDtypeStruct((n_e, ff, LANES), F32), jax.ShapeDtypeStruct((LANES, n_exp), F32)],
         compiler_params=params(("arbitrary", "arbitrary")),
         cost_estimate=cost(25),
         name="experts_all",
-    )(pos, *xs, *ogs, gates, *[wg] * n_sh, *[wu] * n_sh, *[wd] * n_sh)
-
-
-def finish_kernel(dn_ref, far_ref, x_ref, gain_ref, dmid_ref, out_ref, dgain_ref):
+    )(pos, *xs, *ogs, small, *[wg] * n_sh, *[wu] * n_sh, *[wd] * n_sh)
+
+
+def finish_kernel(near_ref, far_ref, x_ref, gain_ref, dmid_ref, resid_ref, out_ref, dgain_ref, block_ref):
     width = x_ref.shape[1]
-    dn = dn_ref[...].astype(F32) + far_ref[...].astype(F32)
-    dgain_ref[...] = dn[:, width:]
+    total = near_ref[...].astype(F32) + far_ref[...].astype(F32)
+    block_ref[...] = resid_ref[...] + total[:, width + LANES :]
+    dgain_ref[...] = jnp.transpose(total[:, width : width + LANES])[:8]
     x = x_ref[...].astype(F32)
     inv = lax.rsqrt(jnp.mean(x * x, axis=-1, keepdims=True) + NORM_EPS)
     hat = x * inv
-    u = gain_ref[...] * dn[:, :width]
+    u = gain_ref[...] * total[:, :width]
     out_ref[...] = dmid_ref[...] + inv * (u - hat * jnp.mean(u * hat, axis=-1, keepdims=True))
 
 
-def finish(dn, far, block_in, gain, d_mid):
+def finish(near, far, block_in, gain, d_mid, resid):
     rows, width = block_in.shape
     return pl.pallas_call(
         finish_kernel,
-        out_shape=[jax.ShapeDtypeStruct((rows, width), F32), jax.ShapeDtypeStruct((rows, LANES), F32)],
+        out_shape=[
+            jax.ShapeDtypeStruct((rows, width), F32),
+            jax.ShapeDtypeStruct((8, rows), F32),
+            jax.ShapeDtypeStruct((rows, width), F32),
+        ],
         compiler_params=params(),
         cost_estimate=cost(2),
         name="finish",
-    )(dn, far, block_in, gain, d_mid)
+    )(near, far, block_in, gain, d_mid, resid)
 
 
 def exchange(x, bit):
@@ -593,14 +632,15 @@
     return lax.ppermute(x, "shard", [(j, j ^ bit) for j in range(size)])
 
 
-def gather_ctx(x):
+def double_ctx(x, bit):
     size = lax.axis_size("ctx")
-    bit = size // 2
-    while bit:
-        far = lax.ppermute(x, "ctx", [(j, j ^ bit) for j in range(size)])
-        x = jnp.concatenate([x, far], axis=0)
-        bit //= 2
-    return x
+    far = lax.ppermute(x, "ctx", [(j, j ^ bit) for j in range(size)])
+    return jnp.concatenate([x, far], axis=0)
+
+
+def ctx_bits():
+    count = lax.axis_size("ctx").bit_length() - 1
+    return [1 << b for b in reversed(range(count))]
 
 
 def ctx_order(size):
@@ -670,51 +710,58 @@
     router_pad = jnp.pad(router_weight, ((0, 0), (0, LANES - n_exp)))
 
     piece = width // n_sh
+    bits = ctx_bits()
+    og_all = lax.dynamic_slice_in_dim(out_grad, s * piece, piece, 1).astype(BF)
+    og_all = og_all.reshape(1, rows, piece // LANES, LANES).swapaxes(1, 2)
+    og_all = double_ctx(og_all, bits[0])
     kv_send, aux_send = project(
-        pos, n_ctx, block_in, gain_one, q_weight, k_weight, v_weight, cos, sin, out_grad, piece
+        pos, n_ctx, block_in, gain_one, q_weight, k_weight, v_weight, cos, sin
     )
     kv_all = swap_ctx(kv_send)
     ow = gather_shard(o_weight)
+    kv_all = after(kv_all, (ow, og_all))
+    for bit in bits[1:-1]:
+        og_all = double_ctx(og_all, bit)
     aux_all = swap_ctx(after(aux_send, kv_all))
     heads = attend(pos, aux_send, kv_all)
     resid_mid, x2, gates, x2_send = mid(
         pos, n_exp, gather_shard(heads), ow, block_in, gain_two, router_pad, routes
     )
-    x2_all = gather_ctx(x2_send)
+    x2 = after(x2, og_all)
+    og_all = double_ctx(og_all, bits[-1])
+    x2_all = double_ctx(x2_send, bits[0])
     moe_part, ex_part = experts_own(pos, x2, out_grad, gates, expert_gate, expert_up, expert_down)
-    d_mid, back_send, dmid_send = back_mid(
-        n_ctx, n_exp, *halves_shard(ex_part), resid_mid, gain_two, gates, router_pad, out_grad, o_weight
+    near, far = halves_shard(ex_part)
+    x2_all = after(x2_all, near)
+    for bit in bits[1:-1]:
+        x2_all = double_ctx(x2_all, bit)
+    d_mid, back_send = back_mid(
+        n_ctx, n_exp, near, after(far, (x2_all, og_all)), resid_mid, gain_two, gates, router_pad, out_grad, o_weight
     )
+    x2_all = double_ctx(x2_all, bits[-1])
     back_all = swap_ctx(after(back_send, aux_all))
-    moe_near, moe_far = halves_shard(moe_part)
-    block_out = resid_mid + moe_near.astype(F32) + moe_far.astype(F32)
-    dn_part, qkv_grad, heads_all = attend_back(
-        pos, aux_all, kv_all, back_all, cos, sin, q_weight, k_weight, v_weight
+    ogs = gather_shard(og_all)
+    xs = gather_shard(x2_all)
+    back_all = after(back_all, (ogs[n_sh // 2], x2_all))
+    dn_part, qkv_grad, o_grad, moe_gain_sum = attend_back(
+        n_exp, pos, aux_all, kv_all, back_all, cos, sin, q_weight, k_weight, v_weight,
+        attn_gain.reshape(width, 1), moe_part
     )
-    in_grad, gain_sum = finish(*halves_shard(dn_part), block_in, gain_one, d_mid)
-    attn_gain_grad = gain_sum[:db, 0] / lax.dynamic_slice_in_dim(attn_gain, i * db, db, 0)
+    in_grad, gain_sum, block_out = finish(*halves_shard(dn_part), block_in, gain_one, d_mid, resid_mid)
+    attn_gain_grad = gain_sum[0, :db]
     q_grad, k_grad, v_grad = qkv_grad[:db, :qw], qkv_grad[:db, qw : qw + kw], qkv_grad[:db, qw + kw :]
-
-    dmid_cols = swap_ctx(after(dmid_send, back_all))
-    o_grad = tn(heads_all.reshape(seq_len, qw), dmid_cols.reshape(seq_len, db))
-
-    gates_all = x2_all[:, piece // LANES * rows :].swapaxes(1, 2).reshape(seq_len, n_exp).astype(F32)
-    gates_all = jnp.pad(gates_all, ((0, 0), (0, LANES - n_exp)))
-    ogs = gather_shard(aux_all[:, qw // LANES : -1])
-    xs = gather_shard(x2_all[:, : piece // LANES * rows])
-    gate_grad, up_grad, down_grad, x_cols = experts_all(
-        pos, xs, ogs, gates_all, expert_gate, expert_up, expert_down
+    o_grad = o_grad[:, :db]
+
+    small = back_all[:, (q_planes + 1) * rows :]
+    gate_grad, up_grad, down_grad, router_grad = experts_all(
+        n_exp, pos, xs, ogs, small, expert_gate, expert_up, expert_down
     )
-    small = back_all[:, q_planes * rows :]
-    d_logits_all = small[:, :n_exp].swapaxes(1, 2).reshape(seq_len, n_exp)
-    router_grad = tn(x_cols.reshape(seq_len, LANES), d_logits_all)
     if db < LANES:
         gate_grad = lax.dynamic_slice_in_dim(gate_grad, lane_at, db, 1)
         up_grad = lax.dynamic_slice_in_dim(up_grad, lane_at, db, 1)
         down_grad = lax.dynamic_slice_in_dim(down_grad, lane_at, db, 2)
         router_grad = lax.dynamic_slice_in_dim(router_grad, lane_at, db, 0)
-    moe_gain_sum = jnp.sum(small[:, n_exp:].astype(F32), axis=0).reshape(width)
-    moe_gain_grad = lax.dynamic_slice_in_dim(moe_gain_sum, i * db, db, 0)
+    moe_gain_grad = lax.dynamic_slice_in_dim(moe_gain_sum.reshape(width), i * db, db, 0)
     return (
         block_out,
         in_grad,

time: 184 us -> 167 us (0.908)
  blocking collectives: 21.9 us -> 0 us
  waiting for transfers between devices: 29 us -> 42.3 us
  other arithmetic: 10.1 us -> 3.61 us
  starting transfers between devices: 30 us -> 34.7 us
  matrix products: 2.72 us -> 0 us
  Pallas kernels: 71.9 us -> 70 us
    all_to_all x1 -> x0, blocking collectives: 21.9 us -> none  [swap_ctx(): return lax.all_to_all(x, 'ctx', 0, 0, tiled=True)]
    ppermute x3 -> x6, waiting for transfers between devices: 9.96 us -> 30.2 us  [double_ctx(): far = lax.ppermute(x, 'ctx', [(j, j ^ bit) for j in range(size)])]
    ppermute x18 -> x16, waiting for transfers between devices: 19.1 us -> 7.5 us  [exchange(): return lax.ppermute(x, 'shard', [(j, j ^ bit) for j in range(size)])]
    ppermute x3 -> x6, starting transfers between devices: 5.24 us -> 10.1 us  [double_ctx(): far = lax.ppermute(x, 'ctx', [(j, j ^ bit) for j in range(size)])]
    all_to_all x3, waiting for transfers between devices: 0.01 us -> 4.56 us  [swap_ctx(): return lax.all_to_all(x, 'ctx', 0, 0, tiled=True)]
    ppermute x18 -> x16, starting transfers between devices: 11.5 us -> 7.14 us  [exchange(): return lax.ppermute(x, 'shard', [(j, j ^ bit) for j in range(size)])]
    all_to_all x3, starting transfers between devices: 13.2 us -> 17.5 us  [swap_ctx(): return lax.all_to_all(x, 'ctx', 0, 0, tiled=True)]
    dot_general x2 -> x0, matrix products: 2.72 us -> none  [tn(): lax.dot_general(a, b, (((0,), (0,)), ((), ())), preferred_element_type=F32)]
  transfers between devices with their start and end apart: 24 -> 25, of which waited for: 5 -> 11; matrix products, arithmetic and copies ran while one was open for 11% -> 8% of each run, Pallas kernels for 36% -> 40%
where the time goes in v2:
time: 167 us; the launch traced here: 166 us
  Pallas kernels  70 us (42%)
  waiting for transfers between devices  42.3 us (25%)
  starting transfers between devices  34.7 us (21%)
  local copies, waits for them, and re-layouts  14.8 us (9%)
  other arithmetic  3.61 us (2%)
    ppermute x6, waiting for transfers between devices, double_ctx(): far = lax.ppermute(x, 'ctx', [(j, j ^ bit) for j in range(size)])  30.2 us
    pallas_call x1, Pallas kernels, experts_all(): pl.pallas_call(functools.partial(experts_all_kernel, n_sh, rows, n_exp),...  23.9 us
    pallas_call x1, Pallas kernels, attend_back(): pl.pallas_call(functools.partial(attend_back_kernel, n_exp), in_specs=[pl...  18.2 us
    all_to_all x3, starting transfers between devices, swap_ctx(): return lax.all_to_all(x, 'ctx', 0, 0, tiled=True)  17.5 us
    pallas_call x1, Pallas kernels, experts_own(): pl.pallas_call(experts_own_kernel, grid_spec=pltpu.PrefetchScalarGridSpec...  11.1 us
    ppermute x6, starting transfers between devices, double_ctx(): far = lax.ppermute(x, 'ctx', [(j, j ^ bit) for j in range(size)])  10.1 us
    ppermute x16, waiting for transfers between devices, exchange(): return lax.ppermute(x, 'shard', [(j, j ^ bit) for j in range(size)])  7.5 us
    ppermute x16, starting transfers between devices, exchange(): return lax.ppermute(x, 'shard', [(j, j ^ bit) for j in range(size)])  7.14 us
  transfers between devices with their start and end apart: 25, of which 11 were waited for; matrix products, arithmetic and copies ran while one was open for 8% of the time, Pallas kernels for 40%

profile of v2, /device:TPU:0, one launch (start us, length us, event | category | flops | bytes accessed | tf_op | source)
XLA Modules:
  0.0 166.4 jit_solution(2347075011095684346)
XLA Ops:
  0.7 3.0 %collective-permute-start.1 = (bf16[256,1024]{1,0:T(8,128)(2,1)}, bf16[256,1024]{1,0:T(8,128)(2,1)S(1)}, u32[]{:S(2)}, u32[]{:S(2)}) collective-permute-start(bf16[256,1024]{1,0:T(8,128)(2,1)} %ow_ref.1), channel_id=1, source_target_pairs={{0,2},{1,3},{2,0},{3,1},{4,6},{5,7},{6,4},{7,5},{8,10},{9,11},{10,... | collective-permute-start | bytes 1572872 | tf_op jit(solution)/shard_map/ppermute | solution.py:632
  3.7 0.7 broadcast_xor_fusion
  4.3 0.6 pad_add_fusion.pos_ref.refs_0_
  4.9 3.6 %project.1 = (bf16[8,2,128,128]{3,2,1,0:T(8,128)(2,1)}, bf16[8,3,128,128]{3,2,1,0:T(8,128)(2,1)}) custom-call(s32[11]{0:T(128)} %pad_add_fusion.pos_ref.refs_0_, bf16[128,1024]{1,0:T(8,128)(2,1)} %x_ref.3, f32[1,1024]{1,0:T(1,128)} %bitcast.16, bf16[1024,256]{1,0:T(8,128)(2,1)} %refs_6_.1, bf16[1024,128]{1,0:T(8,128)(2,1)} %refs_7_.1, ...), custom_call_target="tpu_custom_call" | custom-call | bytes 553500 | tf_op jit(solution)/shard_map/project/pallas_call | solution.py:104
  8.5 5.8 %all-to-all-start = ((bf16[8,2,128,128]{3,2,1,0:T(8,128)(2,1)}), bf16[8,2,128,128]{3,2,1,0:T(8,128)(2,1)S(1)}, u32[]{:S(2)}, u32[]{:S(2)}) async-start(bf16[8,2,128,128]{3,2,1,0:T(8,128)(2,1)} %get-tuple-element.41), calls=%async_computation | async-start | bytes 1048576 | tf_op jit(solution)/shard_map/all_to_all | solution.py:656
  14.4 1.4 collective-permute-done.1.refs_7_
  15.8 1.1 constant_dynamic-slice_fusion
  16.9 0.1 copy.37
  17.0 0.1 copy.32
  17.1 2.9 %collective-permute-start.3 = (bf16[1,2,128,128]{3,2,1,0:T(8,128)(2,1)S(1)}, bf16[1,2,128,128]{3,2,1,0:T(8,128)(2,1)S(1)}, u32[]{:S(2)}, u32[]{:S(2)}) collective-permute-start(bf16[1,2,128,128]{3,2,1,0:T(8,128)(2,1)S(1)} %bitcast.11), channel_id=1, source_target_pairs={{0,16},{4,20},{8,24},{12,28},{16,0},{20,4},{24,8},{28,12},{1,17},{... | collective-permute-start | bytes 196616 | tf_op jit(solution)/shard_map/ppermute | solution.py:637
  20.0 11.4 %collective-permute-done.3 = bf16[1,2,128,128]{3,2,1,0:T(8,128)(2,1)S(1)} collective-permute-done((bf16[1,2,128,128]{3,2,1,0:T(8,128)(2,1)S(1)}, bf16[1,2,128,128]{3,2,1,0:T(8,128)(2,1)S(1)}, u32[]{:S(2)}, u32[]{:S(2)}) %collective-permute-start.3) | collective-permute-done | bytes 65568 | tf_op jit(solution)/shard_map/ppermute | solution.py:637
  31.5 0.1 collective-permute-start.7
  31.5 0.0 copy-start.10
  31.6 0.0 copy-start.11
  31.6 4.2 %all-to-all-start.1 = ((bf16[8,3,128,128]{3,2,1,0:T(8,128)(2,1)}), bf16[8,3,128,128]{3,2,1,0:T(8,128)(2,1)S(1)}, u32[]{:S(2)}, u32[]{:S(2)}) async-start(bf16[8,3,128,128]{3,2,1,0:T(8,128)(2,1)} %get-tuple-element.43.q_ref), calls=%async_computation.1 | async-start | bytes 1572864 | tf_op jit(solution)/shard_map/all_to_all | solution.py:656
  35.8 3.7 %attend.1.refs_1_ = bf16[128,256]{1,0:T(8,128)(2,1)} custom-call(s32[11]{0:T(128)} %pad_add_fusion.pos_ref.refs_0_, bf16[8,3,128,128]{3,2,1,0:T(8,128)(2,1)} %get-tuple-element.43.q_ref, bf16[8,2,128,128]{3,2,1,0:T(8,128)(2,1)} %copy-done), custom_call_target="tpu_custom_call" | custom-call | bytes 553500 | tf_op jit(solution)/shard_map/attend/pallas_call | solution.py:158
  39.5 0.5 collective-permute-start.5
  40.1 0.7 copy.34.refs_12_
  40.8 0.2 copy.33
  41.0 0.8 pad.4.refs_11_.router_ref
  41.7 2.3 %collective-permute-done.5.refs_3_ = bf16[128,256]{1,0:T(8,128)(2,1)S(1)} collective-permute-done((bf16[128,256]{1,0:T(8,128)(2,1)}, bf16[128,256]{1,0:T(8,128)(2,1)S(1)}, u32[]{:S(2)}, u32[]{:S(2)}) %collective-permute-start.5) | collective-permute-done | bytes 65568 | tf_op jit(solution)/shard_map/ppermute | solution.py:632
  44.1 1.2 collective-permute-done.6.refs_4_
  45.3 0.6 copy-done.17
  45.9 3.4 %mid.1 = (f32[128,1024]{1,0:T(8,128)}, bf16[128,1024]{1,0:T(8,128)(2,1)}, f32[128,128]{1,0:T(8,128)}, bf16[1,272,128]{2,1,0:T(8,128)(2,1)}) custom-call(s32[11]{0:T(128)} %pad_add_fusion.pos_ref.refs_0_, bf16[128,256]{1,0:T(8,128)(2,1)} %attend.1.refs_1_, bf16[128,256]{1,0:T(8,128)(2,1)} %copy-done.16, bf16[128,256]{1,0:T(8,128)(2,1)} %copy-done.15, ...), custom_call_target="tpu_custom_call" | custom-call | bytes 738000 | tf_op jit(solution)/shard_map/mid/pallas_call | solution.py:218
  49.3 11.1 %experts_own.1 = (bf16[128,1024]{1,0:T(8,128)(2,1)}, bf16[128,1152]{1,0:T(8,128)(2,1)}) custom-call(s32[11]{0:T(128)} %pad_add_fusion.pos_ref.refs_0_, bf16[128,1024]{1,0:T(8,128)(2,1)} %get-tuple-element.45.x_ref, f32[128,1024]{1,0:T(8,128)} %og_ref.3, f32[128,128]{1,0:T(8,128)} %get-tuple-element.46.gates_ref, bf16[4,1024,512]{2,1,0:T(8,128)(2,1)} %refs_13_.1, ...), custom_call_target="tpu_custom_call" | custom-call | bytes 2029500 | tf_op jit(solution)/shard_map/experts_own/pallas_call | solution.py:277
  60.4 0.2 collective-permute-start.8
  60.6 2.9 %collective-permute-start.10 = (bf16[1,272,128]{2,1,0:T(8,128)(2,1)S(1)}, bf16[1,272,128]{2,1,0:T(8,128)(2,1)S(1)}, u32[]{:S(2)}, u32[]{:S(2)}) collective-permute-start(bf16[1,272,128]{2,1,0:T(8,128)(2,1)S(1)} %copy-done.14), channel_id=1, source_target_pairs={{0,16},{4,20},{8,24},{12,28},{16,0},{20,4},{24,8},{28,12},{1,17},{... | collective-permute-start | bytes 208904 | tf_op jit(solution)/shard_map/ppermute | solution.py:637
  63.5 1.5 collective-permute-start.12
  65.0 2.7 %collective-permute-done.10 = bf16[1,272,128]{2,1,0:T(8,128)(2,1)S(1)} collective-permute-done((bf16[1,272,128]{2,1,0:T(8,128)(2,1)S(1)}, bf16[1,272,128]{2,1,0:T(8,128)(2,1)S(1)}, u32[]{:S(2)}, u32[]{:S(2)}) %collective-permute-start.10) | collective-permute-done | bytes 69664 | tf_op jit(solution)/shard_map/ppermute | solution.py:637
  67.7 1.0 add_convert_fusion.1.ex_ref
  68.8 0.6 collective-permute-start.9
  69.4 0.7 collective-permute-start.11
  70.1 1.7 %collective-permute-done.12 = bf16[4,2,128,128]{3,2,1,0:T(8,128)(2,1)S(1)} collective-permute-done((bf16[4,2,128,128]{3,2,1,0:T(8,128)(2,1)S(1)}, bf16[4,2,128,128]{3,2,1,0:T(8,128)(2,1)S(1)}, u32[]{:S(2)}, u32[]{:S(2)}) %collective-permute-start.12) | collective-permute-done | bytes 262176 | tf_op jit(solution)/shard_map/ppermute | solution.py:637
  71.8 0.1 pad_maximum_fusion.refs_5_
  71.9 2.5 %collective-permute-done.11 = bf16[2,272,128]{2,1,0:T(8,128)(2,1)S(1)} collective-permute-done((bf16[2,272,128]{2,1,0:T(8,128)(2,1)S(1)}, bf16[2,272,128]{2,1,0:T(8,128)(2,1)S(1)}, u32[]{:S(2)}, u32[]{:S(2)}) %collective-permute-start.11) | collective-permute-done | bytes 139296 | tf_op jit(solution)/shard_map/ppermute | solution.py:637
  74.4 0.1 constant_dynamic-update-slice_fusion.3
  74.5 1.5 collective-permute-done.9.far_ref
  76.0 0.7 copy-done.12
  76.7 3.2 %back_mid.1 = (f32[128,1024]{1,0:T(8,128)}, bf16[8,408,128]{2,1,0:T(8,128)(2,1)}) custom-call(bf16[128,1152]{1,0:T(8,128)(2,1)} %copy-done.5, bf16[128,1152]{1,0:T(8,128)(2,1)} %copy-done.12, f32[128,1024]{1,0:T(8,128)} %get-tuple-element.51.resid_ref, f32[1,1024]{1,0:T(1,128)} %bitcast.20, f32[128,128]{1,0:T(8,128)} %get-tuple-element.46.gates_ref, ...), custom_call_target="tpu_custom_call" | custom-call | bytes 553500 | tf_op jit(solution)/shard_map/back_mid/pallas_call | solution.py:344
  80.0 7.5 %all-to-all-start.2 = ((bf16[8,408,128]{2,1,0:T(8,128)(2,1)}), bf16[8,408,128]{2,1,0:T(8,128)(2,1)S(1)}, u32[]{:S(2)}, u32[]{:S(2)}) async-start(bf16[8,408,128]{2,1,0:T(8,128)(2,1)} %get-tuple-element.53), calls=%async_computation.2 | async-start | bytes 1671168 | tf_op jit(solution)/shard_map/all_to_all | solution.py:656
  87.4 0.5 collective-permute-start.13
  88.0 2.0 %collective-permute-start.14 = (bf16[4,272,128]{2,1,0:T(8,128)(2,1)S(1)}, bf16[4,272,128]{2,1,0:T(8,128)(2,1)S(1)}, u32[]{:S(2)}, u32[]{:S(2)}) collective-permute-start(bf16[4,272,128]{2,1,0:T(8,128)(2,1)S(1)} %get-tuple-element.95), channel_id=1, source_target_pairs={{0,4},{4,0},{8,12},{12,8},{16,20},{20,16},{24,28},{28,24},{1,5},{5... | collective-permute-start | bytes 835592 | tf_op jit(solution)/shard_map/ppermute | solution.py:637
  90.0 1.0 copy.35.refs_9_
  91.0 11.9 %collective-permute-done.14 = bf16[4,272,128]{2,1,0:T(8,128)(2,1)S(1)} collective-permute-done((bf16[4,272,128]{2,1,0:T(8,128)(2,1)S(1)}, bf16[4,272,128]{2,1,0:T(8,128)(2,1)S(1)}, u32[]{:S(2)}, u32[]{:S(2)}) %collective-permute-start.14) | collective-permute-done | bytes 278560 | tf_op jit(solution)/shard_map/ppermute | solution.py:637
  103.0 0.6 collective-permute-start.18
  103.6 4.6 %all-to-all-done.2.refs_3_ = bf16[8,408,128]{2,1,0:T(8,128)(2,1)S(1)} async-done(((bf16[8,408,128]{2,1,0:T(8,128)(2,1)}), bf16[8,408,128]{2,1,0:T(8,128)(2,1)S(1)}, u32[]{:S(2)}, u32[]{:S(2)}) %all-to-all-start.2) | async-done | bytes 835616 | tf_op jit(solution)/shard_map/all_to_all | solution.py:656
  108.1 0.9 copy-done.1
  109.0 18.2 %attend_back.1 = (bf16[128,2176]{1,0:T(8,128)(2,1)}, f32[128,512]{1,0:T(8,128)}, f32[256,128]{1,0:T(8,128)}, f32[8,128]{1,0:T(8,128)}) custom-call(s32[11]{0:T(128)} %pad_add_fusion.pos_ref.refs_0_, bf16[8,3,128,128]{3,2,1,0:T(8,128)(2,1)} %copy-done.2, bf16[8,2,128,128]{3,2,1,0:T(8,128)(2,1)} %copy-done, bf16[8,408,128]{2,1,0:T(8,128)(2,1)} %copy-done.1, ...), custom_call_target="tpu_custom_call" | custom-call | bytes 3321000 | tf_op jit(solution)/shard_map/attend_back/pallas_call | solution.py:472
  127.2 0.5 collective-permute-start.20
  127.7 0.1 collective-permute-start.21
  127.8 0.4 collective-permute-start.17
  128.2 0.1 collective-permute-start.19
  128.3 1.1 collective-permute-done.15
  129.3 1.2 add_convert_fusion.near_ref
  130.5 0.6 collective-permute-start.16
  131.1 1.4 slice.19.refs_9_
  132.6 1.6 slice.16
  134.2 23.9 %experts_all.1 = (f32[4,128,512]{2,1,0:T(8,128)}, f32[4,128,512]{2,1,0:T(8,128)}, f32[4,512,128]{2,1,0:T(8,128)}, f32[128,16]{1,0:T(8,128)}) custom-call(s32[11]{0:T(128)} %pad_add_fusion.pos_ref.refs_0_, bf16[8,272,128]{2,1,0:T(8,128)(2,1)} %copy-done.6, bf16[8,272,128]{2,1,0:T(8,128)(2,1)} %collective-permute-done.17.refs_2_, ...), custom_call_target="tpu_custom_call" | custom-call | bytes 4612500 | tf_op jit(solution)/shard_map/experts_all/pallas_call | solution.py:581
  158.1 1.5 copy.36
  159.6 1.3 dynamic_slice.7
  160.8 0.7 fusion
  161.5 0.8 copy-done.7
  162.3 2.9 %finish.1 = (f32[128,1024]{1,0:T(8,128)}, f32[8,128]{1,0:T(8,128)}, f32[128,1024]{1,0:T(8,128)}) custom-call(bf16[128,2176]{1,0:T(8,128)(2,1)} %copy-done.3, bf16[128,2176]{1,0:T(8,128)(2,1)} %copy-done.7, bf16[128,1024]{1,0:T(8,128)(2,1)} %x_ref.3, f32[1,1024]{1,0:T(1,128)} %bitcast.17, f32[128,1024]{1,0:T(8,128)} %get-tuple-element.57.dmid_ref, ...), custom_call_target="tpu_custom_call" | custom-call | bytes 369000 | tf_op jit(solution)/shard_map/finish/pallas_call | solution.py:617
  165.2 1.2 slice_bitcast_fusion
  (60 shorter events, 0.3 us)
Async XLA Ops:
  0.6 39.4 %copy-start.20 = (s32[128,8]{0,1:T(8,128)S(1)}, s32[128,8]{0,1:T(8,128)}, u32[]{:S(2)}) copy-start(s32[128,8]{0,1:T(8,128)} %param.27) | copy-start | bytes 12292
  0.7 40.1 %copy-start.19 = (bf16[1024,16]{0,1:T(8,128)(2,1)S(1)}, bf16[1024,16]{0,1:T(8,128)(2,1)}, u32[]{:S(2)}) copy-start(bf16[1024,16]{0,1:T(8,128)(2,1)} %param.23) | copy-start | bytes 98308
  0.7 15.1 %collective-permute-start.1 = (bf16[256,1024]{1,0:T(8,128)(2,1)}, bf16[256,1024]{1,0:T(8,128)(2,1)S(1)}, u32[]{:S(2)}, u32[]{:S(2)}) collective-permute-start(bf16[256,1024]{1,0:T(8,128)(2,1)} %ow_ref.1), channel_id=1, source_target_pairs={{0,2},{1,3},{2,0},{3,1},{4,6},{5,7},{6,4},{7,5},{8,10},{9,11},{10,... | collective-permute-start | bytes 1572872 | tf_op jit(solution)/shard_map/ppermute | solution.py:632
  8.5 23.0 %all-to-all-start = ((bf16[8,2,128,128]{3,2,1,0:T(8,128)(2,1)}), bf16[8,2,128,128]{3,2,1,0:T(8,128)(2,1)S(1)}, u32[]{:S(2)}, u32[]{:S(2)}) async-start(bf16[8,2,128,128]{3,2,1,0:T(8,128)(2,1)} %get-tuple-element.41), calls=%async_computation | async-start | bytes 1048576 | tf_op jit(solution)/shard_map/all_to_all | solution.py:656
  14.4 17.2 %collective-permute-start = (bf16[256,1024]{1,0:T(8,128)(2,1)}, bf16[256,1024]{1,0:T(8,128)(2,1)S(1)}, u32[]{:S(2)}, u32[]{:S(2)}) collective-permute-start(bf16[256,1024]{1,0:T(8,128)(2,1)} %ow_ref.1), channel_id=1, source_target_pairs={{0,1},{1,0},{2,3},{3,2},{4,5},{5,4},{6,7},{7,6},{8,9},{9,8},{10,11... | collective-permute-start | bytes 1572872 | tf_op jit(solution)/shard_map/ppermute | solution.py:632
  15.8 29.4 %copy-start.9 = (bf16[256,1024]{1,0:T(8,128)(2,1)}, bf16[256,1024]{1,0:T(8,128)(2,1)S(1)}, u32[]{:S(2)}) copy-start(bf16[256,1024]{1,0:T(8,128)(2,1)S(1)} %collective-permute-done.1.refs_7_) | copy-start | bytes 1572868
  15.8 15.8 %collective-permute-start.2 = (bf16[256,1024]{1,0:T(8,128)(2,1)S(1)}, bf16[256,1024]{1,0:T(8,128)(2,1)S(1)}, u32[]{:S(2)}, u32[]{:S(2)}) collective-permute-start(bf16[256,1024]{1,0:T(8,128)(2,1)S(1)} %collective-permute-done.1.refs_7_), channel_id=1, source_target_pairs={{0,1},{1,0},{2,3},{3,2},{4,5},{5,4},{6,7},{7,6},{8,9},{9,8},{10,11... | collective-permute-start | bytes 1572872 | tf_op jit(solution)/shard_map/ppermute | solution.py:632
  17.1 14.3 %collective-permute-start.3 = (bf16[1,2,128,128]{3,2,1,0:T(8,128)(2,1)S(1)}, bf16[1,2,128,128]{3,2,1,0:T(8,128)(2,1)S(1)}, u32[]{:S(2)}, u32[]{:S(2)}) collective-permute-start(bf16[1,2,128,128]{3,2,1,0:T(8,128)(2,1)S(1)} %bitcast.11), channel_id=1, source_target_pairs={{0,16},{4,20},{8,24},{12,28},{16,0},{20,4},{24,8},{28,12},{1,17},{... | collective-permute-start | bytes 196616 | tf_op jit(solution)/shard_map/ppermute | solution.py:637
  31.5 12.5 %collective-permute-start.7 = (bf16[2,2,128,128]{3,2,1,0:T(8,128)(2,1)S(1)}, bf16[2,2,128,128]{3,2,1,0:T(8,128)(2,1)S(1)}, u32[]{:S(2)}, u32[]{:S(2)}) collective-permute-start(bf16[2,2,128,128]{3,2,1,0:T(8,128)(2,1)S(1)} %pad_maximum_fusion.3), channel_id=1, source_target_pairs={{0,8},{4,12},{8,0},{12,4},{16,24},{20,28},{24,16},{28,20},{1,9},{5... | collective-permute-start | bytes 393224 | tf_op jit(solution)/shard_map/ppermute | solution.py:637
  31.5 13.7 %copy-start.10 = (bf16[256,1024]{1,0:T(8,128)(2,1)}, bf16[256,1024]{1,0:T(8,128)(2,1)S(1)}, u32[]{:S(2)}) copy-start(bf16[256,1024]{1,0:T(8,128)(2,1)S(1)} %collective-permute-done.refs_6_) | copy-start | bytes 1572868
  31.6 4.2 %copy-start = (bf16[8,2,128,128]{3,2,1,0:T(8,128)(2,1)}, bf16[8,2,128,128]{3,2,1,0:T(8,128)(2,1)S(1)}, u32[]{:S(2)}) copy-start(bf16[8,2,128,128]{3,2,1,0:T(8,128)(2,1)S(1)} %all-to-all-done.kv_ref.refs_2_) | copy-start | bytes 1572868
  31.6 13.7 %copy-start.11 = (bf16[256,1024]{1,0:T(8,128)(2,1)}, bf16[256,1024]{1,0:T(8,128)(2,1)S(1)}, u32[]{:S(2)}) copy-start(bf16[256,1024]{1,0:T(8,128)(2,1)S(1)} %collective-permute-done.2.refs_8_) | copy-start | bytes 1572868
  31.6 48.4 %all-to-all-start.1 = ((bf16[8,3,128,128]{3,2,1,0:T(8,128)(2,1)}), bf16[8,3,128,128]{3,2,1,0:T(8,128)(2,1)S(1)}, u32[]{:S(2)}, u32[]{:S(2)}) async-start(bf16[8,3,128,128]{3,2,1,0:T(8,128)(2,1)} %get-tuple-element.43.q_ref), calls=%async_computation.1 | async-start | bytes 1572864 | tf_op jit(solution)/shard_map/all_to_all | solution.py:656
  39.5 4.5 %collective-permute-start.5 = (bf16[128,256]{1,0:T(8,128)(2,1)}, bf16[128,256]{1,0:T(8,128)(2,1)S(1)}, u32[]{:S(2)}, u32[]{:S(2)}) collective-permute-start(bf16[128,256]{1,0:T(8,128)(2,1)} %attend.1.refs_1_), channel_id=1, source_target_pairs={{0,2},{1,3},{2,0},{3,1},{4,6},{5,7},{6,4},{7,5},{8,10},{9,11},{10,... | collective-permute-start | bytes 196616 | tf_op jit(solution)/shard_map/ppermute | solution.py:632
  41.7 2.3 %collective-permute-start.4 = (bf16[128,256]{1,0:T(8,128)(2,1)}, bf16[128,256]{1,0:T(8,128)(2,1)S(1)}, u32[]{:S(2)}, u32[]{:S(2)}) collective-permute-start(bf16[128,256]{1,0:T(8,128)(2,1)} %attend.1.refs_1_), channel_id=1, source_target_pairs={{0,1},{1,0},{2,3},{3,2},{4,5},{5,4},{6,7},{7,6},{8,9},{9,8},{10,11... | collective-permute-start | bytes 196616 | tf_op jit(solution)/shard_map/ppermute | solution.py:632
  44.0 1.3 copy-start.15
  44.0 1.3 collective-permute-start.6
  44.0 1.2 copy-start.16
  45.2 0.6 copy-start.17
  49.3 11.3 %copy-start.14 = (bf16[1,272,128]{2,1,0:T(8,128)(2,1)S(1)}, bf16[1,272,128]{2,1,0:T(8,128)(2,1)}, u32[]{:S(2)}) copy-start(bf16[1,272,128]{2,1,0:T(8,128)(2,1)} %get-tuple-element.48) | copy-start | bytes 208900
  60.4 29.6 %copy-start.18 = (f32[1024]{0:T(1024)S(1)}, f32[1024]{0:T(1024)}, u32[]{:S(2)}) copy-start(f32[1024]{0:T(1024)} %param.17) | copy-start | bytes 12292
  60.4 7.3 %collective-permute-start.8 = (bf16[128,1152]{1,0:T(8,128)(2,1)}, bf16[128,1152]{1,0:T(8,128)(2,1)S(1)}, u32[]{:S(2)}, u32[]{:S(2)}) collective-permute-start(bf16[128,1152]{1,0:T(8,128)(2,1)} %get-tuple-element.47), channel_id=1, source_target_pairs={{0,1},{1,0},{2,3},{3,2},{4,5},{5,4},{6,7},{7,6},{8,9},{9,8},{10,11... | collective-permute-start | bytes 884744 | tf_op jit(solution)/shard_map/ppermute | solution.py:632
  60.6 7.1 %collective-permute-start.10 = (bf16[1,272,128]{2,1,0:T(8,128)(2,1)S(1)}, bf16[1,272,128]{2,1,0:T(8,128)(2,1)S(1)}, u32[]{:S(2)}, u32[]{:S(2)}) collective-permute-start(bf16[1,272,128]{2,1,0:T(8,128)(2,1)S(1)} %copy-done.14), channel_id=1, source_target_pairs={{0,16},{4,20},{8,24},{12,28},{16,0},{20,4},{24,8},{28,12},{1,17},{... | collective-permute-start | bytes 208904 | tf_op jit(solution)/shard_map/ppermute | solution.py:637
  63.5 8.3 %collective-permute-start.12 = (bf16[4,2,128,128]{3,2,1,0:T(8,128)(2,1)S(1)}, bf16[4,2,128,128]{3,2,1,0:T(8,128)(2,1)S(1)}, u32[]{:S(2)}, u32[]{:S(2)}) collective-permute-start(bf16[4,2,128,128]{3,2,1,0:T(8,128)(2,1)S(1)} %pad_maximum_fusion.1), channel_id=1, source_target_pairs={{0,4},{4,0},{8,12},{12,8},{16,20},{20,16},{24,28},{28,24},{1,5},{5... | collective-permute-start | bytes 786440 | tf_op jit(solution)/shard_map/ppermute | solution.py:637
  68.7 7.3 %copy-start.5 = (bf16[128,1152]{1,0:T(8,128)(2,1)}, bf16[128,1152]{1,0:T(8,128)(2,1)S(1)}, u32[]{:S(2)}) copy-start(bf16[128,1152]{1,0:T(8,128)(2,1)S(1)} %add_convert_fusion.1.ex_ref) | copy-start | bytes 884740
  68.8 7.3 %collective-permute-start.9 = (bf16[128,1152]{1,0:T(8,128)(2,1)S(1)}, bf16[128,1152]{1,0:T(8,128)(2,1)S(1)}, u32[]{:S(2)}, u32[]{:S(2)}) collective-permute-start(bf16[128,1152]{1,0:T(8,128)(2,1)S(1)} %add_convert_fusion.1.ex_ref), channel_id=1, source_target_pairs={{0,2},{1,3},{2,0},{3,1},{4,6},{5,7},{6,4},{7,5},{8,10},{9,11},{10,... | collective-permute-start | bytes 884744 | tf_op jit(solution)/shard_map/ppermute | solution.py:632
  69.4 5.1 %collective-permute-start.11 = (bf16[2,272,128]{2,1,0:T(8,128)(2,1)S(1)}, bf16[2,272,128]{2,1,0:T(8,128)(2,1)S(1)}, u32[]{:S(2)}, u32[]{:S(2)}) collective-permute-start(bf16[2,272,128]{2,1,0:T(8,128)(2,1)S(1)} %pad_maximum_fusion.2), channel_id=1, source_target_pairs={{0,8},{4,12},{8,0},{12,4},{16,24},{20,28},{24,16},{28,20},{1,9},{5... | collective-permute-start | bytes 417800 | tf_op jit(solution)/shard_map/ppermute | solution.py:637
  71.8 55.4 %copy-start.4 = (bf16[8,2,128,128]{3,2,1,0:T(8,128)(2,1)}, bf16[8,2,128,128]{3,2,1,0:T(8,128)(2,1)S(1)}, u32[]{:S(2)}) copy-start(bf16[8,2,128,128]{3,2,1,0:T(8,128)(2,1)S(1)} %pad_maximum_fusion.refs_5_) | copy-start | bytes 1572868
  76.0 0.7 copy-start.12
  80.0 28.2 %copy-start.2 = (bf16[8,3,128,128]{3,2,1,0:T(8,128)(2,1)}, bf16[8,3,128,128]{3,2,1,0:T(8,128)(2,1)S(1)}, u32[]{:S(2)}) copy-start(bf16[8,3,128,128]{3,2,1,0:T(8,128)(2,1)S(1)} %all-to-all-done.1.refs_1_) | copy-start | bytes 2359300
  80.0 28.1 %all-to-all-start.2 = ((bf16[8,408,128]{2,1,0:T(8,128)(2,1)}), bf16[8,408,128]{2,1,0:T(8,128)(2,1)S(1)}, u32[]{:S(2)}, u32[]{:S(2)}) async-start(bf16[8,408,128]{2,1,0:T(8,128)(2,1)} %get-tuple-element.53), calls=%async_computation.2 | async-start | bytes 1671168 | tf_op jit(solution)/shard_map/all_to_all | solution.py:656
  87.4 16.1 %collective-permute-start.13 = (bf16[8,2,128,128]{3,2,1,0:T(8,128)(2,1)S(1)}, bf16[8,2,128,128]{3,2,1,0:T(8,128)(2,1)}, u32[]{:S(2)}, u32[]{:S(2)}) collective-permute-start(bf16[8,2,128,128]{3,2,1,0:T(8,128)(2,1)S(1)} %pad_maximum_fusion.refs_5_), channel_id=1, source_target_pairs={{0,2},{1,3},{2,0},{3,1},{4,6},{5,7},{6,4},{7,5},{8,10},{9,11},{10,... | collective-permute-start | bytes 1572872 | tf_op jit(solution)/shard_map/ppermute | solution.py:632
  88.0 14.9 %collective-permute-start.14 = (bf16[4,272,128]{2,1,0:T(8,128)(2,1)S(1)}, bf16[4,272,128]{2,1,0:T(8,128)(2,1)S(1)}, u32[]{:S(2)}, u32[]{:S(2)}) collective-permute-start(bf16[4,272,128]{2,1,0:T(8,128)(2,1)S(1)} %get-tuple-element.95), channel_id=1, source_target_pairs={{0,4},{4,0},{8,12},{12,8},{16,20},{20,16},{24,28},{28,24},{1,5},{5... | collective-permute-start | bytes 835592 | tf_op jit(solution)/shard_map/ppermute | solution.py:637
  103.0 31.2 %copy-start.6 = (bf16[8,272,128]{2,1,0:T(8,128)(2,1)}, bf16[8,272,128]{2,1,0:T(8,128)(2,1)S(1)}, u32[]{:S(2)}) copy-start(bf16[8,272,128]{2,1,0:T(8,128)(2,1)S(1)} %constant_dynamic-update-slice_fusion.2.refs_1_) | copy-start | bytes 1671172
  103.0 25.2 %collective-permute-start.18 = (bf16[8,272,128]{2,1,0:T(8,128)(2,1)S(1)}, bf16[8,272,128]{2,1,0:T(8,128)(2,1)S(1)}, u32[]{:S(2)}, u32[]{:S(2)}) collective-permute-start(bf16[8,272,128]{2,1,0:T(8,128)(2,1)S(1)} %constant_dynamic-update-slice_fusion.2.refs_1_), channel_id=1, source_target_pairs={{0,2},{1,3},{2,0},{3,1},{4,6},{5,7},{6,4},{7,5},{8,10},{9,11},{10,... | collective-permute-start | bytes 1671176 | tf_op jit(solution)/shard_map/ppermute | solution.py:632
  108.1 0.9 copy-start.1
  127.2 2.2 %collective-permute-start.15 = (bf16[128,2176]{1,0:T(8,128)(2,1)}, bf16[128,2176]{1,0:T(8,128)(2,1)S(1)}, u32[]{:S(2)}, u32[]{:S(2)}) collective-permute-start(bf16[128,2176]{1,0:T(8,128)(2,1)} %get-tuple-element.56), channel_id=1, source_target_pairs={{0,1},{1,0},{2,3},{3,2},{4,5},{5,4},{6,7},{7,6},{8,9},{9,8},{10,11... | collective-permute-start | bytes 1671176 | tf_op jit(solution)/shard_map/ppermute | solution.py:632
  127.2 6.9 %collective-permute-start.20 = (bf16[8,2,128,128]{3,2,1,0:T(8,128)(2,1)S(1)}, bf16[8,2,128,128]{3,2,1,0:T(8,128)(2,1)}, u32[]{:S(2)}, u32[]{:S(2)}) collective-permute-start(bf16[8,2,128,128]{3,2,1,0:T(8,128)(2,1)S(1)} %pad_maximum_fusion.refs_5_), channel_id=1, source_target_pairs={{0,1},{1,0},{2,3},{3,2},{4,5},{5,4},{6,7},{7,6},{8,9},{9,8},{10,11... | collective-permute-start | bytes 1572872 | tf_op jit(solution)/shard_map/ppermute | solution.py:632
  127.7 6.5 %collective-permute-start.21 = (bf16[8,2,128,128]{3,2,1,0:T(8,128)(2,1)}, bf16[8,2,128,128]{3,2,1,0:T(8,128)(2,1)}, u32[]{:S(2)}, u32[]{:S(2)}) collective-permute-start(bf16[8,2,128,128]{3,2,1,0:T(8,128)(2,1)} %collective-permute-done.13.refs_7_), channel_id=1, source_target_pairs={{0,1},{1,0},{2,3},{3,2},{4,5},{5,4},{6,7},{7,6},{8,9},{9,8},{10,11... | collective-permute-start | bytes 1572872 | tf_op jit(solution)/shard_map/ppermute | solution.py:632
  127.8 6.4 %collective-permute-start.17 = (bf16[8,272,128]{2,1,0:T(8,128)(2,1)S(1)}, bf16[8,272,128]{2,1,0:T(8,128)(2,1)}, u32[]{:S(2)}, u32[]{:S(2)}) collective-permute-start(bf16[8,272,128]{2,1,0:T(8,128)(2,1)S(1)} %constant_dynamic-update-slice_fusion.2.refs_1_), channel_id=1, source_target_pairs={{0,1},{1,0},{2,3},{3,2},{4,5},{5,4},{6,7},{7,6},{8,9},{9,8},{10,11... | collective-permute-start | bytes 1671176 | tf_op jit(solution)/shard_map/ppermute | solution.py:632
  128.2 6.0 %copy-start.8 = (bf16[8,272,128]{2,1,0:T(8,128)(2,1)}, bf16[8,272,128]{2,1,0:T(8,128)(2,1)S(1)}, u32[]{:S(2)}) copy-start(bf16[8,272,128]{2,1,0:T(8,128)(2,1)S(1)} %collective-permute-done.18.refs_3_) | copy-start | bytes 1671172
  128.2 6.0 %collective-permute-start.19 = (bf16[8,272,128]{2,1,0:T(8,128)(2,1)S(1)}, bf16[8,272,128]{2,1,0:T(8,128)(2,1)}, u32[]{:S(2)}, u32[]{:S(2)}) collective-permute-start(bf16[8,272,128]{2,1,0:T(8,128)(2,1)S(1)} %collective-permute-done.18.refs_3_), channel_id=1, source_target_pairs={{0,1},{1,0},{2,3},{3,2},{4,5},{5,4},{6,7},{7,6},{8,9},{9,8},{10,11... | collective-permute-start | bytes 1671176 | tf_op jit(solution)/shard_map/ppermute | solution.py:632
  130.5 27.5 %copy-start.3 = (bf16[128,2176]{1,0:T(8,128)(2,1)}, bf16[128,2176]{1,0:T(8,128)(2,1)S(1)}, u32[]{:S(2)}) copy-start(bf16[128,2176]{1,0:T(8,128)(2,1)S(1)} %add_convert_fusion.near_ref) | copy-start | bytes 1671172
  130.5 31.0 %collective-permute-start.16 = (bf16[128,2176]{1,0:T(8,128)(2,1)S(1)}, bf16[128,2176]{1,0:T(8,128)(2,1)S(1)}, u32[]{:S(2)}, u32[]{:S(2)}) collective-permute-start(bf16[128,2176]{1,0:T(8,128)(2,1)S(1)} %add_convert_fusion.near_ref), channel_id=1, source_target_pairs={{0,2},{1,3},{2,0},{3,1},{4,6},{5,7},{6,4},{7,5},{8,10},{9,11},{10,... | collective-permute-start | bytes 1671176 | tf_op jit(solution)/shard_map/ppermute | solution.py:632
  134.1 26.7 %copy-start.13 = (f32[128,512]{1,0:T(8,128)S(1)}, f32[128,512]{1,0:T(8,128)}, u32[]{:S(2)}) copy-start(f32[128,512]{1,0:T(8,128)} %get-tuple-element.61) | copy-start | bytes 786436
  161.5 0.8 copy-start.7

commit v3 on v2

--- a/solution.py
+++ b/solution.py
@@ -384,7 +384,7 @@
 
 def attend_back_kernel(n_exp, *refs):
     pos_ref, q_ref, kv_ref, do_ref, cos_ref, sin_ref, wq_ref, wk_ref, wv_ref, gcol_ref, moe_ref = refs[:11]
-    dn_ref, qkvg_ref, og_ref, mg_ref, qs, ks, vs, dos, dqs, dkt, dvt, dqkv, hos, hfull = refs[11:]
+    dn_ref, qg_ref, kg_ref, vg_ref, og_ref, mg_ref, qs, ks, vs, dos, dqs, dkt, dvt, dqkv, hos, hfull = refs[11:]
     i = pos_ref[0]
     blocks, _, rows, kw = kv_ref.shape
     heads = kw // HD
@@ -432,7 +432,9 @@
     lax.fori_loop(0, heads, per_head, 0)
     pieces = [(h, g) for h in range(heads) for g in range(group)]
     small = (heads + 1) * rows
-    mg_ref[...] = jnp.sum(do_ref[:, small + n_exp :].astype(F32), axis=0)
+    gain_rows = jnp.sum(do_ref[:, small + n_exp :].astype(F32), axis=0)
+    mine = lax.broadcasted_iota(jnp.int32, gain_rows.shape, 0) == pos_ref[2]
+    mg_ref[...] = jnp.sum(jnp.where(mine, gain_rows, 0.0), axis=0, keepdims=True)
 
     def per_block(j, carry):
         at = pl.ds(pl.multiple_of(j * rows, rows), rows)
@@ -446,7 +448,10 @@
         return carry
 
     lax.fori_loop(0, blocks, per_block, 0, unroll=2)
-    qkvg_ref[...] = tn(q_ref[:, q_ref.shape[1] - 1].reshape(n, LANES), dqkv[...].reshape(n, qw + 2 * kw))
+    qkvg = tn(q_ref[:, q_ref.shape[1] - 1].reshape(n, LANES), dqkv[...].reshape(n, qw + 2 * kw))
+    qg_ref[...] = qkvg[:, :qw]
+    kg_ref[...] = qkvg[:, qw : qw + kw]
+    vg_ref[...] = qkvg[:, qw + kw :]
     og_ref[...] = tn(hfull[...], do_ref[:, heads * rows : (heads + 1) * rows].reshape(n, LANES))
     own = dqkv[i]
     width = wq_ref.shape[0]
@@ -456,7 +461,7 @@
     ).astype(BF)
     mine = pl.ds(pl.multiple_of(i * db, db), db)
     w_rows = jnp.concatenate([wq_ref[mine], wk_ref[mine], wv_ref[mine]], axis=1).astype(F32)
-    gain = jnp.sum(qkvg_ref[:db] * w_rows, axis=1, keepdims=True) / gcol_ref[mine]
+    gain = jnp.sum(qkvg[:db] * w_rows, axis=1, keepdims=True) / gcol_ref[mine]
     if db < rows:
         gain = jnp.concatenate([gain, jnp.zeros((rows - db, 1), F32)], axis=0)
     dn_ref[:, width : width + LANES] = jnp.broadcast_to(gain, (rows, LANES)).astype(BF)
@@ -474,9 +479,11 @@
         in_specs=[pl.BlockSpec(memory_space=pltpu.SMEM)] + [pl.BlockSpec()] * 10,
         out_shape=[
             jax.ShapeDtypeStruct((rows, 2 * width + LANES), BF),
-            jax.ShapeDtypeStruct((LANES, qw + 2 * kw), F32),
+            jax.ShapeDtypeStruct((LANES, qw), F32),
+            jax.ShapeDtypeStruct((LANES, kw), F32),
+            jax.ShapeDtypeStruct((LANES, kw), F32),
             jax.ShapeDtypeStruct((qw, LANES), F32),
-            jax.ShapeDtypeStruct((width // LANES, LANES), F32),
+            jax.ShapeDtypeStruct((1, LANES), F32),
         ],
         scratch_shapes=[
             per_head,
@@ -533,8 +540,6 @@
     @pl.when(e == 0)
     def _():
         part = nn(jnp.concatenate([small_ref[j, :n_exp] for j in block], axis=1), xc)
-        part = jnp.concatenate([part, jnp.zeros((LANES - n_exp, LANES), F32)], axis=0)
-        part = jnp.transpose(part)[:, :n_exp]
 
         @pl.when(c == 0)
         def _():
@@ -571,6 +576,7 @@
     n = blocks * rows
     n_e, width, ff = wg.shape
     nb = math.gcd(blocks, 8)
+    tail = small.shape[1] % rows
     x_tok = pl.BlockSpec((nb, total, LANES), lambda e, c, p: (c, 0, 0))
     o_tok = pl.BlockSpec((nb, planes, rows, LANES), lambda e, c, p: (c, 0, 0, 0))
     row_w = lambda b: pl.BlockSpec((1, piece, ff), lambda e, c, p, b=b: (e, p[1] ^ b, 0))
@@ -585,15 +591,15 @@
             grid=(n_e, blocks // nb),
             in_specs=[x_tok for _ in sh]
             + [o_tok for _ in sh]
-            + [pl.BlockSpec(small.shape, lambda e, c, p: (0, 0, 0))]
+            + [pl.BlockSpec((blocks, tail, LANES), lambda e, c, p: (0, small.shape[1] // tail - 1, 0))]
             + [row_w(b) for b in sh]
             + [row_w(b) for b in sh]
             + [col_w(b) for b in sh],
-            out_specs=[out, out, out_t, pl.BlockSpec((LANES, n_exp), lambda e, c, p: (0, 0))],
+            out_specs=[out, out, out_t, pl.BlockSpec((n_exp, LANES), lambda e, c, p: (0, 0))],
             scratch_shapes=[pltpu.VMEM((LANES, ff), F32)],
         ),
         out_shape=[jax.ShapeDtypeStruct((n_e, LANES, ff), F32)] * 2
-        + [jax.ShapeDtypeStruct((n_e, ff, LANES), F32), jax.ShapeDtypeStruct((LANES, n_exp), F32)],
+        + [jax.ShapeDtypeStruct((n_e, ff, LANES), F32), jax.ShapeDtypeStruct((n_exp, LANES), F32)],
         compiler_params=params(("arbitrary", "arbitrary")),
         cost_estimate=cost(25),
         name="experts_all",
@@ -604,7 +610,7 @@
     width = x_ref.shape[1]
     total = near_ref[...].astype(F32) + far_ref[...].astype(F32)
     block_ref[...] = resid_ref[...] + total[:, width + LANES :]
-    dgain_ref[...] = jnp.transpose(total[:, width : width + LANES])[:8]
+    dgain_ref[...] = jnp.transpose(total[:, width : width + LANES])[:1]
     x = x_ref[...].astype(F32)
     inv = lax.rsqrt(jnp.mean(x * x, axis=-1, keepdims=True) + NORM_EPS)
     hat = x * inv
@@ -618,7 +624,7 @@
         finish_kernel,
         out_shape=[
             jax.ShapeDtypeStruct((rows, width), F32),
-            jax.ShapeDtypeStruct((8, rows), F32),
+            jax.ShapeDtypeStruct((1, rows), F32),
             jax.ShapeDtypeStruct((rows, width), F32),
         ],
         compiler_params=params(),
@@ -743,25 +749,27 @@
     ogs = gather_shard(og_all)
     xs = gather_shard(x2_all)
     back_all = after(back_all, (ogs[n_sh // 2], x2_all))
-    dn_part, qkv_grad, o_grad, moe_gain_sum = attend_back(
+    dn_part, q_grad, k_grad, v_grad, o_grad, moe_gain_sum = attend_back(
         n_exp, pos, aux_all, kv_all, back_all, cos, sin, q_weight, k_weight, v_weight,
         attn_gain.reshape(width, 1), moe_part
     )
     in_grad, gain_sum, block_out = finish(*halves_shard(dn_part), block_in, gain_one, d_mid, resid_mid)
-    attn_gain_grad = gain_sum[0, :db]
-    q_grad, k_grad, v_grad = qkv_grad[:db, :qw], qkv_grad[:db, qw : qw + kw], qkv_grad[:db, qw + kw :]
+    attn_gain_grad = gain_sum.reshape(rows)[:db]
+    q_grad, k_grad, v_grad = q_grad[:db], k_grad[:db], v_grad[:db]
     o_grad = o_grad[:, :db]
 
-    small = back_all[:, (q_planes + 1) * rows :]
-    gate_grad, up_grad, down_grad, router_grad = experts_all(
-        n_exp, pos, xs, ogs, small, expert_gate, expert_up, expert_down
+    gate_grad, up_grad, down_grad, router_t = experts_all(
+        n_exp, pos, xs, ogs, back_all, expert_gate, expert_up, expert_down
     )
     if db < LANES:
         gate_grad = lax.dynamic_slice_in_dim(gate_grad, lane_at, db, 1)
         up_grad = lax.dynamic_slice_in_dim(up_grad, lane_at, db, 1)
         down_grad = lax.dynamic_slice_in_dim(down_grad, lane_at, db, 2)
-        router_grad = lax.dynamic_slice_in_dim(router_grad, lane_at, db, 0)
-    moe_gain_grad = lax.dynamic_slice_in_dim(moe_gain_sum.reshape(width), i * db, db, 0)
+        router_t = lax.dynamic_slice_in_dim(router_t, lane_at, db, 1)
+    router_grad = router_t.T
+    moe_gain_grad = moe_gain_sum.reshape(LANES)
+    if db < LANES:
+        moe_gain_grad = lax.dynamic_slice_in_dim(moe_gain_grad, lane_at, db, 0)
     return (
         block_out,
         in_grad,

time: 167 us -> 164 us (0.982)
  local copies, waits for them, and re-layouts: 14.8 us -> 8.96 us
  waiting for transfers between devices: 42.3 us -> 45.1 us
    slice x3 -> x0, local copies, waits for them, and re-layouts: 3.65 us -> none  [the longest x1 1.57 us: body(): qkv_grad[:db, :qw]]
    ppermute x16, waiting for transfers between devices: 7.5 us -> 10.4 us  [exchange(): return lax.ppermute(x, 'shard', [(j, j ^ bit) for j in range(size)])]
    unnamed x48 -> x53, local copies, waits for them, and re-layouts: 5.7 us -> 5.95 us
  transfers between devices with their start and end apart: 25 -> 25, of which waited for: 11 -> 13; matrix products, arithmetic and copies ran while one was open for 8% -> 5% of each run, Pallas kernels for 40% -> 41%
where the time goes in v3:
time: 164 us; the launch traced here: 163 us
  Pallas kernels  69.9 us (43%)
  waiting for transfers between devices  45.1 us (28%)
  starting transfers between devices  34.9 us (21%)
  local copies, waits for them, and re-layouts  8.96 us (5%)
  other arithmetic  3.63 us (2%)
    ppermute x6, waiting for transfers between devices, double_ctx(): far = lax.ppermute(x, 'ctx', [(j, j ^ bit) for j in range(size)])  30.2 us
    pallas_call x1, Pallas kernels, experts_all(): pl.pallas_call(functools.partial(experts_all_kernel, n_sh, rows, n_exp),...  23.7 us
    pallas_call x1, Pallas kernels, attend_back(): pl.pallas_call(functools.partial(attend_back_kernel, n_exp), in_specs=[pl...  18.2 us
    all_to_all x3, starting transfers between devices, swap_ctx(): return lax.all_to_all(x, 'ctx', 0, 0, tiled=True)  17.4 us
    pallas_call x1, Pallas kernels, experts_own(): pl.pallas_call(experts_own_kernel, grid_spec=pltpu.PrefetchScalarGridSpec...  11.1 us
    ppermute x16, waiting for transfers between devices, exchange(): return lax.ppermute(x, 'shard', [(j, j ^ bit) for j in range(size)])  10.4 us
    ppermute x6, starting transfers between devices, double_ctx(): far = lax.ppermute(x, 'ctx', [(j, j ^ bit) for j in range(size)])  10.1 us
    ppermute x16, starting transfers between devices, exchange(): return lax.ppermute(x, 'shard', [(j, j ^ bit) for j in range(size)])  7.45 us
  transfers between devices with their start and end apart: 25, of which 13 were waited for; matrix products, arithmetic and copies ran while one was open for 5% of the time, Pallas kernels for 41%

profile of v3, /device:TPU:0, one launch (start us, length us, event | category | flops | bytes accessed | tf_op | source)
XLA Modules:
  0.0 163.5 jit_solution(9178464453591299497)
XLA Ops:
  0.7 3.0 %collective-permute-start.1 = (bf16[256,1024]{1,0:T(8,128)(2,1)}, bf16[256,1024]{1,0:T(8,128)(2,1)S(1)}, u32[]{:S(2)}, u32[]{:S(2)}) collective-permute-start(bf16[256,1024]{1,0:T(8,128)(2,1)} %ow_ref.1), channel_id=1, source_target_pairs={{0,2},{1,3},{2,0},{3,1},{4,6},{5,7},{6,4},{7,5},{8,10},{9,11},{10,... | collective-permute-start | bytes 1572872 | tf_op jit(solution)/shard_map/ppermute | solution.py:638
  3.7 0.7 broadcast_xor_fusion
  4.3 0.6 pad_add_fusion.pos_ref.refs_0_
  5.0 3.6 %project.1 = (bf16[8,2,128,128]{3,2,1,0:T(8,128)(2,1)}, bf16[8,3,128,128]{3,2,1,0:T(8,128)(2,1)}) custom-call(s32[11]{0:T(128)} %pad_add_fusion.pos_ref.refs_0_, bf16[128,1024]{1,0:T(8,128)(2,1)} %x_ref.3, f32[1,1024]{1,0:T(1,128)} %bitcast.16, bf16[1024,256]{1,0:T(8,128)(2,1)} %refs_6_.1, bf16[1024,128]{1,0:T(8,128)(2,1)} %refs_7_.1, ...), custom_call_target="tpu_custom_call" | custom-call | bytes 553500 | tf_op jit(solution)/shard_map/project/pallas_call | solution.py:104
  8.6 5.8 %all-to-all-start = ((bf16[8,2,128,128]{3,2,1,0:T(8,128)(2,1)}), bf16[8,2,128,128]{3,2,1,0:T(8,128)(2,1)S(1)}, u32[]{:S(2)}, u32[]{:S(2)}) async-start(bf16[8,2,128,128]{3,2,1,0:T(8,128)(2,1)} %get-tuple-element.43), calls=%async_computation | async-start | bytes 1048576 | tf_op jit(solution)/shard_map/all_to_all | solution.py:662
  14.4 1.4 collective-permute-done.1.refs_7_
  15.8 1.1 constant_dynamic-slice_fusion
  16.9 0.1 copy.35
  17.0 0.1 copy.31
  17.1 2.9 %collective-permute-start.3 = (bf16[1,2,128,128]{3,2,1,0:T(8,128)(2,1)S(1)}, bf16[1,2,128,128]{3,2,1,0:T(8,128)(2,1)S(1)}, u32[]{:S(2)}, u32[]{:S(2)}) collective-permute-start(bf16[1,2,128,128]{3,2,1,0:T(8,128)(2,1)S(1)} %bitcast.11), channel_id=1, source_target_pairs={{0,16},{4,20},{8,24},{12,28},{16,0},{20,4},{24,8},{28,12},{1,17},{... | collective-permute-start | bytes 196616 | tf_op jit(solution)/shard_map/ppermute | solution.py:643
  20.0 11.4 %collective-permute-done.3 = bf16[1,2,128,128]{3,2,1,0:T(8,128)(2,1)S(1)} collective-permute-done((bf16[1,2,128,128]{3,2,1,0:T(8,128)(2,1)S(1)}, bf16[1,2,128,128]{3,2,1,0:T(8,128)(2,1)S(1)}, u32[]{:S(2)}, u32[]{:S(2)}) %collective-permute-start.3) | collective-permute-done | bytes 65568 | tf_op jit(solution)/shard_map/ppermute | solution.py:643
  31.5 0.1 collective-permute-start.7
  31.6 0.0 copy-start.1
  31.6 0.0 copy-start.15
  31.6 4.2 %all-to-all-start.1 = ((bf16[8,3,128,128]{3,2,1,0:T(8,128)(2,1)}), bf16[8,3,128,128]{3,2,1,0:T(8,128)(2,1)S(1)}, u32[]{:S(2)}, u32[]{:S(2)}) async-start(bf16[8,3,128,128]{3,2,1,0:T(8,128)(2,1)} %get-tuple-element.45.q_ref), calls=%async_computation.1 | async-start | bytes 1572864 | tf_op jit(solution)/shard_map/all_to_all | solution.py:662
  35.8 3.7 %attend.1.refs_1_ = bf16[128,256]{1,0:T(8,128)(2,1)} custom-call(s32[11]{0:T(128)} %pad_add_fusion.pos_ref.refs_0_, bf16[8,3,128,128]{3,2,1,0:T(8,128)(2,1)} %get-tuple-element.45.q_ref, bf16[8,2,128,128]{3,2,1,0:T(8,128)(2,1)} %copy-done.1), custom_call_target="tpu_custom_call" | custom-call | bytes 553500 | tf_op jit(solution)/shard_map/attend/pallas_call | solution.py:158
  39.5 0.5 collective-permute-start.5
  40.1 0.7 copy.33.refs_12_
  40.8 0.2 copy.32
  41.0 0.8 pad.4.refs_11_.router_ref
  41.7 2.3 %collective-permute-done.5.refs_3_ = bf16[128,256]{1,0:T(8,128)(2,1)S(1)} collective-permute-done((bf16[128,256]{1,0:T(8,128)(2,1)}, bf16[128,256]{1,0:T(8,128)(2,1)S(1)}, u32[]{:S(2)}, u32[]{:S(2)}) %collective-permute-start.5) | collective-permute-done | bytes 65568 | tf_op jit(solution)/shard_map/ppermute | solution.py:638
  44.1 1.2 collective-permute-done.6.refs_4_
  45.3 0.6 copy-done.20
  45.9 3.4 %mid.1 = (f32[128,1024]{1,0:T(8,128)}, bf16[128,1024]{1,0:T(8,128)(2,1)}, f32[128,128]{1,0:T(8,128)}, bf16[1,272,128]{2,1,0:T(8,128)(2,1)}) custom-call(s32[11]{0:T(128)} %pad_add_fusion.pos_ref.refs_0_, bf16[128,256]{1,0:T(8,128)(2,1)} %attend.1.refs_1_, bf16[128,256]{1,0:T(8,128)(2,1)} %copy-done.19, bf16[128,256]{1,0:T(8,128)(2,1)} %copy-done.18, ...), custom_call_target="tpu_custom_call" | custom-call | bytes 738000 | tf_op jit(solution)/shard_map/mid/pallas_call | solution.py:218
  49.3 11.1 %experts_own.1 = (bf16[128,1024]{1,0:T(8,128)(2,1)}, bf16[128,1152]{1,0:T(8,128)(2,1)}) custom-call(s32[11]{0:T(128)} %pad_add_fusion.pos_ref.refs_0_, bf16[128,1024]{1,0:T(8,128)(2,1)} %get-tuple-element.47.x_ref, f32[128,1024]{1,0:T(8,128)} %og_ref.3, f32[128,128]{1,0:T(8,128)} %get-tuple-element.48.gates_ref, bf16[4,1024,512]{2,1,0:T(8,128)(2,1)} %refs_13_.1, ...), custom_call_target="tpu_custom_call" | custom-call | bytes 2029500 | tf_op jit(solution)/shard_map/experts_own/pallas_call | solution.py:277
  60.4 0.2 collective-permute-start.8
  60.6 2.9 %collective-permute-start.10 = (bf16[1,272,128]{2,1,0:T(8,128)(2,1)S(1)}, bf16[1,272,128]{2,1,0:T(8,128)(2,1)S(1)}, u32[]{:S(2)}, u32[]{:S(2)}) collective-permute-start(bf16[1,272,128]{2,1,0:T(8,128)(2,1)S(1)} %copy-done.17), channel_id=1, source_target_pairs={{0,16},{4,20},{8,24},{12,28},{16,0},{20,4},{24,8},{28,12},{1,17},{... | collective-permute-start | bytes 208904 | tf_op jit(solution)/shard_map/ppermute | solution.py:643
  63.5 1.5 collective-permute-start.12
  65.0 2.7 %collective-permute-done.10 = bf16[1,272,128]{2,1,0:T(8,128)(2,1)S(1)} collective-permute-done((bf16[1,272,128]{2,1,0:T(8,128)(2,1)S(1)}, bf16[1,272,128]{2,1,0:T(8,128)(2,1)S(1)}, u32[]{:S(2)}, u32[]{:S(2)}) %collective-permute-start.10) | collective-permute-done | bytes 69664 | tf_op jit(solution)/shard_map/ppermute | solution.py:643
  67.7 1.0 add_convert_fusion.1.ex_ref
  68.8 0.6 collective-permute-start.9
  69.4 0.7 collective-permute-start.11
  70.1 1.7 %collective-permute-done.12 = bf16[4,2,128,128]{3,2,1,0:T(8,128)(2,1)S(1)} collective-permute-done((bf16[4,2,128,128]{3,2,1,0:T(8,128)(2,1)S(1)}, bf16[4,2,128,128]{3,2,1,0:T(8,128)(2,1)S(1)}, u32[]{:S(2)}, u32[]{:S(2)}) %collective-permute-start.12) | collective-permute-done | bytes 262176 | tf_op jit(solution)/shard_map/ppermute | solution.py:643
  71.8 0.1 pad_maximum_fusion.refs_5_
  71.9 2.5 %collective-permute-done.11 = bf16[2,272,128]{2,1,0:T(8,128)(2,1)S(1)} collective-permute-done((bf16[2,272,128]{2,1,0:T(8,128)(2,1)S(1)}, bf16[2,272,128]{2,1,0:T(8,128)(2,1)S(1)}, u32[]{:S(2)}, u32[]{:S(2)}) %collective-permute-start.11) | collective-permute-done | bytes 139296 | tf_op jit(solution)/shard_map/ppermute | solution.py:643
  74.4 0.1 constant_dynamic-update-slice_fusion.3
  74.5 1.6 %collective-permute-done.9.far_ref = bf16[128,1152]{1,0:T(8,128)(2,1)S(1)} collective-permute-done((bf16[128,1152]{1,0:T(8,128)(2,1)S(1)}, bf16[128,1152]{1,0:T(8,128)(2,1)S(1)}, u32[]{:S(2)}, u32[]{:S(2)}) %collective-permute-start.9) | collective-permute-done | bytes 294944 | tf_op jit(solution)/shard_map/ppermute | solution.py:638
  76.1 0.7 copy-done.16
  76.8 3.2 %back_mid.1 = (f32[128,1024]{1,0:T(8,128)}, bf16[8,408,128]{2,1,0:T(8,128)(2,1)}) custom-call(bf16[128,1152]{1,0:T(8,128)(2,1)} %copy-done.5, bf16[128,1152]{1,0:T(8,128)(2,1)} %copy-done.16, f32[128,1024]{1,0:T(8,128)} %get-tuple-element.53.resid_ref, f32[1,1024]{1,0:T(1,128)} %bitcast.20, f32[128,128]{1,0:T(8,128)} %get-tuple-element.48.gates_ref, ...), custom_call_target="tpu_custom_call" | custom-call | bytes 553500 | tf_op jit(solution)/shard_map/back_mid/pallas_call | solution.py:344
  80.1 7.4 %all-to-all-start.2 = ((bf16[8,408,128]{2,1,0:T(8,128)(2,1)}), bf16[8,408,128]{2,1,0:T(8,128)(2,1)S(1)}, u32[]{:S(2)}, u32[]{:S(2)}) async-start(bf16[8,408,128]{2,1,0:T(8,128)(2,1)} %get-tuple-element.55), calls=%async_computation.2 | async-start | bytes 1671168 | tf_op jit(solution)/shard_map/all_to_all | solution.py:662
  87.5 0.6 collective-permute-start.13
  88.0 2.0 %collective-permute-start.14 = (bf16[4,272,128]{2,1,0:T(8,128)(2,1)S(1)}, bf16[4,272,128]{2,1,0:T(8,128)(2,1)S(1)}, u32[]{:S(2)}, u32[]{:S(2)}) collective-permute-start(bf16[4,272,128]{2,1,0:T(8,128)(2,1)S(1)} %get-tuple-element.73), channel_id=1, source_target_pairs={{0,4},{4,0},{8,12},{12,8},{16,20},{20,16},{24,28},{28,24},{1,5},{5... | collective-permute-start | bytes 835592 | tf_op jit(solution)/shard_map/ppermute | solution.py:643
  90.1 1.0 copy.34.refs_9_
  91.1 11.9 %collective-permute-done.14 = bf16[4,272,128]{2,1,0:T(8,128)(2,1)S(1)} collective-permute-done((bf16[4,272,128]{2,1,0:T(8,128)(2,1)S(1)}, bf16[4,272,128]{2,1,0:T(8,128)(2,1)S(1)}, u32[]{:S(2)}, u32[]{:S(2)}) %collective-permute-start.14) | collective-permute-done | bytes 278560 | tf_op jit(solution)/shard_map/ppermute | solution.py:643
  103.0 0.7 collective-permute-start.18
  103.7 4.5 %all-to-all-done.2.refs_3_.refs_9_ = bf16[8,408,128]{2,1,0:T(8,128)(2,1)S(1)} async-done(((bf16[8,408,128]{2,1,0:T(8,128)(2,1)}), bf16[8,408,128]{2,1,0:T(8,128)(2,1)S(1)}, u32[]{:S(2)}, u32[]{:S(2)}) %all-to-all-start.2) | async-done | bytes 835616 | tf_op jit(solution)/shard_map/all_to_all | solution.py:662
  108.2 0.9 copy-done
  109.1 18.2 %attend_back.1 = (bf16[128,2176]{1,0:T(8,128)(2,1)}, f32[128,256]{1,0:T(8,128)}, f32[128,128]{1,0:T(8,128)}, f32[128,128]{1,0:T(8,128)}, f32[256,128]{1,0:T(8,128)}, /*index=5*/f32[1,128]{1,0:T(1,128)}) custom-call(s32[11]{0:T(128)} %pad_add_fusion.pos_ref.refs_0_, bf16[8,3,128,128]{3,2,1,0:T(8,128)(2,1)} %copy-done.2, bf16[8,2,128,128]{3,2,1,0:T(8,128)(2,1)} %copy-done.1, ...), custom_call_target="tpu_custom_call" | custom-call | bytes 3321000 | tf_op jit(solution)/shard_map/attend_back/pallas_call | solution.py:477
  127.2 0.1 collective-permute-start.15
  127.3 0.5 collective-permute-start.17
  127.8 0.1 collective-permute-start.19
  127.9 1.6 collective-permute-done.15
  129.5 1.2 add_convert_fusion.near_ref
  130.7 0.7 collective-permute-start.16
  131.4 0.5 collective-permute-start.21
  131.9 2.1 %collective-permute-done.20.refs_6_ = bf16[8,2,128,128]{3,2,1,0:T(8,128)(2,1)S(1)} collective-permute-done((bf16[8,2,128,128]{3,2,1,0:T(8,128)(2,1)S(1)}, bf16[8,2,128,128]{3,2,1,0:T(8,128)(2,1)S(1)}, u32[]{:S(2)}, u32[]{:S(2)}) %collective-permute-start.20) | collective-permute-done | bytes 524320 | tf_op jit(solution)/shard_map/ppermute | solution.py:638
  134.0 0.2 collective-permute-done.21.refs_8_
  134.3 0.5 copy-done.11
  134.8 0.2 copy-done.12
  135.1 0.2 copy-done.8
  135.2 0.8 copy-done.9
  136.0 23.7 %experts_all.1 = (f32[4,128,512]{2,1,0:T(8,128)}, f32[4,128,512]{2,1,0:T(8,128)}, f32[4,512,128]{2,1,0:T(8,128)}, f32[16,128]{1,0:T(8,128)}) custom-call(s32[11]{0:T(128)} %pad_add_fusion.pos_ref.refs_0_, bf16[8,272,128]{2,1,0:T(8,128)(2,1)} %copy-done.6, bf16[8,272,128]{2,1,0:T(8,128)(2,1)} %copy-done.8, bf16[8,272,128]{2,1,0:T(8,128)(2,1)} %copy-done.7, ...), custom_call_target="tpu_custom_call" | custom-call | bytes 4612500 | tf_op jit(solution)/shard_map/experts_all/pallas_call | solution.py:587
  159.8 0.8 copy-done.10
  160.6 2.9 %finish.1 = (f32[128,1024]{1,0:T(8,128)}, f32[1,128]{1,0:T(1,128)}, f32[128,1024]{1,0:T(8,128)}) custom-call(bf16[128,2176]{1,0:T(8,128)(2,1)} %copy-done.3, bf16[128,2176]{1,0:T(8,128)(2,1)} %copy-done.10, bf16[128,1024]{1,0:T(8,128)(2,1)} %x_ref.3, f32[1,1024]{1,0:T(1,128)} %bitcast.17, f32[128,1024]{1,0:T(8,128)} %get-tuple-element.59.dmid_ref, ...), custom_call_target="tpu_custom_call" | custom-call | bytes 369000 | tf_op jit(solution)/shard_map/finish/pallas_call | solution.py:623
  (60 shorter events, 0.3 us)
Async XLA Ops:
  0.6 39.4 %copy-start.23 = (s32[128,8]{0,1:T(8,128)S(1)}, s32[128,8]{0,1:T(8,128)}, u32[]{:S(2)}) copy-start(s32[128,8]{0,1:T(8,128)} %param.27) | copy-start | bytes 12292
  0.7 40.1 %copy-start.22 = (bf16[1024,16]{0,1:T(8,128)(2,1)S(1)}, bf16[1024,16]{0,1:T(8,128)(2,1)}, u32[]{:S(2)}) copy-start(bf16[1024,16]{0,1:T(8,128)(2,1)} %param.23) | copy-start | bytes 98308
  0.7 15.1 %collective-permute-start.1 = (bf16[256,1024]{1,0:T(8,128)(2,1)}, bf16[256,1024]{1,0:T(8,128)(2,1)S(1)}, u32[]{:S(2)}, u32[]{:S(2)}) collective-permute-start(bf16[256,1024]{1,0:T(8,128)(2,1)} %ow_ref.1), channel_id=1, source_target_pairs={{0,2},{1,3},{2,0},{3,1},{4,6},{5,7},{6,4},{7,5},{8,10},{9,11},{10,... | collective-permute-start | bytes 1572872 | tf_op jit(solution)/shard_map/ppermute | solution.py:638
  8.6 23.0 %all-to-all-start = ((bf16[8,2,128,128]{3,2,1,0:T(8,128)(2,1)}), bf16[8,2,128,128]{3,2,1,0:T(8,128)(2,1)S(1)}, u32[]{:S(2)}, u32[]{:S(2)}) async-start(bf16[8,2,128,128]{3,2,1,0:T(8,128)(2,1)} %get-tuple-element.43), calls=%async_computation | async-start | bytes 1048576 | tf_op jit(solution)/shard_map/all_to_all | solution.py:662
  14.4 17.2 %collective-permute-start = (bf16[256,1024]{1,0:T(8,128)(2,1)}, bf16[256,1024]{1,0:T(8,128)(2,1)S(1)}, u32[]{:S(2)}, u32[]{:S(2)}) collective-permute-start(bf16[256,1024]{1,0:T(8,128)(2,1)} %ow_ref.1), channel_id=1, source_target_pairs={{0,1},{1,0},{2,3},{3,2},{4,5},{5,4},{6,7},{7,6},{8,9},{9,8},{10,11... | collective-permute-start | bytes 1572872 | tf_op jit(solution)/shard_map/ppermute | solution.py:638
  15.8 29.5 %copy-start.13 = (bf16[256,1024]{1,0:T(8,128)(2,1)}, bf16[256,1024]{1,0:T(8,128)(2,1)S(1)}, u32[]{:S(2)}) copy-start(bf16[256,1024]{1,0:T(8,128)(2,1)S(1)} %collective-permute-done.1.refs_7_) | copy-start | bytes 1572868
  15.8 15.8 %collective-permute-start.2 = (bf16[256,1024]{1,0:T(8,128)(2,1)S(1)}, bf16[256,1024]{1,0:T(8,128)(2,1)S(1)}, u32[]{:S(2)}, u32[]{:S(2)}) collective-permute-start(bf16[256,1024]{1,0:T(8,128)(2,1)S(1)} %collective-permute-done.1.refs_7_), channel_id=1, source_target_pairs={{0,1},{1,0},{2,3},{3,2},{4,5},{5,4},{6,7},{7,6},{8,9},{9,8},{10,11... | collective-permute-start | bytes 1572872 | tf_op jit(solution)/shard_map/ppermute | solution.py:638
  17.1 14.3 %collective-permute-start.3 = (bf16[1,2,128,128]{3,2,1,0:T(8,128)(2,1)S(1)}, bf16[1,2,128,128]{3,2,1,0:T(8,128)(2,1)S(1)}, u32[]{:S(2)}, u32[]{:S(2)}) collective-permute-start(bf16[1,2,128,128]{3,2,1,0:T(8,128)(2,1)S(1)} %bitcast.11), channel_id=1, source_target_pairs={{0,16},{4,20},{8,24},{12,28},{16,0},{20,4},{24,8},{28,12},{1,17},{... | collective-permute-start | bytes 196616 | tf_op jit(solution)/shard_map/ppermute | solution.py:643
  31.5 12.5 %collective-permute-start.7 = (bf16[2,2,128,128]{3,2,1,0:T(8,128)(2,1)S(1)}, bf16[2,2,128,128]{3,2,1,0:T(8,128)(2,1)S(1)}, u32[]{:S(2)}, u32[]{:S(2)}) collective-permute-start(bf16[2,2,128,128]{3,2,1,0:T(8,128)(2,1)S(1)} %pad_maximum_fusion.3), channel_id=1, source_target_pairs={{0,8},{4,12},{8,0},{12,4},{16,24},{20,28},{24,16},{28,20},{1,9},{5... | collective-permute-start | bytes 393224 | tf_op jit(solution)/shard_map/ppermute | solution.py:643
  31.6 13.7 %copy-start.14 = (bf16[256,1024]{1,0:T(8,128)(2,1)}, bf16[256,1024]{1,0:T(8,128)(2,1)S(1)}, u32[]{:S(2)}) copy-start(bf16[256,1024]{1,0:T(8,128)(2,1)S(1)} %collective-permute-done.refs_6_) | copy-start | bytes 1572868
  31.6 4.2 %copy-start.1 = (bf16[8,2,128,128]{3,2,1,0:T(8,128)(2,1)}, bf16[8,2,128,128]{3,2,1,0:T(8,128)(2,1)S(1)}, u32[]{:S(2)}) copy-start(bf16[8,2,128,128]{3,2,1,0:T(8,128)(2,1)S(1)} %all-to-all-done.kv_ref.refs_2_) | copy-start | bytes 1572868
  31.6 13.7 %copy-start.15 = (bf16[256,1024]{1,0:T(8,128)(2,1)}, bf16[256,1024]{1,0:T(8,128)(2,1)S(1)}, u32[]{:S(2)}) copy-start(bf16[256,1024]{1,0:T(8,128)(2,1)S(1)} %collective-permute-done.2.refs_8_) | copy-start | bytes 1572868
  31.6 48.5 %all-to-all-start.1 = ((bf16[8,3,128,128]{3,2,1,0:T(8,128)(2,1)}), bf16[8,3,128,128]{3,2,1,0:T(8,128)(2,1)S(1)}, u32[]{:S(2)}, u32[]{:S(2)}) async-start(bf16[8,3,128,128]{3,2,1,0:T(8,128)(2,1)} %get-tuple-element.45.q_ref), calls=%async_computation.1 | async-start | bytes 1572864 | tf_op jit(solution)/shard_map/all_to_all | solution.py:662
  39.5 4.5 %collective-permute-start.5 = (bf16[128,256]{1,0:T(8,128)(2,1)}, bf16[128,256]{1,0:T(8,128)(2,1)S(1)}, u32[]{:S(2)}, u32[]{:S(2)}) collective-permute-start(bf16[128,256]{1,0:T(8,128)(2,1)} %attend.1.refs_1_), channel_id=1, source_target_pairs={{0,2},{1,3},{2,0},{3,1},{4,6},{5,7},{6,4},{7,5},{8,10},{9,11},{10,... | collective-permute-start | bytes 196616 | tf_op jit(solution)/shard_map/ppermute | solution.py:638
  41.7 2.3 %collective-permute-start.4 = (bf16[128,256]{1,0:T(8,128)(2,1)}, bf16[128,256]{1,0:T(8,128)(2,1)S(1)}, u32[]{:S(2)}, u32[]{:S(2)}) collective-permute-start(bf16[128,256]{1,0:T(8,128)(2,1)} %attend.1.refs_1_), channel_id=1, source_target_pairs={{0,1},{1,0},{2,3},{3,2},{4,5},{5,4},{6,7},{7,6},{8,9},{9,8},{10,11... | collective-permute-start | bytes 196616 | tf_op jit(solution)/shard_map/ppermute | solution.py:638
  44.0 1.3 copy-start.18
  44.0 1.3 collective-permute-start.6
  44.1 1.2 copy-start.19
  45.3 0.6 copy-start.20
  49.3 11.3 %copy-start.17 = (bf16[1,272,128]{2,1,0:T(8,128)(2,1)S(1)}, bf16[1,272,128]{2,1,0:T(8,128)(2,1)}, u32[]{:S(2)}) copy-start(bf16[1,272,128]{2,1,0:T(8,128)(2,1)} %get-tuple-element.50) | copy-start | bytes 208900
  60.4 29.6 %copy-start.21 = (f32[1024]{0:T(1024)S(1)}, f32[1024]{0:T(1024)}, u32[]{:S(2)}) copy-start(f32[1024]{0:T(1024)} %param.17) | copy-start | bytes 12292
  60.4 7.3 %collective-permute-start.8 = (bf16[128,1152]{1,0:T(8,128)(2,1)}, bf16[128,1152]{1,0:T(8,128)(2,1)S(1)}, u32[]{:S(2)}, u32[]{:S(2)}) collective-permute-start(bf16[128,1152]{1,0:T(8,128)(2,1)} %get-tuple-element.49), channel_id=1, source_target_pairs={{0,1},{1,0},{2,3},{3,2},{4,5},{5,4},{6,7},{7,6},{8,9},{9,8},{10,11... | collective-permute-start | bytes 884744 | tf_op jit(solution)/shard_map/ppermute | solution.py:638
  60.6 7.1 %collective-permute-start.10 = (bf16[1,272,128]{2,1,0:T(8,128)(2,1)S(1)}, bf16[1,272,128]{2,1,0:T(8,128)(2,1)S(1)}, u32[]{:S(2)}, u32[]{:S(2)}) collective-permute-start(bf16[1,272,128]{2,1,0:T(8,128)(2,1)S(1)} %copy-done.17), channel_id=1, source_target_pairs={{0,16},{4,20},{8,24},{12,28},{16,0},{20,4},{24,8},{28,12},{1,17},{... | collective-permute-start | bytes 208904 | tf_op jit(solution)/shard_map/ppermute | solution.py:643
  63.5 8.3 %collective-permute-start.12 = (bf16[4,2,128,128]{3,2,1,0:T(8,128)(2,1)S(1)}, bf16[4,2,128,128]{3,2,1,0:T(8,128)(2,1)S(1)}, u32[]{:S(2)}, u32[]{:S(2)}) collective-permute-start(bf16[4,2,128,128]{3,2,1,0:T(8,128)(2,1)S(1)} %pad_maximum_fusion.1), channel_id=1, source_target_pairs={{0,4},{4,0},{8,12},{12,8},{16,20},{20,16},{24,28},{28,24},{1,5},{5... | collective-permute-start | bytes 786440 | tf_op jit(solution)/shard_map/ppermute | solution.py:643
  68.8 7.4 %copy-start.5 = (bf16[128,1152]{1,0:T(8,128)(2,1)}, bf16[128,1152]{1,0:T(8,128)(2,1)S(1)}, u32[]{:S(2)}) copy-start(bf16[128,1152]{1,0:T(8,128)(2,1)S(1)} %add_convert_fusion.1.ex_ref) | copy-start | bytes 884740
  68.8 7.4 %collective-permute-start.9 = (bf16[128,1152]{1,0:T(8,128)(2,1)S(1)}, bf16[128,1152]{1,0:T(8,128)(2,1)S(1)}, u32[]{:S(2)}, u32[]{:S(2)}) collective-permute-start(bf16[128,1152]{1,0:T(8,128)(2,1)S(1)} %add_convert_fusion.1.ex_ref), channel_id=1, source_target_pairs={{0,2},{1,3},{2,0},{3,1},{4,6},{5,7},{6,4},{7,5},{8,10},{9,11},{10,... | collective-permute-start | bytes 884744 | tf_op jit(solution)/shard_map/ppermute | solution.py:638
  69.4 5.1 %collective-permute-start.11 = (bf16[2,272,128]{2,1,0:T(8,128)(2,1)S(1)}, bf16[2,272,128]{2,1,0:T(8,128)(2,1)S(1)}, u32[]{:S(2)}, u32[]{:S(2)}) collective-permute-start(bf16[2,272,128]{2,1,0:T(8,128)(2,1)S(1)} %pad_maximum_fusion.2), channel_id=1, source_target_pairs={{0,8},{4,12},{8,0},{12,4},{16,24},{20,28},{24,16},{28,20},{1,9},{5... | collective-permute-start | bytes 417800 | tf_op jit(solution)/shard_map/ppermute | solution.py:643
  71.9 59.5 %copy-start.4 = (bf16[8,2,128,128]{3,2,1,0:T(8,128)(2,1)}, bf16[8,2,128,128]{3,2,1,0:T(8,128)(2,1)S(1)}, u32[]{:S(2)}) copy-start(bf16[8,2,128,128]{3,2,1,0:T(8,128)(2,1)S(1)} %pad_maximum_fusion.refs_5_) | copy-start | bytes 1572868
  76.1 0.7 copy-start.16
  80.1 28.1 %copy-start.2 = (bf16[8,3,128,128]{3,2,1,0:T(8,128)(2,1)}, bf16[8,3,128,128]{3,2,1,0:T(8,128)(2,1)S(1)}, u32[]{:S(2)}) copy-start(bf16[8,3,128,128]{3,2,1,0:T(8,128)(2,1)S(1)} %all-to-all-done.1.refs_1_) | copy-start | bytes 2359300
  80.1 28.1 %all-to-all-start.2 = ((bf16[8,408,128]{2,1,0:T(8,128)(2,1)}), bf16[8,408,128]{2,1,0:T(8,128)(2,1)S(1)}, u32[]{:S(2)}, u32[]{:S(2)}) async-start(bf16[8,408,128]{2,1,0:T(8,128)(2,1)} %get-tuple-element.55), calls=%async_computation.2 | async-start | bytes 1671168 | tf_op jit(solution)/shard_map/all_to_all | solution.py:662
  87.5 16.2 %collective-permute-start.13 = (bf16[8,2,128,128]{3,2,1,0:T(8,128)(2,1)S(1)}, bf16[8,2,128,128]{3,2,1,0:T(8,128)(2,1)}, u32[]{:S(2)}, u32[]{:S(2)}) collective-permute-start(bf16[8,2,128,128]{3,2,1,0:T(8,128)(2,1)S(1)} %pad_maximum_fusion.refs_5_), channel_id=1, source_target_pairs={{0,2},{1,3},{2,0},{3,1},{4,6},{5,7},{6,4},{7,5},{8,10},{9,11},{10,... | collective-permute-start | bytes 1572872 | tf_op jit(solution)/shard_map/ppermute | solution.py:638
  88.0 14.9 %collective-permute-start.14 = (bf16[4,272,128]{2,1,0:T(8,128)(2,1)S(1)}, bf16[4,272,128]{2,1,0:T(8,128)(2,1)S(1)}, u32[]{:S(2)}, u32[]{:S(2)}) collective-permute-start(bf16[4,272,128]{2,1,0:T(8,128)(2,1)S(1)} %get-tuple-element.73), channel_id=1, source_target_pairs={{0,4},{4,0},{8,12},{12,8},{16,20},{20,16},{24,28},{28,24},{1,5},{5... | collective-permute-start | bytes 835592 | tf_op jit(solution)/shard_map/ppermute | solution.py:643
  103.0 31.3 %copy-start.6 = (bf16[8,272,128]{2,1,0:T(8,128)(2,1)}, bf16[8,272,128]{2,1,0:T(8,128)(2,1)S(1)}, u32[]{:S(2)}) copy-start(bf16[8,272,128]{2,1,0:T(8,128)(2,1)S(1)} %constant_dynamic-update-slice_fusion.2.refs_1_) | copy-start | bytes 1671172
  103.0 24.8 %collective-permute-start.18 = (bf16[8,272,128]{2,1,0:T(8,128)(2,1)S(1)}, bf16[8,272,128]{2,1,0:T(8,128)(2,1)S(1)}, u32[]{:S(2)}, u32[]{:S(2)}) collective-permute-start(bf16[8,272,128]{2,1,0:T(8,128)(2,1)S(1)} %constant_dynamic-update-slice_fusion.2.refs_1_), channel_id=1, source_target_pairs={{0,2},{1,3},{2,0},{3,1},{4,6},{5,7},{6,4},{7,5},{8,10},{9,11},{10,... | collective-permute-start | bytes 1671176 | tf_op jit(solution)/shard_map/ppermute | solution.py:638
  108.2 0.9 copy-start
  127.2 2.2 %collective-permute-start.15 = (bf16[128,2176]{1,0:T(8,128)(2,1)}, bf16[128,2176]{1,0:T(8,128)(2,1)S(1)}, u32[]{:S(2)}, u32[]{:S(2)}) collective-permute-start(bf16[128,2176]{1,0:T(8,128)(2,1)} %get-tuple-element.58), channel_id=1, source_target_pairs={{0,1},{1,0},{2,3},{3,2},{4,5},{5,4},{6,7},{7,6},{8,9},{9,8},{10,11... | collective-permute-start | bytes 1671176 | tf_op jit(solution)/shard_map/ppermute | solution.py:638
  127.3 6.9 %collective-permute-start.17 = (bf16[8,272,128]{2,1,0:T(8,128)(2,1)S(1)}, bf16[8,272,128]{2,1,0:T(8,128)(2,1)S(1)}, u32[]{:S(2)}, u32[]{:S(2)}) collective-permute-start(bf16[8,272,128]{2,1,0:T(8,128)(2,1)S(1)} %constant_dynamic-update-slice_fusion.2.refs_1_), channel_id=1, source_target_pairs={{0,1},{1,0},{2,3},{3,2},{4,5},{5,4},{6,7},{7,6},{8,9},{9,8},{10,11... | collective-permute-start | bytes 1671176 | tf_op jit(solution)/shard_map/ppermute | solution.py:638
  127.8 6.5 %copy-start.7 = (bf16[8,272,128]{2,1,0:T(8,128)(2,1)}, bf16[8,272,128]{2,1,0:T(8,128)(2,1)S(1)}, u32[]{:S(2)}) copy-start(bf16[8,272,128]{2,1,0:T(8,128)(2,1)S(1)} %collective-permute-done.18.refs_3_) | copy-start | bytes 1671172
  127.8 6.4 %collective-permute-start.19 = (bf16[8,272,128]{2,1,0:T(8,128)(2,1)S(1)}, bf16[8,272,128]{2,1,0:T(8,128)(2,1)S(1)}, u32[]{:S(2)}, u32[]{:S(2)}) collective-permute-start(bf16[8,272,128]{2,1,0:T(8,128)(2,1)S(1)} %collective-permute-done.18.refs_3_), channel_id=1, source_target_pairs={{0,1},{1,0},{2,3},{3,2},{4,5},{5,4},{6,7},{7,6},{8,9},{9,8},{10,11... | collective-permute-start | bytes 1671176 | tf_op jit(solution)/shard_map/ppermute | solution.py:638
  130.7 29.1 %copy-start.3 = (bf16[128,2176]{1,0:T(8,128)(2,1)}, bf16[128,2176]{1,0:T(8,128)(2,1)S(1)}, u32[]{:S(2)}) copy-start(bf16[128,2176]{1,0:T(8,128)(2,1)S(1)} %add_convert_fusion.near_ref) | copy-start | bytes 1671172
  130.7 29.1 %collective-permute-start.16 = (bf16[128,2176]{1,0:T(8,128)(2,1)S(1)}, bf16[128,2176]{1,0:T(8,128)(2,1)S(1)}, u32[]{:S(2)}, u32[]{:S(2)}) collective-permute-start(bf16[128,2176]{1,0:T(8,128)(2,1)S(1)} %add_convert_fusion.near_ref), channel_id=1, source_target_pairs={{0,2},{1,3},{2,0},{3,1},{4,6},{5,7},{6,4},{7,5},{8,10},{9,11},{10,... | collective-permute-start | bytes 1671176 | tf_op jit(solution)/shard_map/ppermute | solution.py:638
  131.4 2.6 %collective-permute-start.20 = (bf16[8,2,128,128]{3,2,1,0:T(8,128)(2,1)S(1)}, bf16[8,2,128,128]{3,2,1,0:T(8,128)(2,1)S(1)}, u32[]{:S(2)}, u32[]{:S(2)}) collective-permute-start(bf16[8,2,128,128]{3,2,1,0:T(8,128)(2,1)S(1)} %pad_maximum_fusion.refs_5_), channel_id=1, source_target_pairs={{0,1},{1,0},{2,3},{3,2},{4,5},{5,4},{6,7},{7,6},{8,9},{9,8},{10,11... | collective-permute-start | bytes 1572872 | tf_op jit(solution)/shard_map/ppermute | solution.py:638
  131.4 2.9 %collective-permute-start.21 = (bf16[8,2,128,128]{3,2,1,0:T(8,128)(2,1)}, bf16[8,2,128,128]{3,2,1,0:T(8,128)(2,1)S(1)}, u32[]{:S(2)}, u32[]{:S(2)}) collective-permute-start(bf16[8,2,128,128]{3,2,1,0:T(8,128)(2,1)} %collective-permute-done.13.refs_7_), channel_id=1, source_target_pairs={{0,1},{1,0},{2,3},{3,2},{4,5},{5,4},{6,7},{7,6},{8,9},{9,8},{10,11... | collective-permute-start | bytes 1572872 | tf_op jit(solution)/shard_map/ppermute | solution.py:638
  134.0 0.8 copy-start.11
  134.3 0.8 copy-start.12
  134.3 1.0 copy-start.8
  135.2 0.8 copy-start.9
  159.8 0.8 copy-start.10

commit v4 on v3

--- a/solution.py
+++ b/solution.py
@@ -429,7 +429,7 @@
             lax.fori_loop(0, n // bq, loop, 0)
         return carry
 
-    lax.fori_loop(0, heads, per_head, 0)
+    lax.fori_loop(0, heads, per_head, 0, unroll=n <= 1024)
     pieces = [(h, g) for h in range(heads) for g in range(group)]
     small = (heads + 1) * rows
     gain_rows = jnp.sum(do_ref[:, small + n_exp :].astype(F32), axis=0)

time: 164 us -> 164 us (level)
  no operation moved by 1% of the time
where the time goes in v4:
time: 164 us; the launch traced here: 163 us
  Pallas kernels  69.8 us (43%)
  waiting for transfers between devices  45.1 us (28%)
  starting transfers between devices  34.9 us (21%)
  local copies, waits for them, and re-layouts  8.96 us (5%)
  other arithmetic  3.63 us (2%)
    ppermute x6, waiting for transfers between devices, double_ctx(): far = lax.ppermute(x, 'ctx', [(j, j ^ bit) for j in range(size)])  30.2 us
    pallas_call x1, Pallas kernels, experts_all(): pl.pallas_call(functools.partial(experts_all_kernel, n_sh, rows, n_exp),...  23.5 us
    pallas_call x1, Pallas kernels, attend_back(): pl.pallas_call(functools.partial(attend_back_kernel, n_exp), in_specs=[pl...  18.2 us
    all_to_all x3, starting transfers between devices, swap_ctx(): return lax.all_to_all(x, 'ctx', 0, 0, tiled=True)  17.4 us
    pallas_call x1, Pallas kernels, experts_own(): pl.pallas_call(experts_own_kernel, grid_spec=pltpu.PrefetchScalarGridSpec...  11.1 us
    ppermute x16, waiting for transfers between devices, exchange(): return lax.ppermute(x, 'shard', [(j, j ^ bit) for j in range(size)])  10.4 us
    ppermute x6, starting transfers between devices, double_ctx(): far = lax.ppermute(x, 'ctx', [(j, j ^ bit) for j in range(size)])  10.1 us
    ppermute x16, starting transfers between devices, exchange(): return lax.ppermute(x, 'shard', [(j, j ^ bit) for j in range(size)])  7.43 us
  transfers between devices with their start and end apart: 25, of which 13 were waited for; matrix products, arithmetic and copies ran while one was open for 5% of the time, Pallas kernels for 41%

profile of v4, /device:TPU:0, one launch (start us, length us, event | category | flops | bytes accessed | tf_op | source)
XLA Modules:
  0.0 163.3 jit_solution(10761660642991412045)
XLA Ops:
  0.7 3.0 %collective-permute-start.1 = (bf16[256,1024]{1,0:T(8,128)(2,1)}, bf16[256,1024]{1,0:T(8,128)(2,1)S(1)}, u32[]{:S(2)}, u32[]{:S(2)}) collective-permute-start(bf16[256,1024]{1,0:T(8,128)(2,1)} %ow_ref.1), channel_id=1, source_target_pairs={{0,2},{1,3},{2,0},{3,1},{4,6},{5,7},{6,4},{7,5},{8,10},{9,11},{10,... | collective-permute-start | bytes 1572872 | tf_op jit(solution)/shard_map/ppermute | solution.py:638
  3.7 0.7 broadcast_xor_fusion
  4.3 0.6 pad_add_fusion.pos_ref.refs_0_
  5.0 3.6 %project.1 = (bf16[8,2,128,128]{3,2,1,0:T(8,128)(2,1)}, bf16[8,3,128,128]{3,2,1,0:T(8,128)(2,1)}) custom-call(s32[11]{0:T(128)} %pad_add_fusion.pos_ref.refs_0_, bf16[128,1024]{1,0:T(8,128)(2,1)} %x_ref.3, f32[1,1024]{1,0:T(1,128)} %bitcast.16, bf16[1024,256]{1,0:T(8,128)(2,1)} %refs_6_.1, bf16[1024,128]{1,0:T(8,128)(2,1)} %refs_7_.1, ...), custom_call_target="tpu_custom_call" | custom-call | bytes 553500 | tf_op jit(solution)/shard_map/project/pallas_call | solution.py:104
  8.6 5.8 %all-to-all-start = ((bf16[8,2,128,128]{3,2,1,0:T(8,128)(2,1)}), bf16[8,2,128,128]{3,2,1,0:T(8,128)(2,1)S(1)}, u32[]{:S(2)}, u32[]{:S(2)}) async-start(bf16[8,2,128,128]{3,2,1,0:T(8,128)(2,1)} %get-tuple-element.43), calls=%async_computation | async-start | bytes 1048576 | tf_op jit(solution)/shard_map/all_to_all | solution.py:662
  14.4 1.4 collective-permute-done.1.refs_7_
  15.8 1.1 constant_dynamic-slice_fusion
  16.9 0.1 copy.35
  17.0 0.1 copy.31
  17.1 2.9 %collective-permute-start.3 = (bf16[1,2,128,128]{3,2,1,0:T(8,128)(2,1)S(1)}, bf16[1,2,128,128]{3,2,1,0:T(8,128)(2,1)S(1)}, u32[]{:S(2)}, u32[]{:S(2)}) collective-permute-start(bf16[1,2,128,128]{3,2,1,0:T(8,128)(2,1)S(1)} %bitcast.11), channel_id=1, source_target_pairs={{0,16},{4,20},{8,24},{12,28},{16,0},{20,4},{24,8},{28,12},{1,17},{... | collective-permute-start | bytes 196616 | tf_op jit(solution)/shard_map/ppermute | solution.py:643
  20.0 11.4 %collective-permute-done.3 = bf16[1,2,128,128]{3,2,1,0:T(8,128)(2,1)S(1)} collective-permute-done((bf16[1,2,128,128]{3,2,1,0:T(8,128)(2,1)S(1)}, bf16[1,2,128,128]{3,2,1,0:T(8,128)(2,1)S(1)}, u32[]{:S(2)}, u32[]{:S(2)}) %collective-permute-start.3) | collective-permute-done | bytes 65568 | tf_op jit(solution)/shard_map/ppermute | solution.py:643
  31.5 0.1 collective-permute-start.7
  31.6 0.0 copy-start.1
  31.6 0.0 copy-start.15
  31.6 4.2 %all-to-all-start.1 = ((bf16[8,3,128,128]{3,2,1,0:T(8,128)(2,1)}), bf16[8,3,128,128]{3,2,1,0:T(8,128)(2,1)S(1)}, u32[]{:S(2)}, u32[]{:S(2)}) async-start(bf16[8,3,128,128]{3,2,1,0:T(8,128)(2,1)} %get-tuple-element.45.q_ref), calls=%async_computation.1 | async-start | bytes 1572864 | tf_op jit(solution)/shard_map/all_to_all | solution.py:662
  35.8 3.7 %attend.1.refs_1_ = bf16[128,256]{1,0:T(8,128)(2,1)} custom-call(s32[11]{0:T(128)} %pad_add_fusion.pos_ref.refs_0_, bf16[8,3,128,128]{3,2,1,0:T(8,128)(2,1)} %get-tuple-element.45.q_ref, bf16[8,2,128,128]{3,2,1,0:T(8,128)(2,1)} %copy-done.1), custom_call_target="tpu_custom_call" | custom-call | bytes 553500 | tf_op jit(solution)/shard_map/attend/pallas_call | solution.py:158
  39.5 0.5 collective-permute-start.5
  40.1 0.7 copy.33.refs_12_
  40.8 0.2 copy.32
  41.0 0.8 pad.4.refs_11_.router_ref
  41.7 2.3 %collective-permute-done.5.refs_3_ = bf16[128,256]{1,0:T(8,128)(2,1)S(1)} collective-permute-done((bf16[128,256]{1,0:T(8,128)(2,1)}, bf16[128,256]{1,0:T(8,128)(2,1)S(1)}, u32[]{:S(2)}, u32[]{:S(2)}) %collective-permute-start.5) | collective-permute-done | bytes 65568 | tf_op jit(solution)/shard_map/ppermute | solution.py:638
  44.1 1.2 collective-permute-done.6.refs_4_
  45.3 0.6 copy-done.20
  45.9 3.4 %mid.1 = (f32[128,1024]{1,0:T(8,128)}, bf16[128,1024]{1,0:T(8,128)(2,1)}, f32[128,128]{1,0:T(8,128)}, bf16[1,272,128]{2,1,0:T(8,128)(2,1)}) custom-call(s32[11]{0:T(128)} %pad_add_fusion.pos_ref.refs_0_, bf16[128,256]{1,0:T(8,128)(2,1)} %attend.1.refs_1_, bf16[128,256]{1,0:T(8,128)(2,1)} %copy-done.19, bf16[128,256]{1,0:T(8,128)(2,1)} %copy-done.18, ...), custom_call_target="tpu_custom_call" | custom-call | bytes 738000 | tf_op jit(solution)/shard_map/mid/pallas_call | solution.py:218
  49.3 11.1 %experts_own.1 = (bf16[128,1024]{1,0:T(8,128)(2,1)}, bf16[128,1152]{1,0:T(8,128)(2,1)}) custom-call(s32[11]{0:T(128)} %pad_add_fusion.pos_ref.refs_0_, bf16[128,1024]{1,0:T(8,128)(2,1)} %get-tuple-element.47.x_ref, f32[128,1024]{1,0:T(8,128)} %og_ref.3, f32[128,128]{1,0:T(8,128)} %get-tuple-element.48.gates_ref, bf16[4,1024,512]{2,1,0:T(8,128)(2,1)} %refs_13_.1, ...), custom_call_target="tpu_custom_call" | custom-call | bytes 2029500 | tf_op jit(solution)/shard_map/experts_own/pallas_call | solution.py:277
  60.4 0.2 collective-permute-start.8
  60.6 2.9 %collective-permute-start.10 = (bf16[1,272,128]{2,1,0:T(8,128)(2,1)S(1)}, bf16[1,272,128]{2,1,0:T(8,128)(2,1)S(1)}, u32[]{:S(2)}, u32[]{:S(2)}) collective-permute-start(bf16[1,272,128]{2,1,0:T(8,128)(2,1)S(1)} %copy-done.17), channel_id=1, source_target_pairs={{0,16},{4,20},{8,24},{12,28},{16,0},{20,4},{24,8},{28,12},{1,17},{... | collective-permute-start | bytes 208904 | tf_op jit(solution)/shard_map/ppermute | solution.py:643
  63.5 1.5 collective-permute-start.12
  65.0 2.7 %collective-permute-done.10 = bf16[1,272,128]{2,1,0:T(8,128)(2,1)S(1)} collective-permute-done((bf16[1,272,128]{2,1,0:T(8,128)(2,1)S(1)}, bf16[1,272,128]{2,1,0:T(8,128)(2,1)S(1)}, u32[]{:S(2)}, u32[]{:S(2)}) %collective-permute-start.10) | collective-permute-done | bytes 69664 | tf_op jit(solution)/shard_map/ppermute | solution.py:643
  67.7 1.0 add_convert_fusion.1.ex_ref
  68.8 0.6 collective-permute-start.9
  69.4 0.7 collective-permute-start.11
  70.1 1.7 %collective-permute-done.12 = bf16[4,2,128,128]{3,2,1,0:T(8,128)(2,1)S(1)} collective-permute-done((bf16[4,2,128,128]{3,2,1,0:T(8,128)(2,1)S(1)}, bf16[4,2,128,128]{3,2,1,0:T(8,128)(2,1)S(1)}, u32[]{:S(2)}, u32[]{:S(2)}) %collective-permute-start.12) | collective-permute-done | bytes 262176 | tf_op jit(solution)/shard_map/ppermute | solution.py:643
  71.8 0.1 pad_maximum_fusion.refs_5_
  71.9 2.5 %collective-permute-done.11 = bf16[2,272,128]{2,1,0:T(8,128)(2,1)S(1)} collective-permute-done((bf16[2,272,128]{2,1,0:T(8,128)(2,1)S(1)}, bf16[2,272,128]{2,1,0:T(8,128)(2,1)S(1)}, u32[]{:S(2)}, u32[]{:S(2)}) %collective-permute-start.11) | collective-permute-done | bytes 139296 | tf_op jit(solution)/shard_map/ppermute | solution.py:643
  74.4 0.1 constant_dynamic-update-slice_fusion.3
  74.5 1.6 %collective-permute-done.9.far_ref = bf16[128,1152]{1,0:T(8,128)(2,1)S(1)} collective-permute-done((bf16[128,1152]{1,0:T(8,128)(2,1)S(1)}, bf16[128,1152]{1,0:T(8,128)(2,1)S(1)}, u32[]{:S(2)}, u32[]{:S(2)}) %collective-permute-start.9) | collective-permute-done | bytes 294944 | tf_op jit(solution)/shard_map/ppermute | solution.py:638
  76.1 0.7 copy-done.16
  76.8 3.2 %back_mid.1 = (f32[128,1024]{1,0:T(8,128)}, bf16[8,408,128]{2,1,0:T(8,128)(2,1)}) custom-call(bf16[128,1152]{1,0:T(8,128)(2,1)} %copy-done.5, bf16[128,1152]{1,0:T(8,128)(2,1)} %copy-done.16, f32[128,1024]{1,0:T(8,128)} %get-tuple-element.53.resid_ref, f32[1,1024]{1,0:T(1,128)} %bitcast.20, f32[128,128]{1,0:T(8,128)} %get-tuple-element.48.gates_ref, ...), custom_call_target="tpu_custom_call" | custom-call | bytes 553500 | tf_op jit(solution)/shard_map/back_mid/pallas_call | solution.py:344
  80.1 7.4 %all-to-all-start.2 = ((bf16[8,408,128]{2,1,0:T(8,128)(2,1)}), bf16[8,408,128]{2,1,0:T(8,128)(2,1)S(1)}, u32[]{:S(2)}, u32[]{:S(2)}) async-start(bf16[8,408,128]{2,1,0:T(8,128)(2,1)} %get-tuple-element.55), calls=%async_computation.2 | async-start | bytes 1671168 | tf_op jit(solution)/shard_map/all_to_all | solution.py:662
  87.5 0.6 collective-permute-start.13
  88.0 2.0 %collective-permute-start.14 = (bf16[4,272,128]{2,1,0:T(8,128)(2,1)S(1)}, bf16[4,272,128]{2,1,0:T(8,128)(2,1)S(1)}, u32[]{:S(2)}, u32[]{:S(2)}) collective-permute-start(bf16[4,272,128]{2,1,0:T(8,128)(2,1)S(1)} %get-tuple-element.73), channel_id=1, source_target_pairs={{0,4},{4,0},{8,12},{12,8},{16,20},{20,16},{24,28},{28,24},{1,5},{5... | collective-permute-start | bytes 835592 | tf_op jit(solution)/shard_map/ppermute | solution.py:643
  90.1 1.0 copy.34.refs_9_
  91.1 11.9 %collective-permute-done.14 = bf16[4,272,128]{2,1,0:T(8,128)(2,1)S(1)} collective-permute-done((bf16[4,272,128]{2,1,0:T(8,128)(2,1)S(1)}, bf16[4,272,128]{2,1,0:T(8,128)(2,1)S(1)}, u32[]{:S(2)}, u32[]{:S(2)}) %collective-permute-start.14) | collective-permute-done | bytes 278560 | tf_op jit(solution)/shard_map/ppermute | solution.py:643
  103.0 0.7 collective-permute-start.18
  103.7 4.5 %all-to-all-done.2.refs_3_.refs_9_ = bf16[8,408,128]{2,1,0:T(8,128)(2,1)S(1)} async-done(((bf16[8,408,128]{2,1,0:T(8,128)(2,1)}), bf16[8,408,128]{2,1,0:T(8,128)(2,1)S(1)}, u32[]{:S(2)}, u32[]{:S(2)}) %all-to-all-start.2) | async-done | bytes 835616 | tf_op jit(solution)/shard_map/all_to_all | solution.py:662
  108.2 0.9 copy-done
  109.1 18.2 %attend_back.1 = (bf16[128,2176]{1,0:T(8,128)(2,1)}, f32[128,256]{1,0:T(8,128)}, f32[128,128]{1,0:T(8,128)}, f32[128,128]{1,0:T(8,128)}, f32[256,128]{1,0:T(8,128)}, /*index=5*/f32[1,128]{1,0:T(1,128)}) custom-call(s32[11]{0:T(128)} %pad_add_fusion.pos_ref.refs_0_, bf16[8,3,128,128]{3,2,1,0:T(8,128)(2,1)} %copy-done.2, bf16[8,2,128,128]{3,2,1,0:T(8,128)(2,1)} %copy-done.1, ...), custom_call_target="tpu_custom_call" | custom-call | bytes 3321000 | tf_op jit(solution)/shard_map/attend_back/pallas_call | solution.py:477
  127.3 0.1 collective-permute-start.15
  127.4 0.5 collective-permute-start.17
  127.9 0.1 collective-permute-start.19
  128.0 1.6 collective-permute-done.15
  129.6 1.2 add_convert_fusion.near_ref
  130.8 0.7 collective-permute-start.16
  131.5 0.5 collective-permute-start.21
  132.0 2.1 %collective-permute-done.20.refs_6_ = bf16[8,2,128,128]{3,2,1,0:T(8,128)(2,1)S(1)} collective-permute-done((bf16[8,2,128,128]{3,2,1,0:T(8,128)(2,1)S(1)}, bf16[8,2,128,128]{3,2,1,0:T(8,128)(2,1)S(1)}, u32[]{:S(2)}, u32[]{:S(2)}) %collective-permute-start.20) | collective-permute-done | bytes 524320 | tf_op jit(solution)/shard_map/ppermute | solution.py:638
  134.1 0.2 collective-permute-done.21.refs_8_
  134.4 0.5 copy-done.11
  134.9 0.2 copy-done.12
  135.1 0.2 copy-done.8
  135.3 0.8 copy-done.9
  136.1 23.5 %experts_all.1 = (f32[4,128,512]{2,1,0:T(8,128)}, f32[4,128,512]{2,1,0:T(8,128)}, f32[4,512,128]{2,1,0:T(8,128)}, f32[16,128]{1,0:T(8,128)}) custom-call(s32[11]{0:T(128)} %pad_add_fusion.pos_ref.refs_0_, bf16[8,272,128]{2,1,0:T(8,128)(2,1)} %copy-done.6, bf16[8,272,128]{2,1,0:T(8,128)(2,1)} %copy-done.8, bf16[8,272,128]{2,1,0:T(8,128)(2,1)} %copy-done.7, ...), custom_call_target="tpu_custom_call" | custom-call | bytes 4612500 | tf_op jit(solution)/shard_map/experts_all/pallas_call | solution.py:587
  159.7 0.8 copy-done.10
  160.5 2.9 %finish.1 = (f32[128,1024]{1,0:T(8,128)}, f32[1,128]{1,0:T(1,128)}, f32[128,1024]{1,0:T(8,128)}) custom-call(bf16[128,2176]{1,0:T(8,128)(2,1)} %copy-done.3, bf16[128,2176]{1,0:T(8,128)(2,1)} %copy-done.10, bf16[128,1024]{1,0:T(8,128)(2,1)} %x_ref.3, f32[1,1024]{1,0:T(1,128)} %bitcast.17, f32[128,1024]{1,0:T(8,128)} %get-tuple-element.59.dmid_ref, ...), custom_call_target="tpu_custom_call" | custom-call | bytes 369000 | tf_op jit(solution)/shard_map/finish/pallas_call | solution.py:623
  (60 shorter events, 0.3 us)
Async XLA Ops:
  0.6 39.4 %copy-start.23 = (s32[128,8]{0,1:T(8,128)S(1)}, s32[128,8]{0,1:T(8,128)}, u32[]{:S(2)}) copy-start(s32[128,8]{0,1:T(8,128)} %param.27) | copy-start | bytes 12292
  0.7 40.1 %copy-start.22 = (bf16[1024,16]{0,1:T(8,128)(2,1)S(1)}, bf16[1024,16]{0,1:T(8,128)(2,1)}, u32[]{:S(2)}) copy-start(bf16[1024,16]{0,1:T(8,128)(2,1)} %param.23) | copy-start | bytes 98308
  0.7 15.1 %collective-permute-start.1 = (bf16[256,1024]{1,0:T(8,128)(2,1)}, bf16[256,1024]{1,0:T(8,128)(2,1)S(1)}, u32[]{:S(2)}, u32[]{:S(2)}) collective-permute-start(bf16[256,1024]{1,0:T(8,128)(2,1)} %ow_ref.1), channel_id=1, source_target_pairs={{0,2},{1,3},{2,0},{3,1},{4,6},{5,7},{6,4},{7,5},{8,10},{9,11},{10,... | collective-permute-start | bytes 1572872 | tf_op jit(solution)/shard_map/ppermute | solution.py:638
  8.6 23.0 %all-to-all-start = ((bf16[8,2,128,128]{3,2,1,0:T(8,128)(2,1)}), bf16[8,2,128,128]{3,2,1,0:T(8,128)(2,1)S(1)}, u32[]{:S(2)}, u32[]{:S(2)}) async-start(bf16[8,2,128,128]{3,2,1,0:T(8,128)(2,1)} %get-tuple-element.43), calls=%async_computation | async-start | bytes 1048576 | tf_op jit(solution)/shard_map/all_to_all | solution.py:662
  14.4 17.2 %collective-permute-start = (bf16[256,1024]{1,0:T(8,128)(2,1)}, bf16[256,1024]{1,0:T(8,128)(2,1)S(1)}, u32[]{:S(2)}, u32[]{:S(2)}) collective-permute-start(bf16[256,1024]{1,0:T(8,128)(2,1)} %ow_ref.1), channel_id=1, source_target_pairs={{0,1},{1,0},{2,3},{3,2},{4,5},{5,4},{6,7},{7,6},{8,9},{9,8},{10,11... | collective-permute-start | bytes 1572872 | tf_op jit(solution)/shard_map/ppermute | solution.py:638
  15.8 29.5 %copy-start.13 = (bf16[256,1024]{1,0:T(8,128)(2,1)}, bf16[256,1024]{1,0:T(8,128)(2,1)S(1)}, u32[]{:S(2)}) copy-start(bf16[256,1024]{1,0:T(8,128)(2,1)S(1)} %collective-permute-done.1.refs_7_) | copy-start | bytes 1572868
  15.8 15.8 %collective-permute-start.2 = (bf16[256,1024]{1,0:T(8,128)(2,1)S(1)}, bf16[256,1024]{1,0:T(8,128)(2,1)S(1)}, u32[]{:S(2)}, u32[]{:S(2)}) collective-permute-start(bf16[256,1024]{1,0:T(8,128)(2,1)S(1)} %collective-permute-done.1.refs_7_), channel_id=1, source_target_pairs={{0,1},{1,0},{2,3},{3,2},{4,5},{5,4},{6,7},{7,6},{8,9},{9,8},{10,11... | collective-permute-start | bytes 1572872 | tf_op jit(solution)/shard_map/ppermute | solution.py:638
  17.1 14.3 %collective-permute-start.3 = (bf16[1,2,128,128]{3,2,1,0:T(8,128)(2,1)S(1)}, bf16[1,2,128,128]{3,2,1,0:T(8,128)(2,1)S(1)}, u32[]{:S(2)}, u32[]{:S(2)}) collective-permute-start(bf16[1,2,128,128]{3,2,1,0:T(8,128)(2,1)S(1)} %bitcast.11), channel_id=1, source_target_pairs={{0,16},{4,20},{8,24},{12,28},{16,0},{20,4},{24,8},{28,12},{1,17},{... | collective-permute-start | bytes 196616 | tf_op jit(solution)/shard_map/ppermute | solution.py:643
  31.5 12.5 %collective-permute-start.7 = (bf16[2,2,128,128]{3,2,1,0:T(8,128)(2,1)S(1)}, bf16[2,2,128,128]{3,2,1,0:T(8,128)(2,1)S(1)}, u32[]{:S(2)}, u32[]{:S(2)}) collective-permute-start(bf16[2,2,128,128]{3,2,1,0:T(8,128)(2,1)S(1)} %pad_maximum_fusion.3), channel_id=1, source_target_pairs={{0,8},{4,12},{8,0},{12,4},{16,24},{20,28},{24,16},{28,20},{1,9},{5... | collective-permute-start | bytes 393224 | tf_op jit(solution)/shard_map/ppermute | solution.py:643
  31.6 13.7 %copy-start.14 = (bf16[256,1024]{1,0:T(8,128)(2,1)}, bf16[256,1024]{1,0:T(8,128)(2,1)S(1)}, u32[]{:S(2)}) copy-start(bf16[256,1024]{1,0:T(8,128)(2,1)S(1)} %collective-permute-done.refs_6_) | copy-start | bytes 1572868
  31.6 4.2 %copy-start.1 = (bf16[8,2,128,128]{3,2,1,0:T(8,128)(2,1)}, bf16[8,2,128,128]{3,2,1,0:T(8,128)(2,1)S(1)}, u32[]{:S(2)}) copy-start(bf16[8,2,128,128]{3,2,1,0:T(8,128)(2,1)S(1)} %all-to-all-done.kv_ref.refs_2_) | copy-start | bytes 1572868
  31.6 13.7 %copy-start.15 = (bf16[256,1024]{1,0:T(8,128)(2,1)}, bf16[256,1024]{1,0:T(8,128)(2,1)S(1)}, u32[]{:S(2)}) copy-start(bf16[256,1024]{1,0:T(8,128)(2,1)S(1)} %collective-permute-done.2.refs_8_) | copy-start | bytes 1572868
  31.6 48.5 %all-to-all-start.1 = ((bf16[8,3,128,128]{3,2,1,0:T(8,128)(2,1)}), bf16[8,3,128,128]{3,2,1,0:T(8,128)(2,1)S(1)}, u32[]{:S(2)}, u32[]{:S(2)}) async-start(bf16[8,3,128,128]{3,2,1,0:T(8,128)(2,1)} %get-tuple-element.45.q_ref), calls=%async_computation.1 | async-start | bytes 1572864 | tf_op jit(solution)/shard_map/all_to_all | solution.py:662
  39.5 4.5 %collective-permute-start.5 = (bf16[128,256]{1,0:T(8,128)(2,1)}, bf16[128,256]{1,0:T(8,128)(2,1)S(1)}, u32[]{:S(2)}, u32[]{:S(2)}) collective-permute-start(bf16[128,256]{1,0:T(8,128)(2,1)} %attend.1.refs_1_), channel_id=1, source_target_pairs={{0,2},{1,3},{2,0},{3,1},{4,6},{5,7},{6,4},{7,5},{8,10},{9,11},{10,... | collective-permute-start | bytes 196616 | tf_op jit(solution)/shard_map/ppermute | solution.py:638
  41.7 2.3 %collective-permute-start.4 = (bf16[128,256]{1,0:T(8,128)(2,1)}, bf16[128,256]{1,0:T(8,128)(2,1)S(1)}, u32[]{:S(2)}, u32[]{:S(2)}) collective-permute-start(bf16[128,256]{1,0:T(8,128)(2,1)} %attend.1.refs_1_), channel_id=1, source_target_pairs={{0,1},{1,0},{2,3},{3,2},{4,5},{5,4},{6,7},{7,6},{8,9},{9,8},{10,11... | collective-permute-start | bytes 196616 | tf_op jit(solution)/shard_map/ppermute | solution.py:638
  44.0 1.3 copy-start.18
  44.0 1.3 collective-permute-start.6
  44.1 1.2 copy-start.19
  45.3 0.6 copy-start.20
  49.3 11.3 %copy-start.17 = (bf16[1,272,128]{2,1,0:T(8,128)(2,1)S(1)}, bf16[1,272,128]{2,1,0:T(8,128)(2,1)}, u32[]{:S(2)}) copy-start(bf16[1,272,128]{2,1,0:T(8,128)(2,1)} %get-tuple-element.50) | copy-start | bytes 208900
  60.4 29.6 %copy-start.21 = (f32[1024]{0:T(1024)S(1)}, f32[1024]{0:T(1024)}, u32[]{:S(2)}) copy-start(f32[1024]{0:T(1024)} %param.17) | copy-start | bytes 12292
  60.4 7.3 %collective-permute-start.8 = (bf16[128,1152]{1,0:T(8,128)(2,1)}, bf16[128,1152]{1,0:T(8,128)(2,1)S(1)}, u32[]{:S(2)}, u32[]{:S(2)}) collective-permute-start(bf16[128,1152]{1,0:T(8,128)(2,1)} %get-tuple-element.49), channel_id=1, source_target_pairs={{0,1},{1,0},{2,3},{3,2},{4,5},{5,4},{6,7},{7,6},{8,9},{9,8},{10,11... | collective-permute-start | bytes 884744 | tf_op jit(solution)/shard_map/ppermute | solution.py:638
  60.6 7.1 %collective-permute-start.10 = (bf16[1,272,128]{2,1,0:T(8,128)(2,1)S(1)}, bf16[1,272,128]{2,1,0:T(8,128)(2,1)S(1)}, u32[]{:S(2)}, u32[]{:S(2)}) collective-permute-start(bf16[1,272,128]{2,1,0:T(8,128)(2,1)S(1)} %copy-done.17), channel_id=1, source_target_pairs={{0,16},{4,20},{8,24},{12,28},{16,0},{20,4},{24,8},{28,12},{1,17},{... | collective-permute-start | bytes 208904 | tf_op jit(solution)/shard_map/ppermute | solution.py:643
  63.5 8.3 %collective-permute-start.12 = (bf16[4,2,128,128]{3,2,1,0:T(8,128)(2,1)S(1)}, bf16[4,2,128,128]{3,2,1,0:T(8,128)(2,1)S(1)}, u32[]{:S(2)}, u32[]{:S(2)}) collective-permute-start(bf16[4,2,128,128]{3,2,1,0:T(8,128)(2,1)S(1)} %pad_maximum_fusion.1), channel_id=1, source_target_pairs={{0,4},{4,0},{8,12},{12,8},{16,20},{20,16},{24,28},{28,24},{1,5},{5... | collective-permute-start | bytes 786440 | tf_op jit(solution)/shard_map/ppermute | solution.py:643
  68.8 7.4 %copy-start.5 = (bf16[128,1152]{1,0:T(8,128)(2,1)}, bf16[128,1152]{1,0:T(8,128)(2,1)S(1)}, u32[]{:S(2)}) copy-start(bf16[128,1152]{1,0:T(8,128)(2,1)S(1)} %add_convert_fusion.1.ex_ref) | copy-start | bytes 884740
  68.8 7.4 %collective-permute-start.9 = (bf16[128,1152]{1,0:T(8,128)(2,1)S(1)}, bf16[128,1152]{1,0:T(8,128)(2,1)S(1)}, u32[]{:S(2)}, u32[]{:S(2)}) collective-permute-start(bf16[128,1152]{1,0:T(8,128)(2,1)S(1)} %add_convert_fusion.1.ex_ref), channel_id=1, source_target_pairs={{0,2},{1,3},{2,0},{3,1},{4,6},{5,7},{6,4},{7,5},{8,10},{9,11},{10,... | collective-permute-start | bytes 884744 | tf_op jit(solution)/shard_map/ppermute | solution.py:638
  69.4 5.1 %collective-permute-start.11 = (bf16[2,272,128]{2,1,0:T(8,128)(2,1)S(1)}, bf16[2,272,128]{2,1,0:T(8,128)(2,1)S(1)}, u32[]{:S(2)}, u32[]{:S(2)}) collective-permute-start(bf16[2,272,128]{2,1,0:T(8,128)(2,1)S(1)} %pad_maximum_fusion.2), channel_id=1, source_target_pairs={{0,8},{4,12},{8,0},{12,4},{16,24},{20,28},{24,16},{28,20},{1,9},{5... | collective-permute-start | bytes 417800 | tf_op jit(solution)/shard_map/ppermute | solution.py:643
  71.9 59.6 %copy-start.4 = (bf16[8,2,128,128]{3,2,1,0:T(8,128)(2,1)}, bf16[8,2,128,128]{3,2,1,0:T(8,128)(2,1)S(1)}, u32[]{:S(2)}) copy-start(bf16[8,2,128,128]{3,2,1,0:T(8,128)(2,1)S(1)} %pad_maximum_fusion.refs_5_) | copy-start | bytes 1572868
  76.1 0.7 copy-start.16
  80.1 28.1 %copy-start.2 = (bf16[8,3,128,128]{3,2,1,0:T(8,128)(2,1)}, bf16[8,3,128,128]{3,2,1,0:T(8,128)(2,1)S(1)}, u32[]{:S(2)}) copy-start(bf16[8,3,128,128]{3,2,1,0:T(8,128)(2,1)S(1)} %all-to-all-done.1.refs_1_) | copy-start | bytes 2359300
  80.1 28.1 %all-to-all-start.2 = ((bf16[8,408,128]{2,1,0:T(8,128)(2,1)}), bf16[8,408,128]{2,1,0:T(8,128)(2,1)S(1)}, u32[]{:S(2)}, u32[]{:S(2)}) async-start(bf16[8,408,128]{2,1,0:T(8,128)(2,1)} %get-tuple-element.55), calls=%async_computation.2 | async-start | bytes 1671168 | tf_op jit(solution)/shard_map/all_to_all | solution.py:662
  87.5 16.2 %collective-permute-start.13 = (bf16[8,2,128,128]{3,2,1,0:T(8,128)(2,1)S(1)}, bf16[8,2,128,128]{3,2,1,0:T(8,128)(2,1)}, u32[]{:S(2)}, u32[]{:S(2)}) collective-permute-start(bf16[8,2,128,128]{3,2,1,0:T(8,128)(2,1)S(1)} %pad_maximum_fusion.refs_5_), channel_id=1, source_target_pairs={{0,2},{1,3},{2,0},{3,1},{4,6},{5,7},{6,4},{7,5},{8,10},{9,11},{10,... | collective-permute-start | bytes 1572872 | tf_op jit(solution)/shard_map/ppermute | solution.py:638
  88.0 14.9 %collective-permute-start.14 = (bf16[4,272,128]{2,1,0:T(8,128)(2,1)S(1)}, bf16[4,272,128]{2,1,0:T(8,128)(2,1)S(1)}, u32[]{:S(2)}, u32[]{:S(2)}) collective-permute-start(bf16[4,272,128]{2,1,0:T(8,128)(2,1)S(1)} %get-tuple-element.73), channel_id=1, source_target_pairs={{0,4},{4,0},{8,12},{12,8},{16,20},{20,16},{24,28},{28,24},{1,5},{5... | collective-permute-start | bytes 835592 | tf_op jit(solution)/shard_map/ppermute | solution.py:643
  103.0 31.4 %copy-start.6 = (bf16[8,272,128]{2,1,0:T(8,128)(2,1)}, bf16[8,272,128]{2,1,0:T(8,128)(2,1)S(1)}, u32[]{:S(2)}) copy-start(bf16[8,272,128]{2,1,0:T(8,128)(2,1)S(1)} %constant_dynamic-update-slice_fusion.2.refs_1_) | copy-start | bytes 1671172
  103.0 24.9 %collective-permute-start.18 = (bf16[8,272,128]{2,1,0:T(8,128)(2,1)S(1)}, bf16[8,272,128]{2,1,0:T(8,128)(2,1)S(1)}, u32[]{:S(2)}, u32[]{:S(2)}) collective-permute-start(bf16[8,272,128]{2,1,0:T(8,128)(2,1)S(1)} %constant_dynamic-update-slice_fusion.2.refs_1_), channel_id=1, source_target_pairs={{0,2},{1,3},{2,0},{3,1},{4,6},{5,7},{6,4},{7,5},{8,10},{9,11},{10,... | collective-permute-start | bytes 1671176 | tf_op jit(solution)/shard_map/ppermute | solution.py:638
  108.2 0.9 copy-start
  127.3 2.2 %collective-permute-start.15 = (bf16[128,2176]{1,0:T(8,128)(2,1)}, bf16[128,2176]{1,0:T(8,128)(2,1)S(1)}, u32[]{:S(2)}, u32[]{:S(2)}) collective-permute-start(bf16[128,2176]{1,0:T(8,128)(2,1)} %get-tuple-element.58), channel_id=1, source_target_pairs={{0,1},{1,0},{2,3},{3,2},{4,5},{5,4},{6,7},{7,6},{8,9},{9,8},{10,11... | collective-permute-start | bytes 1671176 | tf_op jit(solution)/shard_map/ppermute | solution.py:638
  127.4 6.9 %collective-permute-start.17 = (bf16[8,272,128]{2,1,0:T(8,128)(2,1)S(1)}, bf16[8,272,128]{2,1,0:T(8,128)(2,1)S(1)}, u32[]{:S(2)}, u32[]{:S(2)}) collective-permute-start(bf16[8,272,128]{2,1,0:T(8,128)(2,1)S(1)} %constant_dynamic-update-slice_fusion.2.refs_1_), channel_id=1, source_target_pairs={{0,1},{1,0},{2,3},{3,2},{4,5},{5,4},{6,7},{7,6},{8,9},{9,8},{10,11... | collective-permute-start | bytes 1671176 | tf_op jit(solution)/shard_map/ppermute | solution.py:638
  127.9 6.4 %copy-start.7 = (bf16[8,272,128]{2,1,0:T(8,128)(2,1)}, bf16[8,272,128]{2,1,0:T(8,128)(2,1)S(1)}, u32[]{:S(2)}) copy-start(bf16[8,272,128]{2,1,0:T(8,128)(2,1)S(1)} %collective-permute-done.18.refs_3_) | copy-start | bytes 1671172
  127.9 6.4 %collective-permute-start.19 = (bf16[8,272,128]{2,1,0:T(8,128)(2,1)S(1)}, bf16[8,272,128]{2,1,0:T(8,128)(2,1)S(1)}, u32[]{:S(2)}, u32[]{:S(2)}) collective-permute-start(bf16[8,272,128]{2,1,0:T(8,128)(2,1)S(1)} %collective-permute-done.18.refs_3_), channel_id=1, source_target_pairs={{0,1},{1,0},{2,3},{3,2},{4,5},{5,4},{6,7},{7,6},{8,9},{9,8},{10,11... | collective-permute-start | bytes 1671176 | tf_op jit(solution)/shard_map/ppermute | solution.py:638
  130.8 28.9 %copy-start.3 = (bf16[128,2176]{1,0:T(8,128)(2,1)}, bf16[128,2176]{1,0:T(8,128)(2,1)S(1)}, u32[]{:S(2)}) copy-start(bf16[128,2176]{1,0:T(8,128)(2,1)S(1)} %add_convert_fusion.near_ref) | copy-start | bytes 1671172
  130.8 28.9 %collective-permute-start.16 = (bf16[128,2176]{1,0:T(8,128)(2,1)S(1)}, bf16[128,2176]{1,0:T(8,128)(2,1)S(1)}, u32[]{:S(2)}, u32[]{:S(2)}) collective-permute-start(bf16[128,2176]{1,0:T(8,128)(2,1)S(1)} %add_convert_fusion.near_ref), channel_id=1, source_target_pairs={{0,2},{1,3},{2,0},{3,1},{4,6},{5,7},{6,4},{7,5},{8,10},{9,11},{10,... | collective-permute-start | bytes 1671176 | tf_op jit(solution)/shard_map/ppermute | solution.py:638
  131.5 2.6 %collective-permute-start.20 = (bf16[8,2,128,128]{3,2,1,0:T(8,128)(2,1)S(1)}, bf16[8,2,128,128]{3,2,1,0:T(8,128)(2,1)S(1)}, u32[]{:S(2)}, u32[]{:S(2)}) collective-permute-start(bf16[8,2,128,128]{3,2,1,0:T(8,128)(2,1)S(1)} %pad_maximum_fusion.refs_5_), channel_id=1, source_target_pairs={{0,1},{1,0},{2,3},{3,2},{4,5},{5,4},{6,7},{7,6},{8,9},{9,8},{10,11... | collective-permute-start | bytes 1572872 | tf_op jit(solution)/shard_map/ppermute | solution.py:638
  131.5 2.9 %collective-permute-start.21 = (bf16[8,2,128,128]{3,2,1,0:T(8,128)(2,1)}, bf16[8,2,128,128]{3,2,1,0:T(8,128)(2,1)S(1)}, u32[]{:S(2)}, u32[]{:S(2)}) collective-permute-start(bf16[8,2,128,128]{3,2,1,0:T(8,128)(2,1)} %collective-permute-done.13.refs_7_), channel_id=1, source_target_pairs={{0,1},{1,0},{2,3},{3,2},{4,5},{5,4},{6,7},{7,6},{8,9},{9,8},{10,11... | collective-permute-start | bytes 1572872 | tf_op jit(solution)/shard_map/ppermute | solution.py:638
  134.1 0.8 copy-start.11
  134.3 0.8 copy-start.12
  134.3 1.0 copy-start.8
  135.3 0.8 copy-start.9
  159.6 0.8 copy-start.10
